TPU v7x, 256 devices: a whole 4x4x8 slice. The times are simulated.
256 devices in a mesh: term: 8 (over y, core), pass: 32 (over x, z).
Axes of the slice: x: 4, y: 4, z: 8, core: 2. Of those that a mesh axis runs over, the one named last changes fastest.
Arguments:
- hidden: bfloat16 [16384, 4096], P('pass', 'term'), may hold values from -16 to 16
- head_weight: bfloat16 [4096, 16384], P('pass', 'term'), may hold values from -0.09375 to 0.09375
- lengths: int32 [256], P('pass'), may hold values from 1 to 64, as said below
Outputs:
- postings: bfloat16 [16384, 256], P(('term', 'pass'))
Inputs may be any that keep to these rules, and one draw needn't show every extreme that they name: Passage p's valid tokens are its first lengths[p] slots; some passage has exactly 64.
All inputs are finite; a program needn't handle non-finite values.
Results may differ from a plain program's by a relative error of at most 0.013.
Values may be sent and summed in bfloat16 or wider, within the bound.
No kernel may reach another device: no remote copies, remote signals or barrier semaphores. Data moves between devices by JAX's collectives and lax.ppermute only.
A program may use at most 64 MiB of HBM per device.

v0:
```python
import jax
import jax.numpy as jnp
from jax import lax
from jax.sharding import PartitionSpec as P


def body(hidden, head_weight, lengths):
    gathered = lax.all_gather(hidden, "term", axis=1, tiled=True)
    passages = lengths.shape[0]
    tokens_per = gathered.shape[0] // passages
    slab_cols = head_weight.shape[1]
    allowed = jnp.arange(tokens_per, dtype=jnp.int32)[None, :] < lengths[:, None]
    logits = jnp.dot(
        gathered,
        lax.all_gather(head_weight, "pass", axis=0, tiled=True),
        preferred_element_type=jnp.float32,
    )
    impacts = jnp.log1p(jnp.maximum(logits, jnp.float32(0.0)))
    impacts = impacts.reshape(passages, tokens_per, slab_cols)
    impacts = jnp.where(allowed[:, :, None], impacts, jnp.float32(0.0))
    pooled = jnp.max(impacts, axis=1).astype(jnp.bfloat16)
    owners = lax.axis_size("pass")
    range_cols = slab_cols // owners
    local_max = jnp.max(pooled.astype(jnp.float32), axis=0)
    column_max = lax.pmax(local_max, "pass")
    payload = (pooled.astype(jnp.float32) / (1.0 + column_max)[None, :]).astype(jnp.bfloat16)
    shaped = payload.reshape(passages, owners, range_cols)
    return jnp.transpose(
        lax.all_to_all(shaped, "pass", split_axis=1, concat_axis=0, tiled=True)[:, 0, :]
    )


def solution(mesh):
    return jax.shard_map(
        body,
        mesh=mesh,
        in_specs=(P("pass", "term"), P("pass", "term"), P("pass")),
        out_specs=P(("term", "pass"), None),
        check_vma=False,
    )
```

profile of v0, /device:TPU:8, one launch (start us, length us, event | category | flops | bytes accessed | tf_op | source)
XLA Modules:
  0.0 297.9 jit_solution(6542916140701454250)
XLA Ops:
  6.5 0.0 all-gather.3.cloned.1.call-start
  6.5 0.7 all-gather.3.cloned.1.call-update
  7.3 0.0 all-gather.5.cloned.1.call-start
  7.3 0.7 all-gather.5.cloned.1.call-update
  8.0 0.7 iota_compare_fusion
  8.7 37.0 %all-gather.3.cloned.1.call-done = bf16[512,4096]{1,0:T(8,128)(2,1)} async-done(((bf16[512,512]{1,0:T(8,128)(2,1)}), bf16[512,4096]{1,0:T(8,128)(2,1)}) %all-gather.3.cloned.1.call-update) | async-done | bytes 4194320 | tf_op jit(solution)/shard_map/all_gather | solution.py:8
  45.8 144.1 %all-gather.5.cloned.1.call-done = bf16[4096,2048]{1,0:T(8,128)(2,1)} async-done(((bf16[128,2048]{1,0:T(8,128)(2,1)}), bf16[4096,2048]{1,0:T(8,128)(2,1)}) %all-gather.5.cloned.1.call-update) | async-done | bytes 16777232 | tf_op jit(solution)/shard_map/all_gather | solution.py:15
  189.9 14.8 %select_reduce_fusion = bf16[8,2048]{1,0:T(8,128)(2,1)S(1)} fusion(pred[8,64]{1,0:T(8,128)(4,1)S(1)} %iota_compare_fusion, bf16[512,4096]{1,0:T(8,128)(2,1)} %all-gather.3.cloned.1.call-done, bf16[4096,2048]{1,0:T(8,128)(2,1)} %all-gather.5.cloned.1.call-done), kind=kOutput, calls=%fused_computation | convolution fusion | flops 8594112512 | bytes 21004800 | tf_op jit(solution)/shard_map/dot_general | solution.py:13
  204.8 0.1 reshape.37
  204.9 72.3 %pmax.7 = f32[2048]{0:T(1024)S(1)} all-reduce(bf16[2048]{0:T(1024)(128)(2,1)S(1)} %convert_reduce_fusion), channel_id=1, replica_groups=mesh['term'=8,'pass'=32] {'pass'}, use_global_device_ids=true, to_apply=%region_2.3 | all-reduce | flops 2048 | bytes 12288 | tf_op jit(solution)/shard_map/pmax | solution.py:25
  277.2 0.1 div.11
  277.3 0.1 reshape.38
  277.4 12.8 %all_to_all.15 = bf16[32,2,256]{2,1,0:T(2,128)(2,1)S(1)} all-to-all(bf16[32,2,256]{2,1,0:T(2,128)(2,1)S(1)} %reshape.38), channel_id=1, replica_groups=mesh['term'=8,'pass'=32] {'pass'}, dimensions={0} | all-to-all | bytes 65536 | tf_op jit(solution)/shard_map/all_to_all | solution.py:29
  290.2 0.1 reshape.39
  290.4 0.7 copy.7
  (5 shorter events, 0.1 us)
Async XLA Ops:
  6.5 39.2 %all-gather.3.cloned.1.call-start = ((), (), s32[]{:S(2)}) async-start(), calls=%async_computation.1 | async-start | bytes 4718592 | tf_op jit(solution)/shard_map/all_gather | solution.py:8
  7.3 182.6 %all-gather.5.cloned.1.call-start = ((), (), s32[]{:S(2)}) async-start(), calls=%async_computation.2 | async-start | bytes 17301504 | tf_op jit(solution)/shard_map/all_gather | solution.py:15
Sparse Core Ops, SparseCore 0:
  9.2 36.5 all-gather.2
  48.4 141.4 all-gather.4
where the time goes:
time: 298 us
  waiting for transfers between devices  183 us (61%)
  blocking collectives  85.1 us (29%)
  matrix products  14.8 us (5%)
  between operations  13.5 us (5%)
    all_gather x1, waiting for transfers between devices, body(): lax.all_gather(head_weight, 'pass', axis=0, tiled=True)  144 us
    pmax x1, blocking collectives, body(): column_max = lax.pmax(local_max, 'pass')  72.3 us
    all_gather x1, waiting for transfers between devices, body(): gathered = lax.all_gather(hidden, 'term', axis=1, tiled=True)  37 us
    dot_general x1, matrix products, body(): jnp.dot(gathered, lax.all_gather(head_weight, 'pass', axis=0, tiled=True)...  14.8 us
    all_to_all x1, blocking collectives, body(): lax.all_to_all(shaped, 'pass', split_axis=1, concat_axis=0, tiled=True)  12.8 us
  transfers between devices with their start and end apart: 2, of which 2 were waited for; matrix products, arithmetic and copies ran while one was open for 0% of the time, Pallas kernels for 0%

commit v1 on v0

v1 whole, which is shorter than its diff:
```python
import functools

import jax
import jax.numpy as jnp
from jax import lax
from jax.experimental import pallas as pl
from jax.experimental.pallas import tpu as pltpu
from jax.sharding import Mesh, PartitionSpec as P

LEN = 64


def pool_kernel(where, a_ref, *refs):
    nz = where.shape[0]
    pieces, (o_ref, w, sems) = refs[:nz], refs[nz:]
    nx, rows = pieces[0].shape[0], pieces[0].shape[1]

    def copies():
        for s in range(nz):
            at = where[s] * rows
            for i in range(nx):
                to = pl.multiple_of(at + i * nz * rows, rows)
                yield pltpu.make_async_copy(
                    pieces[s].at[i], w.at[pl.ds(to, rows)], sems.at[s, i]
                )

    @pl.when(pl.program_id(0) == 0)
    def _():
        for c in copies():
            c.start()
        for c in copies():
            c.wait()

    depth = a_ref.shape[2]
    acc = jnp.dot(a_ref[0], w[:depth], preferred_element_type=jnp.float32)
    for k in range(1, a_ref.shape[0]):
        acc += jnp.dot(
            a_ref[k],
            w[k * depth : (k + 1) * depth],
            preferred_element_type=jnp.float32,
        )
    tokens, cols = acc.shape
    top = jnp.max(acc.reshape(tokens // LEN, LEN, cols), axis=1)
    o_ref[...] = jnp.log1p(jnp.maximum(top, 0.0)).astype(o_ref.dtype)


def pool(where, gathered, pieces, nx):
    blocks, tokens, depth = gathered.shape
    cols = pieces[0].shape[-1]
    per = blocks // nx
    nz = len(pieces)
    return pl.pallas_call(
        pool_kernel,
        out_shape=jax.ShapeDtypeStruct((nx * tokens // LEN, cols), jnp.bfloat16),
        grid_spec=pltpu.PrefetchScalarGridSpec(
            num_scalar_prefetch=1,
            grid=(nx,),
            in_specs=[pl.BlockSpec((per, tokens, depth), lambda i, _: (i, 0, 0))]
            + [pl.BlockSpec(memory_space=pl.ANY)] * nz,
            out_specs=pl.BlockSpec((tokens // LEN, cols), lambda i, _: (i, 0)),
            scratch_shapes=[
                pltpu.VMEM((per * depth, cols), jnp.bfloat16),
                pltpu.SemaphoreType.DMA((nz, nx)),
            ],
        ),
        compiler_params=pltpu.CompilerParams(vmem_limit_bytes=48 << 20),
    )(where, gathered, *pieces)


def ring(block, axis):
    n = lax.axis_size(axis)
    up = [(i, (i + 1) % n) for i in range(n)]
    down = [(i, (i - 1) % n) for i in range(n)]
    out, offsets = [block], [0]
    low = high = block
    for s in range(1, n // 2):
        low = lax.ppermute(low, axis, up)
        high = lax.ppermute(high, axis, down)
        out += [low, high]
        offsets += [-s, s]
    out.append(lax.ppermute(low, axis, up))
    offsets.append(-(n // 2))
    return out, offsets


def body(hidden, head_weight, lengths):
    nx, nz = lax.axis_size("x"), lax.axis_size("z")
    z = lax.axis_index("z")
    rows, cols = head_weight.shape
    per = hidden.shape[0] // lengths.shape[0]
    allowed = jnp.arange(per, dtype=jnp.int32)[None, :] < lengths[:, None]
    hidden = jnp.where(
        allowed[:, :, None], hidden.reshape(-1, per, hidden.shape[1]), 0
    ).reshape(hidden.shape)
    full = lax.all_gather(hidden, ("x", "y", "c"), axis=0, tiled=False)
    head = head_weight.reshape(rows, nx, cols // nx)
    head = lax.all_to_all(head, "x", split_axis=1, concat_axis=0, tiled=False)
    head = head.reshape(nx, rows, cols // nx)
    pieces, offsets = ring(head, "z")
    where = (z + jnp.array(offsets, jnp.int32) + nz) % nz
    pooled = pool(where, full.reshape(-1, *hidden.shape), pieces, nx)
    pooled = pooled.reshape(nx, -1, nz, pooled.shape[1] // nz)
    mine = lax.all_to_all(pooled, "z", split_axis=2, concat_axis=1, tiled=False)
    mine = mine.reshape(-1, mine.shape[-1]).astype(jnp.float32)
    peak = jnp.max(mine, axis=0)
    return jnp.transpose((mine / (1.0 + peak)[None, :]).astype(jnp.bfloat16))


def solution(mesh):
    fine = Mesh(mesh.devices.reshape(4, 2, 4, 8), ("y", "c", "x", "z"))
    return jax.shard_map(
        body,
        mesh=fine,
        in_specs=(P(("x", "z"), ("y", "c")), P(("x", "z"), ("y", "c")), P(("x", "z"))),
        out_specs=P(("y", "c", "x", "z"), None),
        check_vma=False,
    )
```

time: 298 us -> 132 us (0.44)
  the two profiles are of different devices: /device:TPU:8 before, /device:TPU:1 now
where the time goes in v1:
time: 132 us; the launch traced here: 131 us
  waiting for transfers between devices  56 us (42%)
  blocking collectives  26.6 us (20%)
  Pallas kernels  18.4 us (14%)
  between operations  13.4 us (10%)
  starting transfers between devices  11 us (8%)
  other arithmetic  3.46 us (3%)
  local copies, waits for them, and re-layouts  2.67 us (2%)
    ppermute x3, waiting for transfers between devices, ring(): low = lax.ppermute(low, axis, up)  28.7 us
    pallas_call x1, Pallas kernels, pool(): pl.pallas_call(pool_kernel, out_shape=jax.ShapeDtypeStruct((nx * tokens /...  18.4 us
    all_gather x1, waiting for transfers between devices, body(): full = lax.all_gather(hidden, ('x', 'y', 'c'), axis=0, tiled=False)  17.3 us
    all_to_all x1, blocking collectives, body(): mine = lax.all_to_all(pooled, 'z', split_axis=2, concat_axis=1, tiled=False)  13.4 us
    all_to_all x1, blocking collectives, body(): head = lax.all_to_all(head, 'x', split_axis=1, concat_axis=0, tiled=False)  13.2 us
    ppermute x1, waiting for transfers between devices, ring(): out.append(lax.ppermute(low, axis, up))  9.92 us
    ppermute x3, starting transfers between devices, ring(): high = lax.ppermute(high, axis, down)  9.29 us
  transfers between devices with their start and end apart: 8, of which 5 were waited for; matrix products, arithmetic and copies ran while one was open for 2% of the time, Pallas kernels for 0%

profile of v1, /device:TPU:1, one launch (start us, length us, event | category | flops | bytes accessed | tf_op | source)
XLA Modules:
  0.0 131.4 jit_solution(17138035237477534620)
XLA Ops:
  6.5 0.0 all-gather.3.cloned.1.call-start
  6.5 0.7 iota_compare_fusion
  7.3 0.1 lt.30
  7.4 2.0 %broadcast_select_fusion = bf16[512,512]{1,0:T(8,128)(2,1)} fusion(bf16[512,512]{1,0:T(8,128)(2,1)} %param.4, pred[512]{0:T(512)(128)(4,1)S(1)} %lt.30), kind=kLoop, calls=%fused_computation | loop fusion | flops 262144 | bytes 1049088 | tf_op jit(solution)/shard_map/jit(_where)/select_n | solution.py:92
  9.3 0.0 all-gather.3.cloned.1.call-update
  9.4 1.3 copy.10
  10.7 0.2 copy.11
  10.9 13.2 %all_to_all.24 = bf16[1,128,4,512]{3,1,0,2:T(8,128)(2,1)S(1)} all-to-all(bf16[1,128,4,512]{3,1,0,2:T(8,128)(2,1)S(1)} %copy.11), channel_id=1, replica_groups=mesh['y'=4,'c'=2,'x'=4,'z'=8] {'x'}, dimensions={2} | all-to-all | bytes 1048576 | tf_op jit(solution)/shard_map/all_to_all | solution.py:97
  24.1 1.7 %collective-permute-start = (bf16[4,128,512]{2,1,0:T(8,128)(2,1)S(1)}, bf16[4,128,512]{2,1,0:T(8,128)(2,1)S(1)}, u32[]{:S(2)}, u32[]{:S(2)}) collective-permute-start(bf16[4,128,512]{2,1,0:T(8,128)(2,1)S(1)} %bitcast.22), channel_id=1, source_target_pairs={{0,1},{1,2},{2,3},{3,4},{4,5},{5,6},{6,7},{7,0},{8,9},{9,10},{10,1... | collective-permute-start | bytes 1572872 | tf_op jit(solution)/shard_map/ppermute | solution.py:77
  25.8 3.9 %collective-permute-start.1 = (bf16[4,128,512]{2,1,0:T(8,128)(2,1)S(1)}, bf16[4,128,512]{2,1,0:T(8,128)(2,1)S(1)}, u32[]{:S(2)}, u32[]{:S(2)}) collective-permute-start(bf16[4,128,512]{2,1,0:T(8,128)(2,1)S(1)} %bitcast.23), channel_id=1, source_target_pairs={{0,7},{1,0},{2,1},{3,2},{4,3},{5,4},{6,5},{7,6},{8,15},{9,8},{10,9... | collective-permute-start | bytes 1572872 | tf_op jit(solution)/shard_map/ppermute | solution.py:78
  29.7 10.5 %collective-permute-done.refs_1_ = bf16[4,128,512]{2,1,0:T(8,128)(2,1)S(1)} collective-permute-done((bf16[4,128,512]{2,1,0:T(8,128)(2,1)S(1)}, bf16[4,128,512]{2,1,0:T(8,128)(2,1)S(1)}, u32[]{:S(2)}, u32[]{:S(2)}) %collective-permute-start) | collective-permute-done | bytes 524320 | tf_op jit(solution)/shard_map/ppermute | solution.py:77
  40.2 0.0 collective-permute-start.2
  40.2 0.0 collective-permute-done.1.refs_2_
  40.2 2.7 %collective-permute-start.3 = (bf16[4,128,512]{2,1,0:T(8,128)(2,1)S(1)}, bf16[4,128,512]{2,1,0:T(8,128)(2,1)S(1)}, u32[]{:S(2)}, u32[]{:S(2)}) collective-permute-start(bf16[4,128,512]{2,1,0:T(8,128)(2,1)S(1)} %collective-permute-done.1.refs_2_), channel_id=1, source_target_pairs={{0,7},{1,0},{2,1},{3,2},{4,3},{5,4},{6,5},{7,6},{8,15},{9,8},{10,9... | collective-permute-start | bytes 1572872 | tf_op jit(solution)/shard_map/ppermute | solution.py:78
  42.9 9.5 %collective-permute-done.2.refs_3_ = bf16[4,128,512]{2,1,0:T(8,128)(2,1)S(1)} collective-permute-done((bf16[4,128,512]{2,1,0:T(8,128)(2,1)S(1)}, bf16[4,128,512]{2,1,0:T(8,128)(2,1)S(1)}, u32[]{:S(2)}, u32[]{:S(2)}) %collective-permute-start.2) | collective-permute-done | bytes 524320 | tf_op jit(solution)/shard_map/ppermute | solution.py:77
  52.4 0.0 collective-permute-start.4
  52.4 0.0 collective-permute-done.3.refs_4_
  52.4 2.7 %collective-permute-start.5 = (bf16[4,128,512]{2,1,0:T(8,128)(2,1)S(1)}, bf16[4,128,512]{2,1,0:T(8,128)(2,1)}, u32[]{:S(2)}, u32[]{:S(2)}) collective-permute-start(bf16[4,128,512]{2,1,0:T(8,128)(2,1)S(1)} %collective-permute-done.3.refs_4_), channel_id=1, source_target_pairs={{0,7},{1,0},{2,1},{3,2},{4,3},{5,4},{6,5},{7,6},{8,15},{9,8},{10,9... | collective-permute-start | bytes 1572872 | tf_op jit(solution)/shard_map/ppermute | solution.py:78
  55.1 8.7 %collective-permute-done.4.refs_5_ = bf16[4,128,512]{2,1,0:T(8,128)(2,1)S(1)} collective-permute-done((bf16[4,128,512]{2,1,0:T(8,128)(2,1)S(1)}, bf16[4,128,512]{2,1,0:T(8,128)(2,1)S(1)}, u32[]{:S(2)}, u32[]{:S(2)}) %collective-permute-start.4) | collective-permute-done | bytes 524320 | tf_op jit(solution)/shard_map/ppermute | solution.py:77
  63.8 0.0 collective-permute-start.6
  63.8 0.7 and_select_fusion.where
  64.5 0.0 collective-permute-done.5.refs_6_
  64.5 9.9 %collective-permute-done.6.refs_7_ = bf16[4,128,512]{2,1,0:T(8,128)(2,1)} collective-permute-done((bf16[4,128,512]{2,1,0:T(8,128)(2,1)S(1)}, bf16[4,128,512]{2,1,0:T(8,128)(2,1)}, u32[]{:S(2)}, u32[]{:S(2)}) %collective-permute-start.6) | collective-permute-done | bytes 524320 | tf_op jit(solution)/shard_map/ppermute | solution.py:81
  74.4 17.3 %all-gather.3.cloned.1.call-done = bf16[16384,512]{1,0:T(8,128)(2,1)} async-done(((bf16[512,512]{1,0:T(8,128)(2,1)}), bf16[16384,512]{1,0:T(8,128)(2,1)}) %all-gather.3.cloned.1.call-update) | async-done | bytes 16777232 | tf_op jit(solution)/shard_map/all_gather | solution.py:95
  91.7 18.4 %shard_map.46 = bf16[32,512]{1,0:T(8,128)(2,1)S(1)} custom-call(s32[8]{0:T(128)S(1)} %and_select_fusion.where, bf16[32,512,512]{2,1,0:T(8,128)(2,1)} %bitcast.25, bf16[4,128,512]{2,1,0:T(8,128)(2,1)S(1)} %bitcast.24, bf16[4,128,512]{2,1,0:T(8,128)(2,1)S(1)} %collective-permute-done.refs_1_, bf16[4,128,512]{2,1,0:T(8,128)(2,1)S(1)} %collective-permute-done.1.refs_2_, ...), custom_call_target="tpu_custom_call" | custom-call | tf_op jit(solution)/shard_map/pallas_call | solution.py:52
  110.0 0.1 broadcast_in_dim_reshape.7
  110.2 0.1 reshape.37
  110.3 13.4 %all_to_all.25 = bf16[8,2,1024]{2,1,0:T(2,128)(2,1)S(1)} all-to-all(bf16[8,2,1024]{2,1,0:T(2,128)(2,1)S(1)} %reshape.37), channel_id=1, replica_groups=mesh['y'=4,'c'=2,'x'=4,'z'=8] {'z'}, dimensions={0} | all-to-all | bytes 65536 | tf_op jit(solution)/shard_map/all_to_all | solution.py:103
  123.7 0.1 reshape.38
  123.8 0.1 fusion.2
  123.9 0.7 copy.14
  (4 shorter events, 0.0 us)
Async XLA Ops:
  6.5 85.1 %all-gather.3.cloned.1.call-start = ((), (), s32[]{:S(2)}) async-start(), calls=%async_computation.2 | async-start | bytes 17301504 | tf_op jit(solution)/shard_map/all_gather | solution.py:95
  24.1 16.1 %collective-permute-start = (bf16[4,128,512]{2,1,0:T(8,128)(2,1)S(1)}, bf16[4,128,512]{2,1,0:T(8,128)(2,1)S(1)}, u32[]{:S(2)}, u32[]{:S(2)}) collective-permute-start(bf16[4,128,512]{2,1,0:T(8,128)(2,1)S(1)} %bitcast.22), channel_id=1, source_target_pairs={{0,1},{1,2},{2,3},{3,4},{4,5},{5,6},{6,7},{7,0},{8,9},{9,10},{10,1... | collective-permute-start | bytes 1572872 | tf_op jit(solution)/shard_map/ppermute | solution.py:77
  25.8 14.4 %collective-permute-start.1 = (bf16[4,128,512]{2,1,0:T(8,128)(2,1)S(1)}, bf16[4,128,512]{2,1,0:T(8,128)(2,1)S(1)}, u32[]{:S(2)}, u32[]{:S(2)}) collective-permute-start(bf16[4,128,512]{2,1,0:T(8,128)(2,1)S(1)} %bitcast.23), channel_id=1, source_target_pairs={{0,7},{1,0},{2,1},{3,2},{4,3},{5,4},{6,5},{7,6},{8,15},{9,8},{10,9... | collective-permute-start | bytes 1572872 | tf_op jit(solution)/shard_map/ppermute | solution.py:78
  40.2 12.2 %collective-permute-start.2 = (bf16[4,128,512]{2,1,0:T(8,128)(2,1)S(1)}, bf16[4,128,512]{2,1,0:T(8,128)(2,1)S(1)}, u32[]{:S(2)}, u32[]{:S(2)}) collective-permute-start(bf16[4,128,512]{2,1,0:T(8,128)(2,1)S(1)} %collective-permute-done.refs_1_), channel_id=1, source_target_pairs={{0,1},{1,2},{2,3},{3,4},{4,5},{5,6},{6,7},{7,0},{8,9},{9,10},{10,1... | collective-permute-start | bytes 1572872 | tf_op jit(solution)/shard_map/ppermute | solution.py:77
  40.2 12.2 %collective-permute-start.3 = (bf16[4,128,512]{2,1,0:T(8,128)(2,1)S(1)}, bf16[4,128,512]{2,1,0:T(8,128)(2,1)S(1)}, u32[]{:S(2)}, u32[]{:S(2)}) collective-permute-start(bf16[4,128,512]{2,1,0:T(8,128)(2,1)S(1)} %collective-permute-done.1.refs_2_), channel_id=1, source_target_pairs={{0,7},{1,0},{2,1},{3,2},{4,3},{5,4},{6,5},{7,6},{8,15},{9,8},{10,9... | collective-permute-start | bytes 1572872 | tf_op jit(solution)/shard_map/ppermute | solution.py:78
  52.4 11.4 %collective-permute-start.4 = (bf16[4,128,512]{2,1,0:T(8,128)(2,1)S(1)}, bf16[4,128,512]{2,1,0:T(8,128)(2,1)S(1)}, u32[]{:S(2)}, u32[]{:S(2)}) collective-permute-start(bf16[4,128,512]{2,1,0:T(8,128)(2,1)S(1)} %collective-permute-done.2.refs_3_), channel_id=1, source_target_pairs={{0,1},{1,2},{2,3},{3,4},{4,5},{5,6},{6,7},{7,0},{8,9},{9,10},{10,1... | collective-permute-start | bytes 1572872 | tf_op jit(solution)/shard_map/ppermute | solution.py:77
  52.4 12.1 %collective-permute-start.5 = (bf16[4,128,512]{2,1,0:T(8,128)(2,1)S(1)}, bf16[4,128,512]{2,1,0:T(8,128)(2,1)}, u32[]{:S(2)}, u32[]{:S(2)}) collective-permute-start(bf16[4,128,512]{2,1,0:T(8,128)(2,1)S(1)} %collective-permute-done.3.refs_4_), channel_id=1, source_target_pairs={{0,7},{1,0},{2,1},{3,2},{4,3},{5,4},{6,5},{7,6},{8,15},{9,8},{10,9... | collective-permute-start | bytes 1572872 | tf_op jit(solution)/shard_map/ppermute | solution.py:78
  63.8 10.6 %collective-permute-start.6 = (bf16[4,128,512]{2,1,0:T(8,128)(2,1)S(1)}, bf16[4,128,512]{2,1,0:T(8,128)(2,1)}, u32[]{:S(2)}, u32[]{:S(2)}) collective-permute-start(bf16[4,128,512]{2,1,0:T(8,128)(2,1)S(1)} %collective-permute-done.4.refs_5_), channel_id=1, source_target_pairs={{0,1},{1,2},{2,3},{3,4},{4,5},{5,6},{6,7},{7,0},{8,9},{9,10},{10,1... | collective-permute-start | bytes 1572872 | tf_op jit(solution)/shard_map/ppermute | solution.py:81
Sparse Core Ops, SparseCore 0:
  9.9 81.7 all-gather.2

commit v2 on v0

v2 whole, which is shorter than its diff:
```python
import jax
import jax.numpy as jnp
from jax import lax
from jax.experimental import pallas as pl
from jax.experimental.pallas import tpu as pltpu
from jax.sharding import Mesh, PartitionSpec as P

LEN = 64
AXES = ("y", "c", "x", "z")
NY, NC, NX, NZ = SIZES = (4, 2, 4, 8)


def permute(block, move):
    pairs = []
    for y in range(NY):
        for c in range(NC):
            for x in range(NX):
                for z in range(NZ):
                    to = [a % n for a, n in zip(move(y, c, x, z), SIZES)]
                    pairs.append(
                        (
                            ((y * NC + c) * NX + x) * NZ + z,
                            ((to[0] * NC + to[1]) * NX + to[2]) * NZ + to[3],
                        )
                    )
    return lax.ppermute(block, AXES, pairs)


def swap(block):
    return permute(block, lambda y, c, x, z: (y, 1 - c, x, z))


def first(block, s):
    return permute(
        block, lambda y, c, x, z: (y + s, c, x, z) if c == 0 else (y, c, x + s, z)
    )


def second(block, s):
    return permute(
        block, lambda y, c, x, z: (y, c, x + s, z) if c == 0 else (y + s, c, x, z)
    )


def along_z(block):
    return permute(
        block, lambda y, c, x, z: (y, c, x, z + 1) if c == 0 else (y, c, x, z - 1)
    )


def gather_hidden(own):
    lower = first(own, 1)
    upper = first(own, -1)
    three = jnp.concatenate([own, lower, upper], axis=0)
    far = first(upper, -1)
    three_lower = second(three, 1)
    three_upper = second(three, -1)
    far_lower = second(far, 1)
    far_upper = second(far, -1)
    three_far = second(three_lower, 1)
    far_far = second(far_upper, -1)
    return [
        (three, 0),
        (far, 0),
        (three_lower, -1),
        (three_upper, 1),
        (far_lower, -1),
        (far_upper, 1),
        (three_far, 2),
        (far_far, 2),
    ]


def gather_head(piece):
    own = jnp.stack([piece, swap(piece)])
    out = [(own, 0, True)]
    block = own
    for s in range(1, NZ // 2):
        block = along_z(block)
        out += [(block, -s, True), (swap(block), s, False)]
    last = along_z(block[:1])
    out += [(last, NZ // 2, True), (swap(last), NZ // 2, False)]
    return out


def pool_kernel(units, parts, place, *refs):
    n, m = len(units), len(parts)
    hid, head, (o_ref, w, acc) = refs[:n], refs[n : n + m], refs[n + m :]
    y, c, x, z = (place[i] for i in range(4))
    for ref, (steps, mine) in zip(head, parts):
        sign = 1 - 2 * c
        at_z = lax.rem(z + sign * steps + NZ, NZ)
        rows = ref.shape[2]
        for q in range(ref.shape[0]):
            col = c if (q == 0) == mine else 1 - c

            def place_rows(i, _):
                at_x = lax.rem(x - i + NX, NX)
                to = pl.multiple_of((at_x * NZ + at_z) * rows, rows)
                w[col, pl.ds(to, rows), :] = ref[q, i]
                return 0

            lax.fori_loop(0, NX, place_rows, 0)
    acc[...] = jnp.zeros_like(acc)
    depth = hid[0].shape[-1]
    for ref, b in zip(hid, units):

        def unit(u, _):
            a = jnp.where(u == 2, 1, -u) if ref.shape[0] > 1 else 2
            at_y = lax.rem(y + jnp.where(c == 0, a, b) + NY, NY)
            at_x = lax.rem(x + jnp.where(c == 0, b, a) + NX, NX)
            for col in range(NC):
                total = acc[at_x, :, col * w.shape[2] : (col + 1) * w.shape[2]]
                for h in range(NC):
                    f = c if h == 0 else 1 - c
                    row = pl.multiple_of((at_y * NC + f) * depth, depth)
                    total += jnp.dot(
                        ref[u, h],
                        w[col, pl.ds(row, depth), :],
                        preferred_element_type=jnp.float32,
                    )
                acc[at_x, :, col * w.shape[2] : (col + 1) * w.shape[2]] = total
            return 0

        lax.fori_loop(0, ref.shape[0], unit, 0)
    for i in range(NX):
        tokens, cols = acc.shape[1:]
        top = jnp.max(acc[i].reshape(tokens // LEN, LEN, cols), axis=1)
        o_ref[i] = jnp.log1p(jnp.maximum(top, 0.0))


def pool(place, hid, head):
    tokens, depth = hid[0][0].shape[-2:]
    rows, cols = head[0][0].shape[-2:]
    whole = pl.BlockSpec(memory_space=pltpu.VMEM)
    arrays = [h[0] for h in hid] + [h[0] for h in head]

    def kernel(*refs):
        pool_kernel([h[1] for h in hid], [h[1:] for h in head], *refs)

    return pl.pallas_call(
        kernel,
        out_shape=jax.ShapeDtypeStruct((NX, tokens // LEN, NC * cols), jnp.float32),
        in_specs=[pl.BlockSpec(memory_space=pltpu.SMEM)] + [whole] * len(arrays),
        out_specs=whole,
        scratch_shapes=[
            pltpu.VMEM((NC, NX * NZ * rows, cols), jnp.bfloat16),
            pltpu.VMEM((NX, tokens, NC * cols), jnp.float32),
        ],
        compiler_params=pltpu.CompilerParams(vmem_limit_bytes=50 << 20),
    )(place, *arrays)


def body(hidden, head_weight, lengths):
    y, c, x, z = (lax.axis_index(a) for a in AXES)
    tokens, features = hidden.shape
    rows, cols = head_weight.shape
    per = tokens // lengths.shape[0]
    allowed = jnp.arange(per, dtype=jnp.int32)[None, :] < lengths[:, None]
    hidden = jnp.where(
        allowed[:, :, None], hidden.reshape(-1, per, features), 0
    ).reshape(NC, tokens // NC, features)
    kept = lax.dynamic_index_in_dim(hidden, c, 0, keepdims=False)
    other = swap(lax.dynamic_index_in_dim(hidden, 1 - c, 0, keepdims=False))
    units = gather_hidden(jnp.stack([kept, other])[None])

    width = cols // NX
    mine = [lax.dynamic_slice(head_weight, (0, x * width), (rows, width))]
    for s in range(1, NX):
        to = lax.rem(x + s, NX)
        block = lax.dynamic_slice(head_weight, (0, to * width), (rows, width))
        mine.append(permute(block, lambda y, c, x, z: (y, c, x + s, z)))
    parts = gather_head(jnp.stack(mine))

    place = jnp.stack([y, c, x, z]).astype(jnp.int32)
    pooled = pool(place, units, parts).astype(jnp.bfloat16)
    each = width // NZ
    pooled = pooled.reshape(NX * pooled.shape[1], NC, NZ, each)
    pooled = jnp.transpose(pooled, (2, 1, 0, 3)).reshape(NZ * NC, -1, each)
    got = lax.all_to_all(pooled, ("z", "c"), split_axis=0, concat_axis=0, tiled=True)
    got = got.reshape(NZ, NC, NX, -1, each)
    got = jnp.transpose(got, (2, 0, 1, 3, 4)).reshape(-1, each).astype(jnp.float32)
    peak = jnp.max(got, axis=0)
    return jnp.transpose((got / (1.0 + peak)[None, :]).astype(jnp.bfloat16))


def solution(mesh):
    fine = Mesh(mesh.devices.reshape(SIZES), AXES)
    return jax.shard_map(
        body,
        mesh=fine,
        in_specs=(P(("x", "z"), ("y", "c")), P(("x", "z"), ("y", "c")), P(("x", "z"))),
        out_specs=P(("y", "c", "x", "z"), None),
        check_vma=False,
    )
```

time: 298 us -> 117 us (0.39)
  the two profiles are of different devices: /device:TPU:8 before, /device:TPU:1 now
where the time goes in v2:
time: 117 us; the launch traced here: 116 us
  waiting for transfers between devices  45.2 us (39%)
  starting transfers between devices  37.4 us (32%)
  Pallas kernels  17.9 us (15%)
  blocking collectives  11.2 us (10%)
  local copies, waits for them, and re-layouts  3.68 us (3%)
    ppermute x22, waiting for transfers between devices, permute(): return lax.ppermute(block, AXES, pairs)  45.2 us
    ppermute x22, starting transfers between devices, permute(): return lax.ppermute(block, AXES, pairs)  37.4 us
    pallas_call x1, Pallas kernels, pool(): pl.pallas_call(kernel, out_shape=jax.ShapeDtypeStruct((NX, tokens // LEN,...  17.9 us
    all_to_all x1, blocking collectives, body(): lax.all_to_all(pooled, ('z', 'c'), split_axis=0, concat_axis=0, tiled=True)  11.2 us
  transfers between devices with their start and end apart: 22, of which 13 were waited for; matrix products, arithmetic and copies ran while one was open for 2% of the time, Pallas kernels for 0%

profile of v2, /device:TPU:1, one launch (start us, length us, event | category | flops | bytes accessed | tf_op | source)
XLA Modules:
  0.0 116.3 jit_solution(6887640330162758403)
XLA Ops:
  0.0 1.1 dynamic-slice_bitcast_fusion.1
  1.1 2.1 %collective-permute-start.10 = (bf16[128,512]{1,0:T(8,128)(2,1)S(1)}, bf16[128,512]{1,0:T(8,128)(2,1)S(1)}, u32[]{:S(2)}, u32[]{:S(2)}) collective-permute-start(bf16[128,512]{1,0:T(8,128)(2,1)S(1)} %get-tuple-element.8), channel_id=1, source_target_pairs={{0,8},{1,9},{2,10},{3,11},{4,12},{5,13},{6,14},{7,15},{8,16},{9,17... | collective-permute-start | bytes 393224 | tf_op jit(solution)/shard_map/ppermute | solution.py:26
  3.3 1.4 %collective-permute-start.12 = (bf16[128,512]{1,0:T(8,128)(2,1)S(1)}, bf16[128,512]{1,0:T(8,128)(2,1)S(1)}, u32[]{:S(2)}, u32[]{:S(2)}) collective-permute-start(bf16[128,512]{1,0:T(8,128)(2,1)S(1)} %get-tuple-element.9), channel_id=1, source_target_pairs={{0,24},{1,25},{2,26},{3,27},{4,28},{5,29},{6,30},{7,31},{8,0},{9,1... | collective-permute-start | bytes 393224 | tf_op jit(solution)/shard_map/ppermute | solution.py:26
  4.6 1.6 %collective-permute-start.11 = (bf16[128,512]{1,0:T(8,128)(2,1)S(1)}, bf16[128,512]{1,0:T(8,128)(2,1)S(1)}, u32[]{:S(2)}, u32[]{:S(2)}) collective-permute-start(bf16[128,512]{1,0:T(8,128)(2,1)S(1)} %get-tuple-element.10), channel_id=1, source_target_pairs={{0,16},{1,17},{2,18},{3,19},{4,20},{5,21},{6,22},{7,23},{8,24},{9,... | collective-permute-start | bytes 393224 | tf_op jit(solution)/shard_map/ppermute | solution.py:26
  7.1 3.8 %collective-permute-done.11 = bf16[128,512]{1,0:T(8,128)(2,1)S(1)} collective-permute-done((bf16[128,512]{1,0:T(8,128)(2,1)S(1)}, bf16[128,512]{1,0:T(8,128)(2,1)S(1)}, u32[]{:S(2)}, u32[]{:S(2)}) %collective-permute-start.11) | collective-permute-done | bytes 131104 | tf_op jit(solution)/shard_map/ppermute | solution.py:26
  11.0 3.3 %collective-permute-start.13 = (bf16[4,128,512]{2,1,0:T(8,128)(2,1)S(1)}, bf16[4,128,512]{2,1,0:T(8,128)(2,1)S(1)}, u32[]{:S(2)}, u32[]{:S(2)}) collective-permute-start(bf16[4,128,512]{2,1,0:T(8,128)(2,1)S(1)} %get-tuple-element.6), channel_id=1, source_target_pairs={{0,32},{1,33},{2,34},{3,35},{4,36},{5,37},{6,38},{7,39},{8,40},{9,... | collective-permute-start | bytes 1572872 | tf_op jit(solution)/shard_map/ppermute | solution.py:26
  14.7 1.2 %collective-permute-done.13 = bf16[4,128,512]{2,1,0:T(8,128)(2,1)S(1)} collective-permute-done((bf16[4,128,512]{2,1,0:T(8,128)(2,1)S(1)}, bf16[4,128,512]{2,1,0:T(8,128)(2,1)S(1)}, u32[]{:S(2)}, u32[]{:S(2)}) %collective-permute-start.13) | collective-permute-done | bytes 524320 | tf_op jit(solution)/shard_map/ppermute | solution.py:26
  16.0 4.4 %collective-permute-start.14 = (bf16[2,4,128,512]{3,2,1,0:T(8,128)(2,1)S(1)}, bf16[2,4,128,512]{3,2,1,0:T(8,128)(2,1)}, u32[]{:S(2)}, u32[]{:S(2)}) collective-permute-start(bf16[2,4,128,512]{3,2,1,0:T(8,128)(2,1)S(1)} %pad_maximum_fusion.1.refs_9_), channel_id=1, source_target_pairs={{0,1},{1,2},{2,3},{3,4},{4,5},{5,6},{6,7},{7,0},{8,9},{9,10},{10,1... | collective-permute-start | bytes 3145736 | tf_op jit(solution)/shard_map/ppermute | solution.py:26
  20.8 1.5 %collective-permute-done = bf16[256,512]{1,0:T(8,128)(2,1)S(1)} collective-permute-done((bf16[256,512]{1,0:T(8,128)(2,1)S(1)}, bf16[256,512]{1,0:T(8,128)(2,1)S(1)}, u32[]{:S(2)}, u32[]{:S(2)}) %collective-permute-start) | collective-permute-done | bytes 262176 | tf_op jit(solution)/shard_map/ppermute | solution.py:26
  22.3 1.8 %collective-permute-start.2 = (bf16[1,2,256,512]{3,2,1,0:T(8,128)(2,1)S(1)}, bf16[1,2,256,512]{3,2,1,0:T(8,128)(2,1)S(1)}, u32[]{:S(2)}, u32[]{:S(2)}) collective-permute-start(bf16[1,2,256,512]{3,2,1,0:T(8,128)(2,1)S(1)} %maximum_bitcast_fusion), channel_id=1, source_target_pairs={{0,192},{1,193},{2,194},{3,195},{4,196},{5,197},{6,198},{7,199},{8... | collective-permute-start | bytes 1572872 | tf_op jit(solution)/shard_map/ppermute | solution.py:26
  24.1 8.1 %collective-permute-done.14.refs_10_ = bf16[2,4,128,512]{3,2,1,0:T(8,128)(2,1)} collective-permute-done((bf16[2,4,128,512]{3,2,1,0:T(8,128)(2,1)S(1)}, bf16[2,4,128,512]{3,2,1,0:T(8,128)(2,1)}, u32[]{:S(2)}, u32[]{:S(2)}) %collective-permute-start.14) | collective-permute-done | bytes 1048608 | tf_op jit(solution)/shard_map/ppermute | solution.py:26
  32.2 3.4 %collective-permute-start.16 = (bf16[2,4,128,512]{3,2,1,0:T(8,128)(2,1)}, bf16[2,4,128,512]{3,2,1,0:T(8,128)(2,1)}, u32[]{:S(2)}, u32[]{:S(2)}) collective-permute-start(bf16[2,4,128,512]{3,2,1,0:T(8,128)(2,1)} %collective-permute-done.14.refs_10_), channel_id=1, source_target_pairs={{0,1},{1,2},{2,3},{3,4},{4,5},{5,6},{6,7},{7,0},{8,9},{9,10},{10,1... | collective-permute-start | bytes 3145736 | tf_op jit(solution)/shard_map/ppermute | solution.py:26
  35.8 1.2 %collective-permute-start.4 = (bf16[3,2,256,512]{3,2,1,0:T(8,128)(2,1)S(1)}, bf16[3,2,256,512]{3,2,1,0:T(8,128)(2,1)}, u32[]{:S(2)}, u32[]{:S(2)}) collective-permute-start(bf16[3,2,256,512]{3,2,1,0:T(8,128)(2,1)S(1)} %pad_maximum_fusion.refs_1_), channel_id=1, source_target_pairs={{0,8},{1,9},{2,10},{3,11},{4,12},{5,13},{6,14},{7,15},{8,16},{9,17... | collective-permute-start | bytes 4718600 | tf_op jit(solution)/shard_map/ppermute | solution.py:26
  37.0 1.6 %collective-permute-start.5 = (bf16[3,2,256,512]{3,2,1,0:T(8,128)(2,1)S(1)}, bf16[3,2,256,512]{3,2,1,0:T(8,128)(2,1)S(1)}, u32[]{:S(2)}, u32[]{:S(2)}) collective-permute-start(bf16[3,2,256,512]{3,2,1,0:T(8,128)(2,1)S(1)} %pad_maximum_fusion.refs_1_), channel_id=1, source_target_pairs={{0,24},{1,25},{2,26},{3,27},{4,28},{5,29},{6,30},{7,31},{8,0},{9,1... | collective-permute-start | bytes 4718600 | tf_op jit(solution)/shard_map/ppermute | solution.py:26
  38.6 1.7 %collective-permute-start.3 = (bf16[1,2,256,512]{3,2,1,0:T(8,128)(2,1)S(1)}, bf16[1,2,256,512]{3,2,1,0:T(8,128)(2,1)S(1)}, u32[]{:S(2)}, u32[]{:S(2)}) collective-permute-start(bf16[1,2,256,512]{3,2,1,0:T(8,128)(2,1)S(1)} %collective-permute-done.2), channel_id=1, source_target_pairs={{0,192},{1,193},{2,194},{3,195},{4,196},{5,197},{6,198},{7,199},{8... | collective-permute-start | bytes 1572872 | tf_op jit(solution)/shard_map/ppermute | solution.py:26
  40.3 7.4 %collective-permute-done.16.refs_12_ = bf16[2,4,128,512]{3,2,1,0:T(8,128)(2,1)} collective-permute-done((bf16[2,4,128,512]{3,2,1,0:T(8,128)(2,1)}, bf16[2,4,128,512]{3,2,1,0:T(8,128)(2,1)}, u32[]{:S(2)}, u32[]{:S(2)}) %collective-permute-start.16) | collective-permute-done | bytes 1048608 | tf_op jit(solution)/shard_map/ppermute | solution.py:26
  47.7 3.4 %collective-permute-start.18 = (bf16[2,4,128,512]{3,2,1,0:T(8,128)(2,1)}, bf16[2,4,128,512]{3,2,1,0:T(8,128)(2,1)}, u32[]{:S(2)}, u32[]{:S(2)}) collective-permute-start(bf16[2,4,128,512]{3,2,1,0:T(8,128)(2,1)} %collective-permute-done.16.refs_12_), channel_id=1, source_target_pairs={{0,1},{1,2},{2,3},{3,4},{4,5},{5,6},{6,7},{7,0},{8,9},{9,10},{10,1... | collective-permute-start | bytes 3145736 | tf_op jit(solution)/shard_map/ppermute | solution.py:26
  51.1 1.5 %collective-permute-done.3.refs_2_ = bf16[1,2,256,512]{3,2,1,0:T(8,128)(2,1)S(1)} collective-permute-done((bf16[1,2,256,512]{3,2,1,0:T(8,128)(2,1)S(1)}, bf16[1,2,256,512]{3,2,1,0:T(8,128)(2,1)S(1)}, u32[]{:S(2)}, u32[]{:S(2)}) %collective-permute-start.3) | collective-permute-done | bytes 524320 | tf_op jit(solution)/shard_map/ppermute | solution.py:26
  52.6 1.4 %collective-permute-start.7 = (bf16[1,2,256,512]{3,2,1,0:T(8,128)(2,1)S(1)}, bf16[1,2,256,512]{3,2,1,0:T(8,128)(2,1)S(1)}, u32[]{:S(2)}, u32[]{:S(2)}) collective-permute-start(bf16[1,2,256,512]{3,2,1,0:T(8,128)(2,1)S(1)} %collective-permute-done.3.refs_2_), channel_id=1, source_target_pairs={{0,24},{1,25},{2,26},{3,27},{4,28},{5,29},{6,30},{7,31},{8,0},{9,1... | collective-permute-start | bytes 1572872 | tf_op jit(solution)/shard_map/ppermute | solution.py:26
  54.0 2.7 %collective-permute-done.4.refs_3_ = bf16[3,2,256,512]{3,2,1,0:T(8,128)(2,1)} collective-permute-done((bf16[3,2,256,512]{3,2,1,0:T(8,128)(2,1)S(1)}, bf16[3,2,256,512]{3,2,1,0:T(8,128)(2,1)}, u32[]{:S(2)}, u32[]{:S(2)}) %collective-permute-start.4) | collective-permute-done | bytes 1572896 | tf_op jit(solution)/shard_map/ppermute | solution.py:26
  56.8 11.1 %collective-permute-done.7.refs_6_ = bf16[1,2,256,512]{3,2,1,0:T(8,128)(2,1)S(1)} collective-permute-done((bf16[1,2,256,512]{3,2,1,0:T(8,128)(2,1)S(1)}, bf16[1,2,256,512]{3,2,1,0:T(8,128)(2,1)S(1)}, u32[]{:S(2)}, u32[]{:S(2)}) %collective-permute-start.7) | collective-permute-done | bytes 524320 | tf_op jit(solution)/shard_map/ppermute | solution.py:26
  67.9 2.8 %collective-permute-start.9 = (bf16[1,2,256,512]{3,2,1,0:T(8,128)(2,1)S(1)}, bf16[1,2,256,512]{3,2,1,0:T(8,128)(2,1)S(1)}, u32[]{:S(2)}, u32[]{:S(2)}) collective-permute-start(bf16[1,2,256,512]{3,2,1,0:T(8,128)(2,1)S(1)} %collective-permute-done.7.refs_6_), channel_id=1, source_target_pairs={{0,24},{1,25},{2,26},{3,27},{4,28},{5,29},{6,30},{7,31},{8,0},{9,1... | collective-permute-start | bytes 1572872 | tf_op jit(solution)/shard_map/ppermute | solution.py:26
  70.7 1.7 %collective-permute-start.15 = (bf16[2,4,128,512]{3,2,1,0:T(8,128)(2,1)}, bf16[2,4,128,512]{3,2,1,0:T(8,128)(2,1)}, u32[]{:S(2)}, u32[]{:S(2)}) collective-permute-start(bf16[2,4,128,512]{3,2,1,0:T(8,128)(2,1)} %collective-permute-done.14.refs_10_), channel_id=1, source_target_pairs={{0,32},{1,33},{2,34},{3,35},{4,36},{5,37},{6,38},{7,39},{8,40},{9,... | collective-permute-start | bytes 3145736 | tf_op jit(solution)/shard_map/ppermute | solution.py:26
  72.3 1.1 slice.4
  74.2 2.5 %collective-permute-done.9.refs_8_ = bf16[1,2,256,512]{3,2,1,0:T(8,128)(2,1)S(1)} collective-permute-done((bf16[1,2,256,512]{3,2,1,0:T(8,128)(2,1)S(1)}, bf16[1,2,256,512]{3,2,1,0:T(8,128)(2,1)S(1)}, u32[]{:S(2)}, u32[]{:S(2)}) %collective-permute-start.9) | collective-permute-done | bytes 524320 | tf_op jit(solution)/shard_map/ppermute | solution.py:26
  76.8 2.2 %collective-permute-start.19 = (bf16[2,4,128,512]{3,2,1,0:T(8,128)(2,1)}, bf16[2,4,128,512]{3,2,1,0:T(8,128)(2,1)}, u32[]{:S(2)}, u32[]{:S(2)}) collective-permute-start(bf16[2,4,128,512]{3,2,1,0:T(8,128)(2,1)} %collective-permute-done.18.refs_14_), channel_id=1, source_target_pairs={{0,32},{1,33},{2,34},{3,35},{4,36},{5,37},{6,38},{7,39},{8,40},{9,... | collective-permute-start | bytes 3145736 | tf_op jit(solution)/shard_map/ppermute | solution.py:26
  79.0 3.0 %collective-permute-done.20.refs_16_ = bf16[1,4,128,512]{3,2,1,0:T(8,128)(2,1)S(1)} collective-permute-done((bf16[1,4,128,512]{3,2,1,0:T(8,128)(2,1)S(1)}, bf16[1,4,128,512]{3,2,1,0:T(8,128)(2,1)S(1)}, u32[]{:S(2)}, u32[]{:S(2)}) %collective-permute-start.20) | collective-permute-done | bytes 524320 | tf_op jit(solution)/shard_map/ppermute | solution.py:26
  82.1 2.4 %collective-permute-start.21 = (bf16[1,4,128,512]{3,2,1,0:T(8,128)(2,1)S(1)}, bf16[1,4,128,512]{3,2,1,0:T(8,128)(2,1)S(1)}, u32[]{:S(2)}, u32[]{:S(2)}) collective-permute-start(bf16[1,4,128,512]{3,2,1,0:T(8,128)(2,1)S(1)} %collective-permute-done.20.refs_16_), channel_id=1, source_target_pairs={{0,32},{1,33},{2,34},{3,35},{4,36},{5,37},{6,38},{7,39},{8,40},{9,... | collective-permute-start | bytes 1572872 | tf_op jit(solution)/shard_map/ppermute | solution.py:26
  84.5 1.4 %collective-permute-done.21.refs_17_ = bf16[1,4,128,512]{3,2,1,0:T(8,128)(2,1)S(1)} collective-permute-done((bf16[1,4,128,512]{3,2,1,0:T(8,128)(2,1)S(1)}, bf16[1,4,128,512]{3,2,1,0:T(8,128)(2,1)S(1)}, u32[]{:S(2)}, u32[]{:S(2)}) %collective-permute-start.21) | collective-permute-done | bytes 524320 | tf_op jit(solution)/shard_map/ppermute | solution.py:26
  86.0 17.9 %shard_map.37 = f32[4,4,1024]{2,1,0:T(4,128)S(1)} custom-call(s32[4]{0:T(128)S(1)} %pad_add_fusion.refs_0_, bf16[3,2,256,512]{3,2,1,0:T(8,128)(2,1)} %copy-done, bf16[1,2,256,512]{3,2,1,0:T(8,128)(2,1)S(1)} %collective-permute-done.3.refs_2_, bf16[3,2,256,512]{3,2,1,0:T(8,128)(2,1)} %collective-permute-done.4.refs_3_, bf16[3,2,256,512]{3,2,1,0:T(8,128)(2,1)} %copy-done.2, ...), custom_call_target="tpu_custom_call" | custom-call | tf_op jit(solution)/shard_map/pallas_call | solution.py:141
  104.1 11.2 %all_to_all.5 = bf16[16,2,512]{2,1,0:T(2,128)(2,1)S(1)} all-to-all(bf16[16,2,512]{2,1,0:T(2,128)(2,1)S(1)} %reshape.50), channel_id=1, replica_groups=mesh['y'=4,'c'=2,'x'=4,'z'=8] {'z','c'}, dimensions={0} | all-to-all | bytes 65536 | tf_op jit(solution)/shard_map/all_to_all | solution.py:180
  115.6 0.7 copy.6
  (49 shorter events, 3.3 us)
Async XLA Ops:
  0.0 14.4 %copy-start.4 = (s32[8]{0:T(128)S(1)}, s32[8]{0:T(128)}, u32[]{:S(2)}) copy-start(s32[8]{0:T(128)} %param.5) | copy-start | bytes 100
  1.1 5.7 %collective-permute-start.10 = (bf16[128,512]{1,0:T(8,128)(2,1)S(1)}, bf16[128,512]{1,0:T(8,128)(2,1)S(1)}, u32[]{:S(2)}, u32[]{:S(2)}) collective-permute-start(bf16[128,512]{1,0:T(8,128)(2,1)S(1)} %get-tuple-element.8), channel_id=1, source_target_pairs={{0,8},{1,9},{2,10},{3,11},{4,12},{5,13},{6,14},{7,15},{8,16},{9,17... | collective-permute-start | bytes 393224 | tf_op jit(solution)/shard_map/ppermute | solution.py:26
  3.3 3.8 %collective-permute-start.12 = (bf16[128,512]{1,0:T(8,128)(2,1)S(1)}, bf16[128,512]{1,0:T(8,128)(2,1)S(1)}, u32[]{:S(2)}, u32[]{:S(2)}) collective-permute-start(bf16[128,512]{1,0:T(8,128)(2,1)S(1)} %get-tuple-element.9), channel_id=1, source_target_pairs={{0,24},{1,25},{2,26},{3,27},{4,28},{5,29},{6,30},{7,31},{8,0},{9,1... | collective-permute-start | bytes 393224 | tf_op jit(solution)/shard_map/ppermute | solution.py:26
  4.6 6.3 %collective-permute-start.11 = (bf16[128,512]{1,0:T(8,128)(2,1)S(1)}, bf16[128,512]{1,0:T(8,128)(2,1)S(1)}, u32[]{:S(2)}, u32[]{:S(2)}) collective-permute-start(bf16[128,512]{1,0:T(8,128)(2,1)S(1)} %get-tuple-element.10), channel_id=1, source_target_pairs={{0,16},{1,17},{2,18},{3,19},{4,20},{5,21},{6,22},{7,23},{8,24},{9,... | collective-permute-start | bytes 393224 | tf_op jit(solution)/shard_map/ppermute | solution.py:26
  10.9 9.5 %copy-start.3 = (bf16[512,512]{1,0:T(8,128)(2,1)S(1)}, bf16[512,512]{1,0:T(8,128)(2,1)}, u32[]{:S(2)}) copy-start(bf16[512,512]{1,0:T(8,128)(2,1)} %param.3) | copy-start | bytes 1572868
  11.0 4.9 %collective-permute-start.13 = (bf16[4,128,512]{2,1,0:T(8,128)(2,1)S(1)}, bf16[4,128,512]{2,1,0:T(8,128)(2,1)S(1)}, u32[]{:S(2)}, u32[]{:S(2)}) collective-permute-start(bf16[4,128,512]{2,1,0:T(8,128)(2,1)S(1)} %get-tuple-element.6), channel_id=1, source_target_pairs={{0,32},{1,33},{2,34},{3,35},{4,36},{5,37},{6,38},{7,39},{8,40},{9,... | collective-permute-start | bytes 1572872 | tf_op jit(solution)/shard_map/ppermute | solution.py:26
  16.0 6.3 %copy-start.1 = (bf16[2,4,128,512]{3,2,1,0:T(8,128)(2,1)}, bf16[2,4,128,512]{3,2,1,0:T(8,128)(2,1)S(1)}, u32[]{:S(2)}) copy-start(bf16[2,4,128,512]{3,2,1,0:T(8,128)(2,1)S(1)} %pad_maximum_fusion.1.refs_9_) | copy-start | bytes 3145732
  16.0 16.2 %collective-permute-start.14 = (bf16[2,4,128,512]{3,2,1,0:T(8,128)(2,1)S(1)}, bf16[2,4,128,512]{3,2,1,0:T(8,128)(2,1)}, u32[]{:S(2)}, u32[]{:S(2)}) collective-permute-start(bf16[2,4,128,512]{3,2,1,0:T(8,128)(2,1)S(1)} %pad_maximum_fusion.1.refs_9_), channel_id=1, source_target_pairs={{0,1},{1,2},{2,3},{3,4},{4,5},{5,6},{6,7},{7,0},{8,9},{9,10},{10,1... | collective-permute-start | bytes 3145736 | tf_op jit(solution)/shard_map/ppermute | solution.py:26
  20.7 1.6 %collective-permute-start = (bf16[256,512]{1,0:T(8,128)(2,1)S(1)}, bf16[256,512]{1,0:T(8,128)(2,1)S(1)}, u32[]{:S(2)}, u32[]{:S(2)}) collective-permute-start(bf16[256,512]{1,0:T(8,128)(2,1)S(1)} %get-tuple-element.12), channel_id=1, source_target_pairs={{0,32},{1,33},{2,34},{3,35},{4,36},{5,37},{6,38},{7,39},{8,40},{9,... | collective-permute-start | bytes 786440 | tf_op jit(solution)/shard_map/ppermute | solution.py:26
  22.3 13.3 %collective-permute-start.2 = (bf16[1,2,256,512]{3,2,1,0:T(8,128)(2,1)S(1)}, bf16[1,2,256,512]{3,2,1,0:T(8,128)(2,1)S(1)}, u32[]{:S(2)}, u32[]{:S(2)}) collective-permute-start(bf16[1,2,256,512]{3,2,1,0:T(8,128)(2,1)S(1)} %maximum_bitcast_fusion), channel_id=1, source_target_pairs={{0,192},{1,193},{2,194},{3,195},{4,196},{5,197},{6,198},{7,199},{8... | collective-permute-start | bytes 1572872 | tf_op jit(solution)/shard_map/ppermute | solution.py:26
  24.1 11.5 %collective-permute-start.1 = (bf16[1,2,256,512]{3,2,1,0:T(8,128)(2,1)S(1)}, bf16[1,2,256,512]{3,2,1,0:T(8,128)(2,1)S(1)}, u32[]{:S(2)}, u32[]{:S(2)}) collective-permute-start(bf16[1,2,256,512]{3,2,1,0:T(8,128)(2,1)S(1)} %maximum_bitcast_fusion), channel_id=1, source_target_pairs={{0,64},{1,65},{2,66},{3,67},{4,68},{5,69},{6,70},{7,71},{8,72},{9,... | collective-permute-start | bytes 1572872 | tf_op jit(solution)/shard_map/ppermute | solution.py:26
  32.2 15.5 %collective-permute-start.16 = (bf16[2,4,128,512]{3,2,1,0:T(8,128)(2,1)}, bf16[2,4,128,512]{3,2,1,0:T(8,128)(2,1)}, u32[]{:S(2)}, u32[]{:S(2)}) collective-permute-start(bf16[2,4,128,512]{3,2,1,0:T(8,128)(2,1)} %collective-permute-done.14.refs_10_), channel_id=1, source_target_pairs={{0,1},{1,2},{2,3},{3,4},{4,5},{5,6},{6,7},{7,0},{8,9},{9,10},{10,1... | collective-permute-start | bytes 3145736 | tf_op jit(solution)/shard_map/ppermute | solution.py:26
  35.8 46.3 %copy-start = (bf16[3,2,256,512]{3,2,1,0:T(8,128)(2,1)}, bf16[3,2,256,512]{3,2,1,0:T(8,128)(2,1)S(1)}, u32[]{:S(2)}) copy-start(bf16[3,2,256,512]{3,2,1,0:T(8,128)(2,1)S(1)} %pad_maximum_fusion.refs_1_) | copy-start | bytes 4718596
  35.8 21.0 %collective-permute-start.4 = (bf16[3,2,256,512]{3,2,1,0:T(8,128)(2,1)S(1)}, bf16[3,2,256,512]{3,2,1,0:T(8,128)(2,1)}, u32[]{:S(2)}, u32[]{:S(2)}) collective-permute-start(bf16[3,2,256,512]{3,2,1,0:T(8,128)(2,1)S(1)} %pad_maximum_fusion.refs_1_), channel_id=1, source_target_pairs={{0,8},{1,9},{2,10},{3,11},{4,12},{5,13},{6,14},{7,15},{8,16},{9,17... | collective-permute-start | bytes 4718600 | tf_op jit(solution)/shard_map/ppermute | solution.py:26
  37.0 36.5 %collective-permute-start.5 = (bf16[3,2,256,512]{3,2,1,0:T(8,128)(2,1)S(1)}, bf16[3,2,256,512]{3,2,1,0:T(8,128)(2,1)S(1)}, u32[]{:S(2)}, u32[]{:S(2)}) collective-permute-start(bf16[3,2,256,512]{3,2,1,0:T(8,128)(2,1)S(1)} %pad_maximum_fusion.refs_1_), channel_id=1, source_target_pairs={{0,24},{1,25},{2,26},{3,27},{4,28},{5,29},{6,30},{7,31},{8,0},{9,1... | collective-permute-start | bytes 4718600 | tf_op jit(solution)/shard_map/ppermute | solution.py:26
  38.6 14.0 %collective-permute-start.3 = (bf16[1,2,256,512]{3,2,1,0:T(8,128)(2,1)S(1)}, bf16[1,2,256,512]{3,2,1,0:T(8,128)(2,1)S(1)}, u32[]{:S(2)}, u32[]{:S(2)}) collective-permute-start(bf16[1,2,256,512]{3,2,1,0:T(8,128)(2,1)S(1)} %collective-permute-done.2), channel_id=1, source_target_pairs={{0,192},{1,193},{2,194},{3,195},{4,196},{5,197},{6,198},{7,199},{8... | collective-permute-start | bytes 1572872 | tf_op jit(solution)/shard_map/ppermute | solution.py:26
  47.7 23.0 %collective-permute-start.18 = (bf16[2,4,128,512]{3,2,1,0:T(8,128)(2,1)}, bf16[2,4,128,512]{3,2,1,0:T(8,128)(2,1)}, u32[]{:S(2)}, u32[]{:S(2)}) collective-permute-start(bf16[2,4,128,512]{3,2,1,0:T(8,128)(2,1)} %collective-permute-done.16.refs_12_), channel_id=1, source_target_pairs={{0,1},{1,2},{2,3},{3,4},{4,5},{5,6},{6,7},{7,0},{8,9},{9,10},{10,1... | collective-permute-start | bytes 3145736 | tf_op jit(solution)/shard_map/ppermute | solution.py:26
  52.6 15.3 %collective-permute-start.7 = (bf16[1,2,256,512]{3,2,1,0:T(8,128)(2,1)S(1)}, bf16[1,2,256,512]{3,2,1,0:T(8,128)(2,1)S(1)}, u32[]{:S(2)}, u32[]{:S(2)}) collective-permute-start(bf16[1,2,256,512]{3,2,1,0:T(8,128)(2,1)S(1)} %collective-permute-done.3.refs_2_), channel_id=1, source_target_pairs={{0,24},{1,25},{2,26},{3,27},{4,28},{5,29},{6,30},{7,31},{8,0},{9,1... | collective-permute-start | bytes 1572872 | tf_op jit(solution)/shard_map/ppermute | solution.py:26
  54.0 19.4 %collective-permute-start.6 = (bf16[1,2,256,512]{3,2,1,0:T(8,128)(2,1)S(1)}, bf16[1,2,256,512]{3,2,1,0:T(8,128)(2,1)S(1)}, u32[]{:S(2)}, u32[]{:S(2)}) collective-permute-start(bf16[1,2,256,512]{3,2,1,0:T(8,128)(2,1)S(1)} %collective-permute-done.3.refs_2_), channel_id=1, source_target_pairs={{0,8},{1,9},{2,10},{3,11},{4,12},{5,13},{6,14},{7,15},{8,16},{9,17... | collective-permute-start | bytes 1572872 | tf_op jit(solution)/shard_map/ppermute | solution.py:26
  56.8 27.7 %collective-permute-start.8 = (bf16[3,2,256,512]{3,2,1,0:T(8,128)(2,1)}, bf16[3,2,256,512]{3,2,1,0:T(8,128)(2,1)}, u32[]{:S(2)}, u32[]{:S(2)}) collective-permute-start(bf16[3,2,256,512]{3,2,1,0:T(8,128)(2,1)} %collective-permute-done.4.refs_3_), channel_id=1, source_target_pairs={{0,8},{1,9},{2,10},{3,11},{4,12},{5,13},{6,14},{7,15},{8,16},{9,17... | collective-permute-start | bytes 4718600 | tf_op jit(solution)/shard_map/ppermute | solution.py:26
  67.9 8.9 %collective-permute-start.9 = (bf16[1,2,256,512]{3,2,1,0:T(8,128)(2,1)S(1)}, bf16[1,2,256,512]{3,2,1,0:T(8,128)(2,1)S(1)}, u32[]{:S(2)}, u32[]{:S(2)}) collective-permute-start(bf16[1,2,256,512]{3,2,1,0:T(8,128)(2,1)S(1)} %collective-permute-done.7.refs_6_), channel_id=1, source_target_pairs={{0,24},{1,25},{2,26},{3,27},{4,28},{5,29},{6,30},{7,31},{8,0},{9,1... | collective-permute-start | bytes 1572872 | tf_op jit(solution)/shard_map/ppermute | solution.py:26
  70.7 13.8 %collective-permute-start.15 = (bf16[2,4,128,512]{3,2,1,0:T(8,128)(2,1)}, bf16[2,4,128,512]{3,2,1,0:T(8,128)(2,1)}, u32[]{:S(2)}, u32[]{:S(2)}) collective-permute-start(bf16[2,4,128,512]{3,2,1,0:T(8,128)(2,1)} %collective-permute-done.14.refs_10_), channel_id=1, source_target_pairs={{0,32},{1,33},{2,34},{3,35},{4,36},{5,37},{6,38},{7,39},{8,40},{9,... | collective-permute-start | bytes 3145736 | tf_op jit(solution)/shard_map/ppermute | solution.py:26
  73.4 11.1 %collective-permute-start.17 = (bf16[2,4,128,512]{3,2,1,0:T(8,128)(2,1)}, bf16[2,4,128,512]{3,2,1,0:T(8,128)(2,1)}, u32[]{:S(2)}, u32[]{:S(2)}) collective-permute-start(bf16[2,4,128,512]{3,2,1,0:T(8,128)(2,1)} %collective-permute-done.16.refs_12_), channel_id=1, source_target_pairs={{0,32},{1,33},{2,34},{3,35},{4,36},{5,37},{6,38},{7,39},{8,40},{9,... | collective-permute-start | bytes 3145736 | tf_op jit(solution)/shard_map/ppermute | solution.py:26
  73.5 8.5 %copy-start.2 = (bf16[3,2,256,512]{3,2,1,0:T(8,128)(2,1)}, bf16[3,2,256,512]{3,2,1,0:T(8,128)(2,1)S(1)}, u32[]{:S(2)}) copy-start(bf16[3,2,256,512]{3,2,1,0:T(8,128)(2,1)S(1)} %collective-permute-done.5.refs_4_) | copy-start | bytes 4718596
  73.5 8.5 %collective-permute-start.20 = (bf16[1,4,128,512]{3,2,1,0:T(8,128)(2,1)S(1)}, bf16[1,4,128,512]{3,2,1,0:T(8,128)(2,1)S(1)}, u32[]{:S(2)}, u32[]{:S(2)}) collective-permute-start(bf16[1,4,128,512]{3,2,1,0:T(8,128)(2,1)S(1)} %slice.4), channel_id=1, source_target_pairs={{0,1},{1,2},{2,3},{3,4},{4,5},{5,6},{6,7},{7,0},{8,9},{9,10},{10,1... | collective-permute-start | bytes 1572872 | tf_op jit(solution)/shard_map/ppermute | solution.py:26
  76.8 9.2 %collective-permute-start.19 = (bf16[2,4,128,512]{3,2,1,0:T(8,128)(2,1)}, bf16[2,4,128,512]{3,2,1,0:T(8,128)(2,1)}, u32[]{:S(2)}, u32[]{:S(2)}) collective-permute-start(bf16[2,4,128,512]{3,2,1,0:T(8,128)(2,1)} %collective-permute-done.18.refs_14_), channel_id=1, source_target_pairs={{0,32},{1,33},{2,34},{3,35},{4,36},{5,37},{6,38},{7,39},{8,40},{9,... | collective-permute-start | bytes 3145736 | tf_op jit(solution)/shard_map/ppermute | solution.py:26
  82.1 3.9 %collective-permute-start.21 = (bf16[1,4,128,512]{3,2,1,0:T(8,128)(2,1)S(1)}, bf16[1,4,128,512]{3,2,1,0:T(8,128)(2,1)S(1)}, u32[]{:S(2)}, u32[]{:S(2)}) collective-permute-start(bf16[1,4,128,512]{3,2,1,0:T(8,128)(2,1)S(1)} %collective-permute-done.20.refs_16_), channel_id=1, source_target_pairs={{0,32},{1,33},{2,34},{3,35},{4,36},{5,37},{6,38},{7,39},{8,40},{9,... | collective-permute-start | bytes 1572872 | tf_op jit(solution)/shard_map/ppermute | solution.py:26

commit v3 on v0

v3 whole, which is shorter than its diff:
```python
import jax
import jax.numpy as jnp
from jax import lax
from jax.experimental import pallas as pl
from jax.experimental.pallas import tpu as pltpu
from jax.sharding import Mesh, PartitionSpec as P

LEN = 64
AXES = ("y", "c", "x", "z")
NY, NC, NX, NZ = SIZES = (4, 2, 4, 8)
VMEM = pl.BlockSpec(memory_space=pltpu.VMEM)
SMEM = pl.BlockSpec(memory_space=pltpu.SMEM)


def permute(block, move):
    pairs = []
    for y in range(NY):
        for c in range(NC):
            for x in range(NX):
                for z in range(NZ):
                    to = [a % n for a, n in zip(move(y, c, x, z), SIZES)]
                    pairs.append(
                        (
                            ((y * NC + c) * NX + x) * NZ + z,
                            ((to[0] * NC + to[1]) * NX + to[2]) * NZ + to[3],
                        )
                    )
    return lax.ppermute(block, AXES, pairs)


def swap(block):
    return permute(block, lambda y, c, x, z: (y, 1 - c, x, z))


def first(block, s):
    return permute(
        block, lambda y, c, x, z: (y + s, c, x, z) if c == 0 else (y, c, x + s, z)
    )


def second(block, s):
    return permute(
        block, lambda y, c, x, z: (y, c, x + s, z) if c == 0 else (y + s, c, x, z)
    )


def along_z(block):
    return permute(
        block, lambda y, c, x, z: (y, c, x, z + 1) if c == 0 else (y, c, x, z - 1)
    )


def prep_kernel(place, lengths, hid, head, kept, other, *blocks):
    c, x = place[1], place[2]
    half, width = kept.shape[0], blocks[0].shape[1]
    for out, part in ((kept, c), (other, 1 - c)):
        for p in range(half // LEN):
            n = lengths[part * (half // LEN) + p]
            at = pl.multiple_of(part * half + p * LEN, LEN)
            rows = hid[pl.ds(at, LEN), :]
            j = lax.broadcasted_iota(jnp.int32, rows.shape, 0)
            zero = jnp.zeros_like(rows)
            out[p * LEN : (p + 1) * LEN, :] = jnp.where(j < n, rows, zero)
    for s, out in enumerate(blocks):
        at = pl.multiple_of(lax.rem(x + s, NX) * width, width)
        out[...] = head[:, pl.ds(at, width)]


def prep(place, lengths, hidden, head):
    half = jax.ShapeDtypeStruct((hidden.shape[0] // NC, hidden.shape[1]), hidden.dtype)
    block = jax.ShapeDtypeStruct((head.shape[0], head.shape[1] // NX), head.dtype)
    return pl.pallas_call(
        prep_kernel,
        out_shape=[half, half] + [block] * NX,
        in_specs=[SMEM, SMEM, VMEM, VMEM],
        out_specs=[VMEM] * (2 + NX),
    )(place, lengths, hidden, head)


ORDER = (
    ("h0", ()),
    ("x1", ()),
    ("x3", ()),
    ("x2", ()),
    ("f-", ("h0",)),
    ("f+", ()),
    ("sU-", ("x1",)),
    ("A1", ("x2", "x3")),
    ("sU+", ()),
    ("b0", ("f-",)),
    ("ff", ("f+",)),
    ("B1", ("b0",)),
    ("sP-", ("sU-",)),
    ("A2", ("A1",)),
    ("sP+", ("sU+",)),
    ("B2", ("B1",)),
    ("cB1", ("ff",)),
    ("sF-", ("cB1",)),
    ("A3", ("A2",)),
    ("cA2", ("sP-",)),
    ("sF+", ("cA2",)),
    ("B3", ("B2",)),
    ("gU", ("sP+",)),
    ("gP", ("sF-",)),
    ("A4", ("A3",)),
    ("gF", ("sF+",)),
    ("cB3", ("B3",)),
    ("cB2", ("gU",)),
    ("cA3", ("cB3",)),
    ("cA1", ("cB2",)),
    ("cA4", ("A4",)),
)


def exchange(kept, other, blocks):
    got = {"kept": kept, "other": other}

    def own():
        if "own" not in got:
            got["own"] = jnp.stack([kept, got["h0"]])[None]
        return got["own"]

    def pair():
        if "pair" not in got:
            got["pair"] = jnp.concatenate([got["f+"], got["f-"]], axis=0)
        return got["pair"]

    def piece():
        if "A0" not in got:
            got["A0"] = jnp.stack([blocks[0], got["x1"], got["x2"], got["x3"]])
        return got["A0"]

    def across(s):
        return lambda b: permute(b, lambda y, c, x, z: (y, c, x + s, z))

    moves = {
        "h0": (swap, lambda: other),
        "x1": (across(1), lambda: blocks[1]),
        "x2": (across(2), lambda: blocks[2]),
        "x3": (across(3), lambda: blocks[3]),
        "f+": (lambda b: first(b, 1), own),
        "f-": (lambda b: first(b, -1), own),
        "ff": (lambda b: first(b, 1), lambda: got["f+"]),
        "sU+": (lambda b: second(b, 1), own),
        "sU-": (lambda b: second(b, -1), own),
        "sP+": (lambda b: second(b, 1), pair),
        "sP-": (lambda b: second(b, -1), pair),
        "sF+": (lambda b: second(b, 1), lambda: got["ff"]),
        "sF-": (lambda b: second(b, -1), lambda: got["ff"]),
        "gU": (lambda b: second(b, -1), lambda: got["sU-"]),
        "gP": (lambda b: second(b, 1), lambda: got["sP+"]),
        "gF": (lambda b: second(b, -1), lambda: got["sF-"]),
        "b0": (swap, piece),
        "A1": (along_z, piece),
        "B1": (along_z, lambda: got["b0"]),
        "A2": (along_z, lambda: got["A1"]),
        "B2": (along_z, lambda: got["B1"]),
        "A3": (along_z, lambda: got["A2"]),
        "B3": (along_z, lambda: got["B2"]),
        "A4": (along_z, lambda: got["A3"]),
    }
    for n in ("A1", "B1", "A2", "B2", "A3", "B3", "A4"):
        moves["c" + n] = (swap, lambda n=n: got[n])
    for name, arrived in ORDER:
        move, operand = moves[name]
        block = operand()
        if arrived:
            block = lax.optimization_barrier((block, *(got[a] for a in arrived)))[0]
        got[name] = move(block)
    return got


def hidden_blocks(got):
    return [
        (got["own"], 0, 0),
        (got["sU+"], 0, -1),
        (got["sU-"], 0, 1),
        (got["pair"], None, 0),
        (got["ff"], 2, 0),
        (got["gU"], 0, 2),
        (got["sP+"], None, -1),
        (got["sP-"], None, 1),
        (got["sF+"], 2, -1),
        (got["sF-"], 2, 1),
        (got["gF"], 2, 2),
        (got["gP"], None, 2),
    ]


def head_pieces(got):
    mine, theirs, steps = [got["A0"]], [got["b0"]], [0]
    for s in ("1", "2", "3"):
        mine += [got["A" + s], got["cB" + s]]
        theirs += [got["B" + s], got["cA" + s]]
        steps += [-int(s), int(s)]
    return mine + [got["A4"]], theirs + [got["cA4"]], steps + [NZ // 2]


def pool_kernel(units, steps, place, *refs):
    n, m = len(units), len(steps)
    hid, head = refs[:n], (refs[n : n + m], refs[n + m : n + 2 * m])
    o_ref, acc = refs[n + 2 * m :]
    y, c, x, z = (place[i] for i in range(4))
    rows = head[0][0].shape[1]
    per = hid[0].shape[-1] // rows
    from_z = [lax.rem(z + (1 - 2 * c) * s + NZ, NZ) for s in steps]
    halves = [jnp.where(lax.div(f, per) == c, 0, 1) for f in from_z]
    lanes = [pl.multiple_of(lax.rem(f, per) * rows, rows) for f in from_z]
    acc[...] = jnp.zeros_like(acc)
    for ref, (a, b) in zip(hid, units):

        def unit(u, _):
            along = 2 * u - 1 if a is None else a
            at_y = lax.rem(y + jnp.where(c == 0, along, b) + NY, NY)
            at_x = lax.rem(x + jnp.where(c == 0, b, along) + NX, NX)
            i = lax.rem(x - at_y + NX, NX)
            left = jnp.concatenate(
                [ref[u, h, :, pl.ds(at, rows)] for h, at in zip(halves, lanes)], axis=1
            )
            for col in range(NC):
                right = jnp.concatenate([p[i] for p in head[col]], axis=0)
                acc[col, at_x] += jnp.dot(
                    left, right, preferred_element_type=jnp.float32
                )
            return 0

        lax.fori_loop(0, ref.shape[0], unit, 0)
    for col in range(NC):
        for i in range(NX):
            tokens, cols = acc.shape[2:]
            top = jnp.max(acc[col, i].reshape(tokens // LEN, LEN, cols), axis=1)
            o_ref[lax.rem(c + col, NC), i] = jnp.log1p(jnp.maximum(top, 0.0))


def pool(place, hid, head):
    mine, theirs, steps = head
    tokens = hid[0][0].shape[-2]
    cols = mine[0].shape[-1]
    arrays = [h[0] for h in hid] + mine + theirs

    def kernel(*refs):
        pool_kernel([h[1:] for h in hid], steps, *refs)

    return pl.pallas_call(
        kernel,
        out_shape=jax.ShapeDtypeStruct((NC, NX, tokens // LEN, cols), jnp.float32),
        in_specs=[SMEM] + [VMEM] * len(arrays),
        out_specs=VMEM,
        scratch_shapes=[pltpu.VMEM((NC, NX, tokens, cols), jnp.float32)],
        compiler_params=pltpu.CompilerParams(vmem_limit_bytes=14 << 20),
    )(place, *arrays)


def body(hidden, head_weight, lengths):
    place = jnp.stack([lax.axis_index(a) for a in AXES]).astype(jnp.int32)
    kept, other, *blocks = prep(place, lengths, hidden, head_weight)
    got = exchange(kept, other, blocks)
    pooled = pool(place, hidden_blocks(got), head_pieces(got)).astype(jnp.bfloat16)
    each = pooled.shape[-1] // NZ
    pooled = pooled.reshape(NC, NX * pooled.shape[2], NZ, each)
    pooled = jnp.transpose(pooled, (2, 0, 1, 3)).reshape(NZ * NC, -1, each)
    got = lax.all_to_all(pooled, ("z", "c"), split_axis=0, concat_axis=0, tiled=True)
    got = got.reshape(NZ, NC, NX, -1, each)
    got = jnp.transpose(got, (2, 0, 1, 3, 4)).reshape(-1, each).astype(jnp.float32)
    peak = jnp.max(got, axis=0)
    return jnp.transpose((got / (1.0 + peak)[None, :]).astype(jnp.bfloat16))


def solution(mesh):
    fine = Mesh(mesh.devices.reshape(SIZES), AXES)
    return jax.shard_map(
        body,
        mesh=fine,
        in_specs=(P(("x", "z"), ("y", "c")), P(("x", "z"), ("y", "c")), P(("x", "z"))),
        out_specs=P(("y", "c", "x", "z"), None),
        check_vma=False,
    )
```

time: 298 us -> 114 us (0.38)
  the two profiles are of different devices: /device:TPU:8 before, /device:TPU:1 now
where the time goes in v3:
time: 114 us
  starting transfers between devices  42.6 us (37%)
  waiting for transfers between devices  40 us (35%)
  Pallas kernels  14.4 us (13%)
  blocking collectives  13.7 us (12%)
  other arithmetic  1.77 us (2%)
  local copies, waits for them, and re-layouts  1.16 us (1%)
    ppermute x31, starting transfers between devices, permute(): return lax.ppermute(block, AXES, pairs)  42.6 us
    ppermute x31, waiting for transfers between devices, permute(): return lax.ppermute(block, AXES, pairs)  40 us
    all_to_all x1, blocking collectives, body(): lax.all_to_all(pooled, ('z', 'c'), split_axis=0, concat_axis=0, tiled=True)  13.7 us
    pallas_call x1, Pallas kernels, pool(): pl.pallas_call(kernel, out_shape=jax.ShapeDtypeStruct((NC, NX, tokens //...  12.1 us
  transfers between devices with their start and end apart: 31, of which 16 were waited for; matrix products, arithmetic and copies ran while one was open for 0% of the time, Pallas kernels for 0%

profile of v3, /device:TPU:1, one launch (start us, length us, event | category | flops | bytes accessed | tf_op | source)
XLA Modules:
  0.0 113.7 jit_solution(17583003686274091160)
XLA Ops:
  0.6 2.3 %shard_map.37 = (bf16[256,512]{1,0:T(8,128)(2,1)}, bf16[256,512]{1,0:T(8,128)(2,1)}, bf16[128,512]{1,0:T(8,128)(2,1)}, bf16[128,512]{1,0:T(8,128)(2,1)}, bf16[12...) custom-call(s32[4]{0:T(128)} %pad_add_fusion.place.refs_0_, s32[8]{0:T(128)} %lengths.1, bf16[512,512]{1,0:T(8,128)(2,1)} %hid.1, ...), custom_call_target="tpu_custom_call" | custom-call | tf_op jit(solution)/shard_map/pallas_call | solution.py:72
  2.8 3.2 %collective-permute-start = (bf16[256,512]{1,0:T(8,128)(2,1)}, bf16[256,512]{1,0:T(8,128)(2,1)S(1)}, u32[]{:S(2)}, u32[]{:S(2)}) collective-permute-start(bf16[256,512]{1,0:T(8,128)(2,1)} %get-tuple-element.37), channel_id=1, source_target_pairs={{0,32},{1,33},{2,34},{3,35},{4,36},{5,37},{6,38},{7,39},{8,40},{9,... | collective-permute-start | bytes 786440 | tf_op jit(solution)/shard_map/ppermute | solution.py:28
  6.1 1.4 %collective-permute-done = bf16[256,512]{1,0:T(8,128)(2,1)S(1)} collective-permute-done((bf16[256,512]{1,0:T(8,128)(2,1)}, bf16[256,512]{1,0:T(8,128)(2,1)S(1)}, u32[]{:S(2)}, u32[]{:S(2)}) %collective-permute-start) | collective-permute-done | bytes 262176 | tf_op jit(solution)/shard_map/ppermute | solution.py:28
  7.5 1.1 maximum_bitcast_fusion.refs_1_
  8.5 0.8 collective-permute-start.5
  10.1 1.0 collective-permute-start.10
  11.1 1.5 %collective-permute-start.11 = (bf16[128,512]{1,0:T(8,128)(2,1)S(1)}, bf16[128,512]{1,0:T(8,128)(2,1)S(1)}, u32[]{:S(2)}, u32[]{:S(2)}) collective-permute-start(bf16[128,512]{1,0:T(8,128)(2,1)S(1)} %copy-done.2), channel_id=1, source_target_pairs={{0,24},{1,25},{2,26},{3,27},{4,28},{5,29},{6,30},{7,31},{8,0},{9,1... | collective-permute-start | bytes 393224 | tf_op jit(solution)/shard_map/ppermute | solution.py:28
  12.6 3.7 %collective-permute-done.2 = bf16[128,512]{1,0:T(8,128)(2,1)S(1)} collective-permute-done((bf16[128,512]{1,0:T(8,128)(2,1)S(1)}, bf16[128,512]{1,0:T(8,128)(2,1)S(1)}, u32[]{:S(2)}, u32[]{:S(2)}) %collective-permute-start.2) | collective-permute-done | bytes 131104 | tf_op jit(solution)/shard_map/ppermute | solution.py:28
  16.3 3.2 %collective-permute-start.1 = (bf16[1,2,256,512]{3,2,1,0:T(8,128)(2,1)S(1)}, bf16[1,2,256,512]{3,2,1,0:T(8,128)(2,1)S(1)}, u32[]{:S(2)}, u32[]{:S(2)}) collective-permute-start(bf16[1,2,256,512]{3,2,1,0:T(8,128)(2,1)S(1)} %maximum_bitcast_fusion.refs_1_), channel_id=1, source_target_pairs={{0,8},{1,9},{2,10},{3,11},{4,12},{5,13},{6,14},{7,15},{8,16},{9,17... | collective-permute-start | bytes 1572872 | tf_op jit(solution)/shard_map/ppermute | solution.py:28
  19.6 2.9 %collective-permute-done.11 = bf16[128,512]{1,0:T(8,128)(2,1)S(1)} collective-permute-done((bf16[128,512]{1,0:T(8,128)(2,1)S(1)}, bf16[128,512]{1,0:T(8,128)(2,1)S(1)}, u32[]{:S(2)}, u32[]{:S(2)}) %collective-permute-start.11) | collective-permute-done | bytes 131104 | tf_op jit(solution)/shard_map/ppermute | solution.py:28
  22.7 4.7 %collective-permute-start.12 = (bf16[4,128,512]{2,1,0:T(8,128)(2,1)S(1)}, bf16[4,128,512]{2,1,0:T(8,128)(2,1)S(1)}, u32[]{:S(2)}, u32[]{:S(2)}) collective-permute-start(bf16[4,128,512]{2,1,0:T(8,128)(2,1)S(1)} %pad_maximum_fusion.refs_13_), channel_id=1, source_target_pairs={{0,1},{1,2},{2,3},{3,4},{4,5},{5,6},{6,7},{7,0},{8,9},{9,10},{10,1... | collective-permute-start | bytes 1572872 | tf_op jit(solution)/shard_map/ppermute | solution.py:28
  27.8 3.6 %collective-permute-done.1.refs_2_ = bf16[1,2,256,512]{3,2,1,0:T(8,128)(2,1)S(1)} collective-permute-done((bf16[1,2,256,512]{3,2,1,0:T(8,128)(2,1)S(1)}, bf16[1,2,256,512]{3,2,1,0:T(8,128)(2,1)S(1)}, u32[]{:S(2)}, u32[]{:S(2)}) %collective-permute-start.1) | collective-permute-done | bytes 524320 | tf_op jit(solution)/shard_map/ppermute | solution.py:28
  31.4 2.7 %collective-permute-start.9 = (bf16[2,2,256,512]{3,2,1,0:T(8,128)(2,1)S(1)}, bf16[2,2,256,512]{3,2,1,0:T(8,128)(2,1)S(1)}, u32[]{:S(2)}, u32[]{:S(2)}) collective-permute-start(bf16[2,2,256,512]{3,2,1,0:T(8,128)(2,1)S(1)} %constant_dynamic-update-slice_fusion.refs_4_), channel_id=1, source_target_pairs={{0,24},{1,25},{2,26},{3,27},{4,28},{5,29},{6,30},{7,31},{8,0},{9,1... | collective-permute-start | bytes 3145736 | tf_op jit(solution)/shard_map/ppermute | solution.py:28
  34.1 5.4 %collective-permute-start.17 = (bf16[4,128,512]{2,1,0:T(8,128)(2,1)S(1)}, bf16[4,128,512]{2,1,0:T(8,128)(2,1)S(1)}, u32[]{:S(2)}, u32[]{:S(2)}) collective-permute-start(bf16[4,128,512]{2,1,0:T(8,128)(2,1)S(1)} %collective-permute-done.16.refs_21_), channel_id=1, source_target_pairs={{0,1},{1,2},{2,3},{3,4},{4,5},{5,6},{6,7},{7,0},{8,9},{9,10},{10,1... | collective-permute-start | bytes 1572872 | tf_op jit(solution)/shard_map/ppermute | solution.py:28
  39.5 0.7 collective-permute-start.13
  40.2 5.4 %collective-permute-done.17.refs_22_ = bf16[4,128,512]{2,1,0:T(8,128)(2,1)S(1)} collective-permute-done((bf16[4,128,512]{2,1,0:T(8,128)(2,1)S(1)}, bf16[4,128,512]{2,1,0:T(8,128)(2,1)S(1)}, u32[]{:S(2)}, u32[]{:S(2)}) %collective-permute-start.17) | collective-permute-done | bytes 524320 | tf_op jit(solution)/shard_map/ppermute | solution.py:28
  45.6 3.4 %collective-permute-start.22 = (bf16[4,128,512]{2,1,0:T(8,128)(2,1)S(1)}, bf16[4,128,512]{2,1,0:T(8,128)(2,1)S(1)}, u32[]{:S(2)}, u32[]{:S(2)}) collective-permute-start(bf16[4,128,512]{2,1,0:T(8,128)(2,1)S(1)} %collective-permute-done.17.refs_22_), channel_id=1, source_target_pairs={{0,1},{1,2},{2,3},{3,4},{4,5},{5,6},{6,7},{7,0},{8,9},{9,10},{10,1... | collective-permute-start | bytes 1572872 | tf_op jit(solution)/shard_map/ppermute | solution.py:28
  49.0 4.2 %collective-permute-done.6.refs_5_ = bf16[1,2,256,512]{3,2,1,0:T(8,128)(2,1)S(1)} collective-permute-done((bf16[1,2,256,512]{3,2,1,0:T(8,128)(2,1)S(1)}, bf16[1,2,256,512]{3,2,1,0:T(8,128)(2,1)S(1)}, u32[]{:S(2)}, u32[]{:S(2)}) %collective-permute-start.6) | collective-permute-done | bytes 524320 | tf_op jit(solution)/shard_map/ppermute | solution.py:28
  53.3 3.3 %collective-permute-start.24 = (bf16[4,128,512]{2,1,0:T(8,128)(2,1)S(1)}, bf16[4,128,512]{2,1,0:T(8,128)(2,1)S(1)}, u32[]{:S(2)}, u32[]{:S(2)}) collective-permute-start(bf16[4,128,512]{2,1,0:T(8,128)(2,1)S(1)} %collective-permute-done.13.refs_16_), channel_id=1, source_target_pairs={{0,1},{1,2},{2,3},{3,4},{4,5},{5,6},{6,7},{7,0},{8,9},{9,10},{10,1... | collective-permute-start | bytes 1572872 | tf_op jit(solution)/shard_map/ppermute | solution.py:28
  56.9 3.1 %collective-permute-start.25 = (bf16[4,128,512]{2,1,0:T(8,128)(2,1)S(1)}, bf16[4,128,512]{2,1,0:T(8,128)(2,1)S(1)}, u32[]{:S(2)}, u32[]{:S(2)}) collective-permute-start(bf16[4,128,512]{2,1,0:T(8,128)(2,1)S(1)} %collective-permute-done.22.refs_24_), channel_id=1, source_target_pairs={{0,1},{1,2},{2,3},{3,4},{4,5},{5,6},{6,7},{7,0},{8,9},{9,10},{10,1... | collective-permute-start | bytes 1572872 | tf_op jit(solution)/shard_map/ppermute | solution.py:28
  60.0 2.7 %collective-permute-done.24.refs_18_ = bf16[4,128,512]{2,1,0:T(8,128)(2,1)S(1)} collective-permute-done((bf16[4,128,512]{2,1,0:T(8,128)(2,1)S(1)}, bf16[4,128,512]{2,1,0:T(8,128)(2,1)S(1)}, u32[]{:S(2)}, u32[]{:S(2)}) %collective-permute-start.24) | collective-permute-done | bytes 524320 | tf_op jit(solution)/shard_map/ppermute | solution.py:28
  62.7 3.1 %collective-permute-start.27 = (bf16[4,128,512]{2,1,0:T(8,128)(2,1)S(1)}, bf16[4,128,512]{2,1,0:T(8,128)(2,1)S(1)}, u32[]{:S(2)}, u32[]{:S(2)}) collective-permute-start(bf16[4,128,512]{2,1,0:T(8,128)(2,1)S(1)} %collective-permute-done.24.refs_18_), channel_id=1, source_target_pairs={{0,1},{1,2},{2,3},{3,4},{4,5},{5,6},{6,7},{7,0},{8,9},{9,10},{10,1... | collective-permute-start | bytes 1572872 | tf_op jit(solution)/shard_map/ppermute | solution.py:28
  65.9 2.4 %collective-permute-done.25.refs_26_ = bf16[4,128,512]{2,1,0:T(8,128)(2,1)S(1)} collective-permute-done((bf16[4,128,512]{2,1,0:T(8,128)(2,1)S(1)}, bf16[4,128,512]{2,1,0:T(8,128)(2,1)S(1)}, u32[]{:S(2)}, u32[]{:S(2)}) %collective-permute-start.25) | collective-permute-done | bytes 524320 | tf_op jit(solution)/shard_map/ppermute | solution.py:28
  68.3 2.1 %collective-permute-start.26 = (bf16[4,128,512]{2,1,0:T(8,128)(2,1)S(1)}, bf16[4,128,512]{2,1,0:T(8,128)(2,1)S(1)}, u32[]{:S(2)}, u32[]{:S(2)}) collective-permute-start(bf16[4,128,512]{2,1,0:T(8,128)(2,1)S(1)} %collective-permute-done.25.refs_26_), channel_id=1, source_target_pairs={{0,32},{1,33},{2,34},{3,35},{4,36},{5,37},{6,38},{7,39},{8,40},{9,... | collective-permute-start | bytes 1572872 | tf_op jit(solution)/shard_map/ppermute | solution.py:28
  70.5 3.4 %collective-permute-done.27.refs_20_ = bf16[4,128,512]{2,1,0:T(8,128)(2,1)S(1)} collective-permute-done((bf16[4,128,512]{2,1,0:T(8,128)(2,1)S(1)}, bf16[4,128,512]{2,1,0:T(8,128)(2,1)S(1)}, u32[]{:S(2)}, u32[]{:S(2)}) %collective-permute-start.27) | collective-permute-done | bytes 524320 | tf_op jit(solution)/shard_map/ppermute | solution.py:28
  74.0 2.1 %collective-permute-start.30 = (bf16[4,128,512]{2,1,0:T(8,128)(2,1)S(1)}, bf16[4,128,512]{2,1,0:T(8,128)(2,1)S(1)}, u32[]{:S(2)}, u32[]{:S(2)}) collective-permute-start(bf16[4,128,512]{2,1,0:T(8,128)(2,1)S(1)} %collective-permute-done.27.refs_20_), channel_id=1, source_target_pairs={{0,32},{1,33},{2,34},{3,35},{4,36},{5,37},{6,38},{7,39},{8,40},{9,... | collective-permute-start | bytes 1572872 | tf_op jit(solution)/shard_map/ppermute | solution.py:28
  76.1 0.7 collective-permute-start.20
  77.6 0.7 collective-permute-done.28.refs_23_
  78.3 6.1 %collective-permute-done.20.refs_11_ = bf16[1,2,256,512]{3,2,1,0:T(8,128)(2,1)S(1)} collective-permute-done((bf16[1,2,256,512]{3,2,1,0:T(8,128)(2,1)S(1)}, bf16[1,2,256,512]{3,2,1,0:T(8,128)(2,1)S(1)}, u32[]{:S(2)}, u32[]{:S(2)}) %collective-permute-start.20) | collective-permute-done | bytes 524320 | tf_op jit(solution)/shard_map/ppermute | solution.py:28
  84.5 2.2 %collective-permute-done.21.refs_12_ = bf16[2,2,256,512]{3,2,1,0:T(8,128)(2,1)S(1)} collective-permute-done((bf16[2,2,256,512]{3,2,1,0:T(8,128)(2,1)S(1)}, bf16[2,2,256,512]{3,2,1,0:T(8,128)(2,1)S(1)}, u32[]{:S(2)}, u32[]{:S(2)}) %collective-permute-start.21) | collective-permute-done | bytes 1048608 | tf_op jit(solution)/shard_map/ppermute | solution.py:28
  86.7 12.1 %shard_map.38 = f32[2,4,4,512]{3,2,1,0:T(4,128)S(1)} custom-call(s32[4]{0:T(128)S(1)} %copy-done, bf16[1,2,256,512]{3,2,1,0:T(8,128)(2,1)S(1)} %maximum_bitcast_fusion.refs_1_, bf16[1,2,256,512]{3,2,1,0:T(8,128)(2,1)S(1)} %collective-permute-done.1.refs_2_, bf16[1,2,256,512]{3,2,1,0:T(8,128)(2,1)S(1)} %collective-permute-done.3.refs_3_, ...), custom_call_target="tpu_custom_call" | custom-call | tf_op jit(solution)/shard_map/pallas_call | solution.py:244
  99.1 13.7 %all_to_all.5 = bf16[16,2,512]{2,1,0:T(2,128)(2,1)S(1)} all-to-all(bf16[16,2,512]{2,1,0:T(2,128)(2,1)S(1)} %reshape.20), channel_id=1, replica_groups=mesh['y'=4,'c'=2,'x'=4,'z'=8] {'z','c'}, dimensions={0} | all-to-all | bytes 65536 | tf_op jit(solution)/shard_map/all_to_all | solution.py:262
  (58 shorter events, 4.4 us)
Async XLA Ops:
  2.8 4.6 %collective-permute-start = (bf16[256,512]{1,0:T(8,128)(2,1)}, bf16[256,512]{1,0:T(8,128)(2,1)S(1)}, u32[]{:S(2)}, u32[]{:S(2)}) collective-permute-start(bf16[256,512]{1,0:T(8,128)(2,1)} %get-tuple-element.37), channel_id=1, source_target_pairs={{0,32},{1,33},{2,34},{3,35},{4,36},{5,37},{6,38},{7,39},{8,40},{9,... | collective-permute-start | bytes 786440 | tf_op jit(solution)/shard_map/ppermute | solution.py:28
  8.5 14.1 %collective-permute-start.5 = (bf16[1,2,256,512]{3,2,1,0:T(8,128)(2,1)S(1)}, bf16[1,2,256,512]{3,2,1,0:T(8,128)(2,1)S(1)}, u32[]{:S(2)}, u32[]{:S(2)}) collective-permute-start(bf16[1,2,256,512]{3,2,1,0:T(8,128)(2,1)S(1)} %maximum_bitcast_fusion.refs_1_), channel_id=1, source_target_pairs={{0,192},{1,193},{2,194},{3,195},{4,196},{5,197},{6,198},{7,199},{8... | collective-permute-start | bytes 1572872 | tf_op jit(solution)/shard_map/ppermute | solution.py:28
  9.3 7.0 %collective-permute-start.2 = (bf16[128,512]{1,0:T(8,128)(2,1)S(1)}, bf16[128,512]{1,0:T(8,128)(2,1)S(1)}, u32[]{:S(2)}, u32[]{:S(2)}) collective-permute-start(bf16[128,512]{1,0:T(8,128)(2,1)S(1)} %copy-done.4), channel_id=1, source_target_pairs={{0,8},{1,9},{2,10},{3,11},{4,12},{5,13},{6,14},{7,15},{8,16},{9,17... | collective-permute-start | bytes 393224 | tf_op jit(solution)/shard_map/ppermute | solution.py:28
  10.1 9.4 %collective-permute-start.10 = (bf16[128,512]{1,0:T(8,128)(2,1)S(1)}, bf16[128,512]{1,0:T(8,128)(2,1)S(1)}, u32[]{:S(2)}, u32[]{:S(2)}) collective-permute-start(bf16[128,512]{1,0:T(8,128)(2,1)S(1)} %copy-done.3), channel_id=1, source_target_pairs={{0,16},{1,17},{2,18},{3,19},{4,20},{5,21},{6,22},{7,23},{8,24},{9,... | collective-permute-start | bytes 393224 | tf_op jit(solution)/shard_map/ppermute | solution.py:28
  11.1 11.5 %collective-permute-start.11 = (bf16[128,512]{1,0:T(8,128)(2,1)S(1)}, bf16[128,512]{1,0:T(8,128)(2,1)S(1)}, u32[]{:S(2)}, u32[]{:S(2)}) collective-permute-start(bf16[128,512]{1,0:T(8,128)(2,1)S(1)} %copy-done.2), channel_id=1, source_target_pairs={{0,24},{1,25},{2,26},{3,27},{4,28},{5,29},{6,30},{7,31},{8,0},{9,1... | collective-permute-start | bytes 393224 | tf_op jit(solution)/shard_map/ppermute | solution.py:28
  12.6 14.9 %collective-permute-start.4 = (bf16[1,2,256,512]{3,2,1,0:T(8,128)(2,1)S(1)}, bf16[1,2,256,512]{3,2,1,0:T(8,128)(2,1)S(1)}, u32[]{:S(2)}, u32[]{:S(2)}) collective-permute-start(bf16[1,2,256,512]{3,2,1,0:T(8,128)(2,1)S(1)} %maximum_bitcast_fusion.refs_1_), channel_id=1, source_target_pairs={{0,64},{1,65},{2,66},{3,67},{4,68},{5,69},{6,70},{7,71},{8,72},{9,... | collective-permute-start | bytes 1572872 | tf_op jit(solution)/shard_map/ppermute | solution.py:28
  16.3 15.1 %collective-permute-start.1 = (bf16[1,2,256,512]{3,2,1,0:T(8,128)(2,1)S(1)}, bf16[1,2,256,512]{3,2,1,0:T(8,128)(2,1)S(1)}, u32[]{:S(2)}, u32[]{:S(2)}) collective-permute-start(bf16[1,2,256,512]{3,2,1,0:T(8,128)(2,1)S(1)} %maximum_bitcast_fusion.refs_1_), channel_id=1, source_target_pairs={{0,8},{1,9},{2,10},{3,11},{4,12},{5,13},{6,14},{7,15},{8,16},{9,17... | collective-permute-start | bytes 1572872 | tf_op jit(solution)/shard_map/ppermute | solution.py:28
  19.5 8.3 %collective-permute-start.3 = (bf16[1,2,256,512]{3,2,1,0:T(8,128)(2,1)S(1)}, bf16[1,2,256,512]{3,2,1,0:T(8,128)(2,1)S(1)}, u32[]{:S(2)}, u32[]{:S(2)}) collective-permute-start(bf16[1,2,256,512]{3,2,1,0:T(8,128)(2,1)S(1)} %maximum_bitcast_fusion.refs_1_), channel_id=1, source_target_pairs={{0,24},{1,25},{2,26},{3,27},{4,28},{5,29},{6,30},{7,31},{8,0},{9,1... | collective-permute-start | bytes 1572872 | tf_op jit(solution)/shard_map/ppermute | solution.py:28
  22.6 11.4 %collective-permute-start.16 = (bf16[4,128,512]{2,1,0:T(8,128)(2,1)S(1)}, bf16[4,128,512]{2,1,0:T(8,128)(2,1)S(1)}, u32[]{:S(2)}, u32[]{:S(2)}) collective-permute-start(bf16[4,128,512]{2,1,0:T(8,128)(2,1)S(1)} %pad_maximum_fusion.refs_13_), channel_id=1, source_target_pairs={{0,32},{1,33},{2,34},{3,35},{4,36},{5,37},{6,38},{7,39},{8,40},{9,... | collective-permute-start | bytes 1572872 | tf_op jit(solution)/shard_map/ppermute | solution.py:28
  22.7 16.8 %collective-permute-start.12 = (bf16[4,128,512]{2,1,0:T(8,128)(2,1)S(1)}, bf16[4,128,512]{2,1,0:T(8,128)(2,1)S(1)}, u32[]{:S(2)}, u32[]{:S(2)}) collective-permute-start(bf16[4,128,512]{2,1,0:T(8,128)(2,1)S(1)} %pad_maximum_fusion.refs_13_), channel_id=1, source_target_pairs={{0,1},{1,2},{2,3},{3,4},{4,5},{5,6},{6,7},{7,0},{8,9},{9,10},{10,1... | collective-permute-start | bytes 1572872 | tf_op jit(solution)/shard_map/ppermute | solution.py:28
  27.5 59.2 %copy-start = (s32[4]{0:T(128)S(1)}, s32[4]{0:T(128)}, u32[]{:S(2)}) copy-start(s32[4]{0:T(128)} %pad_add_fusion.place.refs_0_) | copy-start | bytes 52
  31.4 25.2 %collective-permute-start.7 = (bf16[2,2,256,512]{3,2,1,0:T(8,128)(2,1)S(1)}, bf16[2,2,256,512]{3,2,1,0:T(8,128)(2,1)S(1)}, u32[]{:S(2)}, u32[]{:S(2)}) collective-permute-start(bf16[2,2,256,512]{3,2,1,0:T(8,128)(2,1)S(1)} %constant_dynamic-update-slice_fusion.refs_4_), channel_id=1, source_target_pairs={{0,8},{1,9},{2,10},{3,11},{4,12},{5,13},{6,14},{7,15},{8,16},{9,17... | collective-permute-start | bytes 3145736 | tf_op jit(solution)/shard_map/ppermute | solution.py:28
  31.4 25.2 %collective-permute-start.9 = (bf16[2,2,256,512]{3,2,1,0:T(8,128)(2,1)S(1)}, bf16[2,2,256,512]{3,2,1,0:T(8,128)(2,1)S(1)}, u32[]{:S(2)}, u32[]{:S(2)}) collective-permute-start(bf16[2,2,256,512]{3,2,1,0:T(8,128)(2,1)S(1)} %constant_dynamic-update-slice_fusion.refs_4_), channel_id=1, source_target_pairs={{0,24},{1,25},{2,26},{3,27},{4,28},{5,29},{6,30},{7,31},{8,0},{9,1... | collective-permute-start | bytes 3145736 | tf_op jit(solution)/shard_map/ppermute | solution.py:28
  34.1 11.6 %collective-permute-start.17 = (bf16[4,128,512]{2,1,0:T(8,128)(2,1)S(1)}, bf16[4,128,512]{2,1,0:T(8,128)(2,1)S(1)}, u32[]{:S(2)}, u32[]{:S(2)}) collective-permute-start(bf16[4,128,512]{2,1,0:T(8,128)(2,1)S(1)} %collective-permute-done.16.refs_21_), channel_id=1, source_target_pairs={{0,1},{1,2},{2,3},{3,4},{4,5},{5,6},{6,7},{7,0},{8,9},{9,10},{10,1... | collective-permute-start | bytes 1572872 | tf_op jit(solution)/shard_map/ppermute | solution.py:28
  39.5 13.8 %collective-permute-start.6 = (bf16[1,2,256,512]{3,2,1,0:T(8,128)(2,1)S(1)}, bf16[1,2,256,512]{3,2,1,0:T(8,128)(2,1)S(1)}, u32[]{:S(2)}, u32[]{:S(2)}) collective-permute-start(bf16[1,2,256,512]{3,2,1,0:T(8,128)(2,1)S(1)} %collective-permute-done.4), channel_id=1, source_target_pairs={{0,64},{1,65},{2,66},{3,67},{4,68},{5,69},{6,70},{7,71},{8,72},{9,... | collective-permute-start | bytes 1572872 | tf_op jit(solution)/shard_map/ppermute | solution.py:28
  39.5 13.8 %collective-permute-start.13 = (bf16[4,128,512]{2,1,0:T(8,128)(2,1)S(1)}, bf16[4,128,512]{2,1,0:T(8,128)(2,1)S(1)}, u32[]{:S(2)}, u32[]{:S(2)}) collective-permute-start(bf16[4,128,512]{2,1,0:T(8,128)(2,1)S(1)} %collective-permute-done.12.refs_14_), channel_id=1, source_target_pairs={{0,1},{1,2},{2,3},{3,4},{4,5},{5,6},{6,7},{7,0},{8,9},{9,10},{10,1... | collective-permute-start | bytes 1572872 | tf_op jit(solution)/shard_map/ppermute | solution.py:28
  45.6 11.2 %collective-permute-start.22 = (bf16[4,128,512]{2,1,0:T(8,128)(2,1)S(1)}, bf16[4,128,512]{2,1,0:T(8,128)(2,1)S(1)}, u32[]{:S(2)}, u32[]{:S(2)}) collective-permute-start(bf16[4,128,512]{2,1,0:T(8,128)(2,1)S(1)} %collective-permute-done.17.refs_22_), channel_id=1, source_target_pairs={{0,1},{1,2},{2,3},{3,4},{4,5},{5,6},{6,7},{7,0},{8,9},{9,10},{10,1... | collective-permute-start | bytes 1572872 | tf_op jit(solution)/shard_map/ppermute | solution.py:28
  53.3 6.7 %collective-permute-start.18 = (bf16[4,128,512]{2,1,0:T(8,128)(2,1)S(1)}, bf16[4,128,512]{2,1,0:T(8,128)(2,1)S(1)}, u32[]{:S(2)}, u32[]{:S(2)}) collective-permute-start(bf16[4,128,512]{2,1,0:T(8,128)(2,1)S(1)} %collective-permute-done.17.refs_22_), channel_id=1, source_target_pairs={{0,32},{1,33},{2,34},{3,35},{4,36},{5,37},{6,38},{7,39},{8,40},{9,... | collective-permute-start | bytes 1572872 | tf_op jit(solution)/shard_map/ppermute | solution.py:28
  53.3 9.4 %collective-permute-start.24 = (bf16[4,128,512]{2,1,0:T(8,128)(2,1)S(1)}, bf16[4,128,512]{2,1,0:T(8,128)(2,1)S(1)}, u32[]{:S(2)}, u32[]{:S(2)}) collective-permute-start(bf16[4,128,512]{2,1,0:T(8,128)(2,1)S(1)} %collective-permute-done.13.refs_16_), channel_id=1, source_target_pairs={{0,1},{1,2},{2,3},{3,4},{4,5},{5,6},{6,7},{7,0},{8,9},{9,10},{10,1... | collective-permute-start | bytes 1572872 | tf_op jit(solution)/shard_map/ppermute | solution.py:28
  56.6 9.2 %collective-permute-start.8 = (bf16[1,2,256,512]{3,2,1,0:T(8,128)(2,1)S(1)}, bf16[1,2,256,512]{3,2,1,0:T(8,128)(2,1)S(1)}, u32[]{:S(2)}, u32[]{:S(2)}) collective-permute-start(bf16[1,2,256,512]{3,2,1,0:T(8,128)(2,1)S(1)} %collective-permute-done.3.refs_3_), channel_id=1, source_target_pairs={{0,24},{1,25},{2,26},{3,27},{4,28},{5,29},{6,30},{7,31},{8,0},{9,1... | collective-permute-start | bytes 1572872 | tf_op jit(solution)/shard_map/ppermute | solution.py:28
  56.6 9.2 %collective-permute-start.14 = (bf16[4,128,512]{2,1,0:T(8,128)(2,1)S(1)}, bf16[4,128,512]{2,1,0:T(8,128)(2,1)S(1)}, u32[]{:S(2)}, u32[]{:S(2)}) collective-permute-start(bf16[4,128,512]{2,1,0:T(8,128)(2,1)S(1)} %collective-permute-done.13.refs_16_), channel_id=1, source_target_pairs={{0,32},{1,33},{2,34},{3,35},{4,36},{5,37},{6,38},{7,39},{8,40},{9,... | collective-permute-start | bytes 1572872 | tf_op jit(solution)/shard_map/ppermute | solution.py:28
  56.9 11.5 %collective-permute-start.25 = (bf16[4,128,512]{2,1,0:T(8,128)(2,1)S(1)}, bf16[4,128,512]{2,1,0:T(8,128)(2,1)S(1)}, u32[]{:S(2)}, u32[]{:S(2)}) collective-permute-start(bf16[4,128,512]{2,1,0:T(8,128)(2,1)S(1)} %collective-permute-done.22.refs_24_), channel_id=1, source_target_pairs={{0,1},{1,2},{2,3},{3,4},{4,5},{5,6},{6,7},{7,0},{8,9},{9,10},{10,1... | collective-permute-start | bytes 1572872 | tf_op jit(solution)/shard_map/ppermute | solution.py:28
  60.0 10.6 %collective-permute-start.19 = (bf16[1,2,256,512]{3,2,1,0:T(8,128)(2,1)S(1)}, bf16[1,2,256,512]{3,2,1,0:T(8,128)(2,1)S(1)}, u32[]{:S(2)}, u32[]{:S(2)}) collective-permute-start(bf16[1,2,256,512]{3,2,1,0:T(8,128)(2,1)S(1)} %collective-permute-done.6.refs_5_), channel_id=1, source_target_pairs={{0,24},{1,25},{2,26},{3,27},{4,28},{5,29},{6,30},{7,31},{8,0},{9,1... | collective-permute-start | bytes 1572872 | tf_op jit(solution)/shard_map/ppermute | solution.py:28
  62.7 11.2 %collective-permute-start.27 = (bf16[4,128,512]{2,1,0:T(8,128)(2,1)S(1)}, bf16[4,128,512]{2,1,0:T(8,128)(2,1)S(1)}, u32[]{:S(2)}, u32[]{:S(2)}) collective-permute-start(bf16[4,128,512]{2,1,0:T(8,128)(2,1)S(1)} %collective-permute-done.24.refs_18_), channel_id=1, source_target_pairs={{0,1},{1,2},{2,3},{3,4},{4,5},{5,6},{6,7},{7,0},{8,9},{9,10},{10,1... | collective-permute-start | bytes 1572872 | tf_op jit(solution)/shard_map/ppermute | solution.py:28
  65.8 10.2 %collective-permute-start.23 = (bf16[4,128,512]{2,1,0:T(8,128)(2,1)S(1)}, bf16[4,128,512]{2,1,0:T(8,128)(2,1)S(1)}, u32[]{:S(2)}, u32[]{:S(2)}) collective-permute-start(bf16[4,128,512]{2,1,0:T(8,128)(2,1)S(1)} %collective-permute-done.22.refs_24_), channel_id=1, source_target_pairs={{0,32},{1,33},{2,34},{3,35},{4,36},{5,37},{6,38},{7,39},{8,40},{9,... | collective-permute-start | bytes 1572872 | tf_op jit(solution)/shard_map/ppermute | solution.py:28
  65.8 10.2 %collective-permute-start.15 = (bf16[1,2,256,512]{3,2,1,0:T(8,128)(2,1)S(1)}, bf16[1,2,256,512]{3,2,1,0:T(8,128)(2,1)S(1)}, u32[]{:S(2)}, u32[]{:S(2)}) collective-permute-start(bf16[1,2,256,512]{3,2,1,0:T(8,128)(2,1)S(1)} %collective-permute-done.6.refs_5_), channel_id=1, source_target_pairs={{0,8},{1,9},{2,10},{3,11},{4,12},{5,13},{6,14},{7,15},{8,16},{9,17... | collective-permute-start | bytes 1572872 | tf_op jit(solution)/shard_map/ppermute | solution.py:28
  68.3 8.4 %collective-permute-start.26 = (bf16[4,128,512]{2,1,0:T(8,128)(2,1)S(1)}, bf16[4,128,512]{2,1,0:T(8,128)(2,1)S(1)}, u32[]{:S(2)}, u32[]{:S(2)}) collective-permute-start(bf16[4,128,512]{2,1,0:T(8,128)(2,1)S(1)} %collective-permute-done.25.refs_26_), channel_id=1, source_target_pairs={{0,32},{1,33},{2,34},{3,35},{4,36},{5,37},{6,38},{7,39},{8,40},{9,... | collective-permute-start | bytes 1572872 | tf_op jit(solution)/shard_map/ppermute | solution.py:28
  70.5 16.2 %collective-permute-start.21 = (bf16[2,2,256,512]{3,2,1,0:T(8,128)(2,1)S(1)}, bf16[2,2,256,512]{3,2,1,0:T(8,128)(2,1)S(1)}, u32[]{:S(2)}, u32[]{:S(2)}) collective-permute-start(bf16[2,2,256,512]{3,2,1,0:T(8,128)(2,1)S(1)} %collective-permute-done.7.refs_7_), channel_id=1, source_target_pairs={{0,8},{1,9},{2,10},{3,11},{4,12},{5,13},{6,14},{7,15},{8,16},{9,17... | collective-permute-start | bytes 3145736 | tf_op jit(solution)/shard_map/ppermute | solution.py:28
  74.0 3.6 %collective-permute-start.30 = (bf16[4,128,512]{2,1,0:T(8,128)(2,1)S(1)}, bf16[4,128,512]{2,1,0:T(8,128)(2,1)S(1)}, u32[]{:S(2)}, u32[]{:S(2)}) collective-permute-start(bf16[4,128,512]{2,1,0:T(8,128)(2,1)S(1)} %collective-permute-done.27.refs_20_), channel_id=1, source_target_pairs={{0,32},{1,33},{2,34},{3,35},{4,36},{5,37},{6,38},{7,39},{8,40},{9,... | collective-permute-start | bytes 1572872 | tf_op jit(solution)/shard_map/ppermute | solution.py:28
  76.0 2.3 %collective-permute-start.28 = (bf16[4,128,512]{2,1,0:T(8,128)(2,1)S(1)}, bf16[4,128,512]{2,1,0:T(8,128)(2,1)S(1)}, u32[]{:S(2)}, u32[]{:S(2)}) collective-permute-start(bf16[4,128,512]{2,1,0:T(8,128)(2,1)S(1)} %collective-permute-done.12.refs_14_), channel_id=1, source_target_pairs={{0,32},{1,33},{2,34},{3,35},{4,36},{5,37},{6,38},{7,39},{8,40},{9,... | collective-permute-start | bytes 1572872 | tf_op jit(solution)/shard_map/ppermute | solution.py:28
  76.1 8.4 %collective-permute-start.20 = (bf16[1,2,256,512]{3,2,1,0:T(8,128)(2,1)S(1)}, bf16[1,2,256,512]{3,2,1,0:T(8,128)(2,1)S(1)}, u32[]{:S(2)}, u32[]{:S(2)}) collective-permute-start(bf16[1,2,256,512]{3,2,1,0:T(8,128)(2,1)S(1)} %collective-permute-done.19.refs_10_), channel_id=1, source_target_pairs={{0,24},{1,25},{2,26},{3,27},{4,28},{5,29},{6,30},{7,31},{8,0},{9,1... | collective-permute-start | bytes 1572872 | tf_op jit(solution)/shard_map/ppermute | solution.py:28
  76.8 7.7 %collective-permute-start.29 = (bf16[4,128,512]{2,1,0:T(8,128)(2,1)S(1)}, bf16[4,128,512]{2,1,0:T(8,128)(2,1)S(1)}, u32[]{:S(2)}, u32[]{:S(2)}) collective-permute-start(bf16[4,128,512]{2,1,0:T(8,128)(2,1)S(1)} %collective-permute-done.24.refs_18_), channel_id=1, source_target_pairs={{0,32},{1,33},{2,34},{3,35},{4,36},{5,37},{6,38},{7,39},{8,40},{9,... | collective-permute-start | bytes 1572872 | tf_op jit(solution)/shard_map/ppermute | solution.py:28
  (4 other events, 23.2 us)

commit v4 on v3

v4 whole, which is shorter than its diff:
```python
import jax
import jax.numpy as jnp
from jax import lax
from jax.experimental import pallas as pl
from jax.experimental.pallas import tpu as pltpu
from jax.sharding import Mesh, PartitionSpec as P

LEN = 64
AXES = ("y", "c", "x", "z")
NY, NC, NX, NZ = SIZES = (4, 2, 4, 8)
VMEM = pl.BlockSpec(memory_space=pltpu.VMEM)
SMEM = pl.BlockSpec(memory_space=pltpu.SMEM)


def permute(block, move):
    pairs = []
    for y in range(NY):
        for c in range(NC):
            for x in range(NX):
                for z in range(NZ):
                    to = [a % n for a, n in zip(move(y, c, x, z), SIZES)]
                    pairs.append(
                        (
                            ((y * NC + c) * NX + x) * NZ + z,
                            ((to[0] * NC + to[1]) * NX + to[2]) * NZ + to[3],
                        )
                    )
    return lax.ppermute(block, AXES, pairs)


def swap(block):
    return permute(block, lambda y, c, x, z: (y, 1 - c, x, z))


def first(block, s):
    return permute(
        block, lambda y, c, x, z: (y + s, c, x, z) if c == 0 else (y, c, x + s, z)
    )


def second(block, s):
    return permute(
        block, lambda y, c, x, z: (y, c, x + s, z) if c == 0 else (y + s, c, x, z)
    )


def along_z(block):
    return permute(
        block, lambda y, c, x, z: (y, c, x, z + 1) if c == 0 else (y, c, x, z - 1)
    )


def across_z(block):
    return permute(
        block, lambda y, c, x, z: (y, 0, x, z + 1) if c == 1 else (y, 1, x, z - 1)
    )


def prep_kernel(place, lengths, hid, head, kept, other, blocks):
    c = place[1]
    half, width = kept.shape[0], blocks.shape[2]
    for out, part in ((kept, c), (other, 1 - c)):
        for p in range(half // LEN):
            n = lengths[part * (half // LEN) + p]
            at = pl.multiple_of(part * half + p * LEN, LEN)
            rows = hid[pl.ds(at, LEN), :]
            j = lax.broadcasted_iota(jnp.int32, rows.shape, 0)
            zero = jnp.zeros_like(rows)
            out[p * LEN : (p + 1) * LEN, :] = jnp.where(j < n, rows, zero)
    for s in range(blocks.shape[0]):
        blocks[s] = head[:, s * width : (s + 1) * width]


def prep(place, lengths, hidden, head):
    rows, cols = head.shape
    half = jax.ShapeDtypeStruct((hidden.shape[0] // NC, hidden.shape[1]), hidden.dtype)
    blocks = jax.ShapeDtypeStruct((NX, rows, cols // NX), head.dtype)
    return pl.pallas_call(
        prep_kernel,
        out_shape=[half, half, blocks],
        in_specs=[SMEM, SMEM, VMEM, VMEM],
        out_specs=[VMEM] * 3,
        compiler_params=pltpu.CompilerParams(vmem_limit_bytes=6 << 20),
    )(place, lengths, hidden, head)


ORDER = (
    ("h0", ()),
    ("f+", ()),
    ("f-", ()),
    ("A1", ("f+", "f-")),
    ("B1", ("f+", "f-")),
    ("sP+", ()),
    ("sP-", ()),
    ("ff", ()),
    ("sU-", ()),
    ("sU+", ()),
    ("A2", ("sU+", "sU-")),
    ("B2", ()),
    ("sF-", ()),
    ("gP", ()),
    ("A3", ("sP+", "sP-", "ff")),
    ("B3", ("sF-",)),
    ("B0", ("A1",)),
    ("c1", ()),
    ("gF", ()),
    ("sF+", ()),
    ("gU", ()),
    ("c2", ("c1", "B0")),
    ("A4", ("gU",)),
    ("c3", ("gP", "gF", "sum1")),
    ("c4", ("sF+", "c2", "c3", "sum2")),
)


def exchange(place, kept, other, blocks):
    got = {"kept": kept, "other": other}

    def own():
        if "own" not in got:
            got["own"] = jnp.stack([kept, got["h0"]])[None]
        return got["own"]

    def pair():
        if "pair" not in got:
            got["pair"] = jnp.concatenate([got["f+"], got["f-"]], axis=0)
        return got["pair"]

    def piece():
        if "A0" not in got:
            got["A0"] = lax.all_to_all(blocks, "x", split_axis=0, concat_axis=0)
        return got["A0"]

    moves = {
        "h0": (swap, lambda: other),
        "f+": (lambda b: first(b, 1), own),
        "f-": (lambda b: first(b, -1), own),
        "ff": (lambda b: first(b, 1), lambda: got["f+"]),
        "sU+": (lambda b: second(b, 1), own),
        "sU-": (lambda b: second(b, -1), own),
        "sP+": (lambda b: second(b, 1), pair),
        "sP-": (lambda b: second(b, -1), pair),
        "sF+": (lambda b: second(b, 1), lambda: got["ff"]),
        "sF-": (lambda b: second(b, -1), lambda: got["ff"]),
        "gU": (lambda b: second(b, -1), lambda: got["sU-"]),
        "gP": (lambda b: second(b, 1), lambda: got["sP+"]),
        "gF": (lambda b: second(b, -1), lambda: got["sF-"]),
        "B0": (swap, piece),
        "A1": (along_z, piece),
        "B1": (across_z, piece),
        "A2": (along_z, lambda: got["A1"]),
        "B2": (along_z, lambda: got["B1"]),
        "A3": (along_z, lambda: got["A2"]),
        "B3": (along_z, lambda: got["B2"]),
        "A4": (along_z, lambda: got["A3"]),
    }
    moves["c4"] = (swap, lambda: got["A4"])
    for n in "123":
        moves["c" + n] = (swap, lambda n=n: jnp.stack([got["A" + n], got["B" + n]]))
    for name, arrived in ORDER:
        for k in range(len(STAGES)):
            if "sum%d" % (k + 1) in arrived:
                got["sum%d" % (k + 1)] = run_stage(k, place, got)
        move, operand = moves[name]
        block = operand()
        if arrived:
            block = lax.optimization_barrier((block, *(got[a] for a in arrived)))[0]
        got[name] = move(block)
    for k in range(len(STAGES)):
        if "sum%d" % (k + 1) not in got:
            got["sum%d" % (k + 1)] = run_stage(k, place, got)
    return got["sum%d" % len(STAGES)]


STEPS = {
    "own": (0, 0),
    "sU+": (0, -1),
    "sU-": (0, 1),
    "pair": (None, 0),
    "ff": (2, 0),
    "gU": (0, 2),
    "sP+": (None, -1),
    "sP-": (None, 1),
    "sF+": (2, -1),
    "sF-": (2, 1),
    "gF": (2, 2),
    "gP": (None, 2),
}
PIECES = {
    0: ("A0", "B0"),
    -1: ("A1", "B1"),
    1: ("c1", "c1"),
    -2: ("A2", "B2"),
    2: ("c2", "c2"),
    -3: ("A3", "B3"),
    3: ("c3", "c3"),
    4: ("A4", "c4"),
}
ONE, TWO, THREE = (-1, -2), (0, -3, 1, 2), (3, 4)
EARLY, LATER = ("own", "pair", "ff", "sP+", "sP-", "sU+", "sU-"), ("sF-", "gP", "gF", "gU")
STAGES = (
    [(n, ONE) for n in EARLY],
    [(n, TWO) for n in EARLY] + [(n, ONE + TWO) for n in LATER],
    [(n, THREE) for n in EARLY + LATER] + [("sF+", ONE + TWO + THREE)],
)


def stage_kernel(work, names, before, last, *refs):
    n = len(names)
    place, arrays, o_ref = refs[0], dict(zip(names, refs[1 : 1 + n])), refs[-1 - last]
    acc = refs[-1]
    y, c, x, z = (place[i] for i in range(4))
    rows = arrays[PIECES[work[0][1][0]][0]].shape[-2]

    def pick(step, col):
        ref = arrays[PIECES[step][col]]
        return ref.at[1 - col] if len(ref.shape) == 4 else ref

    if before:
        acc[...] = refs[1 + n][...]
    else:
        acc[...] = jnp.zeros_like(acc)
    for name, steps in work:
        ref = arrays[name]
        a, b = STEPS[name]
        per = ref.shape[-1] // rows
        at_z = [lax.rem(z + (1 - 2 * c) * s + NZ, NZ) for s in steps]
        halves = [jnp.where(lax.div(f, per) == c, 0, 1) for f in at_z]
        lanes = [pl.multiple_of(lax.rem(f, per) * rows, rows) for f in at_z]

        def unit(u, _):
            along = 2 * u - 1 if a is None else a
            at_y = lax.rem(y + jnp.where(c == 0, along, b) + NY, NY)
            at_x = lax.rem(x + jnp.where(c == 0, b, along) + NX, NX)
            left = jnp.concatenate(
                [ref[u, h, :, pl.ds(at, rows)] for h, at in zip(halves, lanes)], axis=1
            )
            for col in range(NC):
                right = jnp.concatenate(
                    [pick(s, col)[at_y] for s in steps], axis=0
                )
                acc[col, at_x] += jnp.dot(
                    left, right, preferred_element_type=jnp.float32
                )
            return 0

        lax.fori_loop(0, ref.shape[0], unit, 0)
    if last:
        for col in range(NC):
            for i in range(NX):
                tokens, cols = acc.shape[2:]
                top = jnp.max(acc[col, i].reshape(tokens // LEN, LEN, cols), axis=1)
                o_ref[lax.rem(c + col, NC), i] = jnp.log1p(jnp.maximum(top, 0.0))


def run_stage(k, place, got):
    tokens = got["own"].shape[-2]
    cols = got["A0"].shape[-1]
    total = jax.ShapeDtypeStruct((NC, NX, tokens, cols), jnp.float32)
    result = jax.ShapeDtypeStruct((NC, NX, tokens // LEN, cols), jnp.float32)
    work = STAGES[k]
    names = list(dict.fromkeys(n for n, _ in work))
    names += list(dict.fromkeys(p for _, ss in work for s in ss for p in PIECES[s]))
    last = k == len(STAGES) - 1
    carried = [got["sum%d" % k]] if k else []

    def kernel(*refs):
        stage_kernel(work, names, k > 0, last, *refs)

    return pl.pallas_call(
        kernel,
        out_shape=result if last else total,
        in_specs=[SMEM] + [VMEM] * (len(names) + len(carried)),
        out_specs=VMEM,
        scratch_shapes=[pltpu.VMEM(total.shape, total.dtype)] if last else [],
        input_output_aliases={1 + len(names): 0} if carried and not last else {},
        compiler_params=pltpu.CompilerParams(vmem_limit_bytes=14 << 20),
    )(place, *(got[n] for n in names), *carried)


def body(hidden, head_weight, lengths):
    place = jnp.stack([lax.axis_index(a) for a in AXES]).astype(jnp.int32)
    kept, other, blocks = prep(place, lengths, hidden, head_weight)
    pooled = exchange(place, kept, other, blocks).astype(jnp.bfloat16)
    each = pooled.shape[-1] // NZ
    pooled = pooled.reshape(NC, NX * pooled.shape[2], NZ, each)
    pooled = jnp.transpose(pooled, (2, 0, 1, 3)).reshape(NZ * NC, -1, each)
    got = lax.all_to_all(pooled, ("z", "c"), split_axis=0, concat_axis=0, tiled=True)
    got = got.reshape(NZ, NC, NX, -1, each)
    got = jnp.transpose(got, (2, 0, 1, 3, 4)).reshape(-1, each).astype(jnp.float32)
    peak = jnp.max(got, axis=0)
    return jnp.transpose((got / (1.0 + peak)[None, :]).astype(jnp.bfloat16))


def solution(mesh):
    fine = Mesh(mesh.devices.reshape(SIZES), AXES)
    return jax.shard_map(
        body,
        mesh=fine,
        in_specs=(P(("x", "z"), ("y", "c")), P(("x", "z"), ("y", "c")), P(("x", "z"))),
        out_specs=P(("y", "c", "x", "z"), None),
        check_vma=False,
    )
```

time: 114 us -> 108 us (0.947)
  waiting for transfers between devices: 40 us -> 25.4 us
  Pallas kernels: 14.4 us -> 19.4 us
  starting transfers between devices: 42.6 us -> 46.3 us
  local copies, waits for them, and re-layouts: 1.16 us -> 3.88 us
  blocking collectives: 13.7 us -> 12.3 us
  other arithmetic: 1.77 us -> 0.51 us
    ppermute x31 -> x25, waiting for transfers between devices: 40 us -> 17.8 us  [permute(): return lax.ppermute(block, AXES, pairs)]
    all_to_all x0 -> x1, waiting for transfers between devices: none -> 7.59 us  [piece(): got['A0'] = lax.all_to_all(blocks, 'x', split_axis=0, concat_axis=0)]
    pallas_call x2 -> x4, Pallas kernels: 14.4 us -> 19.4 us  [the longest x3 18 us: run_stage(): pl.pallas_call(kernel, out_shape=result if last else total, in_specs=[SME...]
    all_to_all x0 -> x1, starting transfers between devices: none -> 3.47 us  [piece(): got['A0'] = lax.all_to_all(blocks, 'x', split_axis=0, concat_axis=0)]
    unnamed x13 -> x9, local copies, waits for them, and re-layouts: 0.27 us -> 2.99 us
    all_to_all x1, blocking collectives: 13.7 us -> 12.3 us  [body(): lax.all_to_all(pooled, ('z', 'c'), split_axis=0, concat_axis=0, tiled=True)]
    ppermute x31 -> x25, starting transfers between devices: 42.6 us -> 42.8 us  [permute(): return lax.ppermute(block, AXES, pairs)]
  transfers between devices with their start and end apart: 31 -> 26, of which waited for: 16 -> 9; matrix products, arithmetic and copies ran while one was open for 0% -> 0% of each run, Pallas kernels for 0% -> 11%
where the time goes in v4:
time: 108 us
  starting transfers between devices  46.3 us (43%)
  waiting for transfers between devices  25.4 us (24%)
  Pallas kernels  19.4 us (18%)
  blocking collectives  12.3 us (11%)
  local copies, waits for them, and re-layouts  3.88 us (4%)
    ppermute x25, starting transfers between devices, permute(): return lax.ppermute(block, AXES, pairs)  42.8 us
    pallas_call x3, Pallas kernels, run_stage(): pl.pallas_call(kernel, out_shape=result if last else total, in_specs=[SME...  18 us
    ppermute x25, waiting for transfers between devices, permute(): return lax.ppermute(block, AXES, pairs)  17.8 us
    all_to_all x1, blocking collectives, body(): lax.all_to_all(pooled, ('z', 'c'), split_axis=0, concat_axis=0, tiled=True)  12.3 us
    all_to_all x1, waiting for transfers between devices, piece(): got['A0'] = lax.all_to_all(blocks, 'x', split_axis=0, concat_axis=0)  7.59 us
    all_to_all x1, starting transfers between devices, piece(): got['A0'] = lax.all_to_all(blocks, 'x', split_axis=0, concat_axis=0)  3.47 us
    unnamed x9, local copies, waits for them, and re-layouts  2.99 us
  transfers between devices with their start and end apart: 26, of which 9 were waited for; matrix products, arithmetic and copies ran while one was open for 0% of the time, Pallas kernels for 11%

profile of v4, /device:TPU:1, one launch (start us, length us, event | category | flops | bytes accessed | tf_op | source)
XLA Modules:
  0.0 107.9 jit_solution(12157255615052613828)
XLA Ops:
  0.1 1.0 copy-done
  1.1 1.0 copy-done.1
  2.8 1.4 %shard_map.37 = (bf16[256,512]{1,0:T(8,128)(2,1)S(1)}, bf16[256,512]{1,0:T(8,128)(2,1)S(1)}, bf16[4,128,512]{2,1,0:T(8,128)(2,1)}) custom-call(s32[4]{0:T(128)S(1)} %pad_add_fusion.place.refs_0_, s32[8]{0:T(128)S(1)} %copy-done.2, bf16[512,512]{1,0:T(8,128)(2,1)S(1)} %copy-done, bf16[128,2048]{1,0:T(8,128)(2,1)S(1)} %copy-done.1), custom_call_target="tpu_custom_call" | custom-call | tf_op jit(solution)/shard_map/pallas_call | solution.py:78
  4.3 3.2 %collective-permute-start = (bf16[256,512]{1,0:T(8,128)(2,1)S(1)}, bf16[256,512]{1,0:T(8,128)(2,1)S(1)}, u32[]{:S(2)}, u32[]{:S(2)}) collective-permute-start(bf16[256,512]{1,0:T(8,128)(2,1)S(1)} %get-tuple-element.18), channel_id=1, source_target_pairs={{0,32},{1,33},{2,34},{3,35},{4,36},{5,37},{6,38},{7,39},{8,40},{9,... | collective-permute-start | bytes 786440 | tf_op jit(solution)/shard_map/ppermute | solution.py:28
  7.5 1.2 %collective-permute-done = bf16[256,512]{1,0:T(8,128)(2,1)S(1)} collective-permute-done((bf16[256,512]{1,0:T(8,128)(2,1)S(1)}, bf16[256,512]{1,0:T(8,128)(2,1)S(1)}, u32[]{:S(2)}, u32[]{:S(2)}) %collective-permute-start) | collective-permute-done | bytes 262176 | tf_op jit(solution)/shard_map/ppermute | solution.py:28
  8.8 2.7 %collective-permute-start.2 = (bf16[1,2,256,512]{3,2,1,0:T(8,128)(2,1)S(1)}, bf16[1,2,256,512]{3,2,1,0:T(8,128)(2,1)S(1)}, u32[]{:S(2)}, u32[]{:S(2)}) collective-permute-start(bf16[1,2,256,512]{3,2,1,0:T(8,128)(2,1)S(1)} %maximum_bitcast_fusion.refs_1_), channel_id=1, source_target_pairs={{0,192},{1,193},{2,194},{3,195},{4,196},{5,197},{6,198},{7,199},{8... | collective-permute-start | bytes 1572872 | tf_op jit(solution)/shard_map/ppermute | solution.py:28
  11.5 3.5 %all-to-all-start = ((bf16[4,128,512]{2,1,0:T(8,128)(2,1)}), bf16[4,128,512]{2,1,0:T(8,128)(2,1)S(1)}, u32[]{:S(2)}, u32[]{:S(2)}) async-start(bf16[4,128,512]{2,1,0:T(8,128)(2,1)} %get-tuple-element.19), calls=%async_computation | async-start | bytes 1048576 | tf_op jit(solution)/shard_map/all_to_all | solution.py:131
  14.9 1.1 collective-permute-start.7
  16.5 7.6 %all-to-all-done.refs_12_.refs_20_ = bf16[4,128,512]{2,1,0:T(8,128)(2,1)S(1)} async-done(((bf16[4,128,512]{2,1,0:T(8,128)(2,1)}), bf16[4,128,512]{2,1,0:T(8,128)(2,1)S(1)}, u32[]{:S(2)}, u32[]{:S(2)}) %all-to-all-start) | async-done | bytes 524320 | tf_op jit(solution)/shard_map/all_to_all | solution.py:131
  24.1 2.1 %collective-permute-start.13 = (bf16[4,128,512]{2,1,0:T(8,128)(2,1)S(1)}, bf16[4,128,512]{2,1,0:T(8,128)(2,1)S(1)}, u32[]{:S(2)}, u32[]{:S(2)}) collective-permute-start(bf16[4,128,512]{2,1,0:T(8,128)(2,1)S(1)} %all-to-all-done.refs_12_.refs_20_), channel_id=1, source_target_pairs={{0,1},{1,2},{2,3},{3,4},{4,5},{5,6},{6,7},{7,0},{8,9},{9,10},{10,1... | collective-permute-start | bytes 1572872 | tf_op jit(solution)/shard_map/ppermute | solution.py:28
  26.3 3.1 %collective-permute-start.4 = (bf16[2,2,256,512]{3,2,1,0:T(8,128)(2,1)S(1)}, bf16[2,2,256,512]{3,2,1,0:T(8,128)(2,1)S(1)}, u32[]{:S(2)}, u32[]{:S(2)}) collective-permute-start(bf16[2,2,256,512]{3,2,1,0:T(8,128)(2,1)S(1)} %constant_dynamic-update-slice_fusion.refs_2_), channel_id=1, source_target_pairs={{0,8},{1,9},{2,10},{3,11},{4,12},{5,13},{6,14},{7,15},{8,16},{9,17... | collective-permute-start | bytes 3145736 | tf_op jit(solution)/shard_map/ppermute | solution.py:28
  29.4 1.5 %collective-permute-start.5 = (bf16[2,2,256,512]{3,2,1,0:T(8,128)(2,1)S(1)}, bf16[2,2,256,512]{3,2,1,0:T(8,128)(2,1)S(1)}, u32[]{:S(2)}, u32[]{:S(2)}) collective-permute-start(bf16[2,2,256,512]{3,2,1,0:T(8,128)(2,1)S(1)} %constant_dynamic-update-slice_fusion.refs_2_), channel_id=1, source_target_pairs={{0,24},{1,25},{2,26},{3,27},{4,28},{5,29},{6,30},{7,31},{8,0},{9,1... | collective-permute-start | bytes 3145736 | tf_op jit(solution)/shard_map/ppermute | solution.py:28
  30.9 1.3 %collective-permute-start.3 = (bf16[1,2,256,512]{3,2,1,0:T(8,128)(2,1)S(1)}, bf16[1,2,256,512]{3,2,1,0:T(8,128)(2,1)S(1)}, u32[]{:S(2)}, u32[]{:S(2)}) collective-permute-start(bf16[1,2,256,512]{3,2,1,0:T(8,128)(2,1)S(1)} %collective-permute-done.1), channel_id=1, source_target_pairs={{0,64},{1,65},{2,66},{3,67},{4,68},{5,69},{6,70},{7,71},{8,72},{9,... | collective-permute-start | bytes 1572872 | tf_op jit(solution)/shard_map/ppermute | solution.py:28
  32.4 3.3 %collective-permute-start.14 = (bf16[4,128,512]{2,1,0:T(8,128)(2,1)S(1)}, bf16[4,128,512]{2,1,0:T(8,128)(2,1)S(1)}, u32[]{:S(2)}, u32[]{:S(2)}) collective-permute-start(bf16[4,128,512]{2,1,0:T(8,128)(2,1)S(1)} %collective-permute-done.13.refs_8_.refs_18_.refs_16_), channel_id=1, source_target_pairs={{0,1},{1,2},{2,3},{3,4},{4,5},{5,6},{6,7},{7,0},{8,9},{9,10},{10,1... | collective-permute-start | bytes 1572872 | tf_op jit(solution)/shard_map/ppermute | solution.py:28
  35.7 8.8 %collective-permute-done.16.refs_9_.refs_19_.refs_17_ = bf16[4,128,512]{2,1,0:T(8,128)(2,1)S(1)} collective-permute-done((bf16[4,128,512]{2,1,0:T(8,128)(2,1)S(1)}, bf16[4,128,512]{2,1,0:T(8,128)(2,1)S(1)}, u32[]{:S(2)}, u32[]{:S(2)}) %collective-permute-start.16) | collective-permute-done | bytes 524320 | tf_op jit(solution)/shard_map/ppermute | solution.py:28
  44.8 2.3 %collective-permute-done.3.refs_3_ = bf16[1,2,256,512]{3,2,1,0:T(8,128)(2,1)S(1)} collective-permute-done((bf16[1,2,256,512]{3,2,1,0:T(8,128)(2,1)S(1)}, bf16[1,2,256,512]{3,2,1,0:T(8,128)(2,1)S(1)}, u32[]{:S(2)}, u32[]{:S(2)}) %collective-permute-start.3) | collective-permute-done | bytes 524320 | tf_op jit(solution)/shard_map/ppermute | solution.py:28
  47.7 1.8 %collective-permute-start.8 = (bf16[1,2,256,512]{3,2,1,0:T(8,128)(2,1)S(1)}, bf16[1,2,256,512]{3,2,1,0:T(8,128)(2,1)S(1)}, u32[]{:S(2)}, u32[]{:S(2)}) collective-permute-start(bf16[1,2,256,512]{3,2,1,0:T(8,128)(2,1)S(1)} %collective-permute-done.3.refs_3_), channel_id=1, source_target_pairs={{0,24},{1,25},{2,26},{3,27},{4,28},{5,29},{6,30},{7,31},{8,0},{9,1... | collective-permute-start | bytes 1572872 | tf_op jit(solution)/shard_map/ppermute | solution.py:28
  49.6 2.3 %collective-permute-start.22 = (bf16[4,128,512]{2,1,0:T(8,128)(2,1)S(1)}, bf16[4,128,512]{2,1,0:T(8,128)(2,1)S(1)}, u32[]{:S(2)}, u32[]{:S(2)}) collective-permute-start(bf16[4,128,512]{2,1,0:T(8,128)(2,1)S(1)} %all-to-all-done.refs_12_.refs_20_), channel_id=1, source_target_pairs={{0,32},{1,33},{2,34},{3,35},{4,36},{5,37},{6,38},{7,39},{8,40},{9,... | collective-permute-start | bytes 1572872 | tf_op jit(solution)/shard_map/ppermute | solution.py:28
  51.9 0.9 collective-permute-start.9
  52.8 2.6 %collective-permute-done.17.refs_11_.refs_21_.refs_19_ = bf16[4,128,512]{2,1,0:T(8,128)(2,1)S(1)} collective-permute-done((bf16[4,128,512]{2,1,0:T(8,128)(2,1)S(1)}, bf16[4,128,512]{2,1,0:T(8,128)(2,1)S(1)}, u32[]{:S(2)}, u32[]{:S(2)}) %collective-permute-start.17) | collective-permute-done | bytes 524320 | tf_op jit(solution)/shard_map/ppermute | solution.py:28
  55.3 1.6 %collective-permute-start.15 = (bf16[4,128,512]{2,1,0:T(8,128)(2,1)S(1)}, bf16[4,128,512]{2,1,0:T(8,128)(2,1)S(1)}, u32[]{:S(2)}, u32[]{:S(2)}) collective-permute-start(bf16[4,128,512]{2,1,0:T(8,128)(2,1)S(1)} %collective-permute-done.14.refs_10_.refs_20_.refs_18_), channel_id=1, source_target_pairs={{0,1},{1,2},{2,3},{3,4},{4,5},{5,6},{6,7},{7,0},{8,9},{9,10},{10,1... | collective-permute-start | bytes 1572872 | tf_op jit(solution)/shard_map/ppermute | solution.py:28
  57.0 2.3 %collective-permute-start.18 = (bf16[4,128,512]{2,1,0:T(8,128)(2,1)S(1)}, bf16[4,128,512]{2,1,0:T(8,128)(2,1)S(1)}, u32[]{:S(2)}, u32[]{:S(2)}) collective-permute-start(bf16[4,128,512]{2,1,0:T(8,128)(2,1)S(1)} %collective-permute-done.17.refs_11_.refs_21_.refs_19_), channel_id=1, source_target_pairs={{0,1},{1,2},{2,3},{3,4},{4,5},{5,6},{6,7},{7,0},{8,9},{9,10},{10,1... | collective-permute-start | bytes 1572872 | tf_op jit(solution)/shard_map/ppermute | solution.py:28
  59.3 3.4 %collective-permute-start.10 = (bf16[1,2,256,512]{3,2,1,0:T(8,128)(2,1)S(1)}, bf16[1,2,256,512]{3,2,1,0:T(8,128)(2,1)S(1)}, u32[]{:S(2)}, u32[]{:S(2)}) collective-permute-start(bf16[1,2,256,512]{3,2,1,0:T(8,128)(2,1)S(1)} %collective-permute-done.8.refs_8_), channel_id=1, source_target_pairs={{0,24},{1,25},{2,26},{3,27},{4,28},{5,29},{6,30},{7,31},{8,0},{9,1... | collective-permute-start | bytes 1572872 | tf_op jit(solution)/shard_map/ppermute | solution.py:28
  62.7 3.5 %shard_map.38.refs_22_ = f32[2,4,256,512]{3,2,1,0:T(8,128)S(1)} custom-call(s32[4]{0:T(128)S(1)} %pad_add_fusion.place.refs_0_, bf16[1,2,256,512]{3,2,1,0:T(8,128)(2,1)S(1)} %maximum_bitcast_fusion.refs_1_, bf16[2,2,256,512]{3,2,1,0:T(8,128)(2,1)S(1)} %constant_dynamic-update-slice_fusion.refs_2_, ...), custom_call_target="tpu_custom_call" | custom-call | tf_op jit(solution)/shard_map/pallas_call | solution.py:270
  66.5 2.5 %collective-permute-start.23 = (bf16[2,4,128,512]{3,2,1,0:T(8,128)(2,1)S(1)}, bf16[2,4,128,512]{3,2,1,0:T(8,128)(2,1)S(1)}, u32[]{:S(2)}, u32[]{:S(2)}) collective-permute-start(bf16[2,4,128,512]{3,2,1,0:T(8,128)(2,1)S(1)} %pad_maximum_fusion.1), channel_id=1, source_target_pairs={{0,32},{1,33},{2,34},{3,35},{4,36},{5,37},{6,38},{7,39},{8,40},{9,... | collective-permute-start | bytes 3145736 | tf_op jit(solution)/shard_map/ppermute | solution.py:28
  69.7 5.1 %collective-permute-start.19 = (bf16[2,4,128,512]{3,2,1,0:T(8,128)(2,1)S(1)}, bf16[2,4,128,512]{3,2,1,0:T(8,128)(2,1)S(1)}, u32[]{:S(2)}, u32[]{:S(2)}) collective-permute-start(bf16[2,4,128,512]{3,2,1,0:T(8,128)(2,1)S(1)} %pad_maximum_fusion), channel_id=1, source_target_pairs={{0,32},{1,33},{2,34},{3,35},{4,36},{5,37},{6,38},{7,39},{8,40},{9,... | collective-permute-start | bytes 3145736 | tf_op jit(solution)/shard_map/ppermute | solution.py:28
  74.8 0.7 collective-permute-start.20
  75.5 8.3 %shard_map.39.refs_26_ = f32[2,4,256,512]{3,2,1,0:T(8,128)S(1)} custom-call(s32[4]{0:T(128)S(1)} %pad_add_fusion.place.refs_0_, bf16[1,2,256,512]{3,2,1,0:T(8,128)(2,1)S(1)} %maximum_bitcast_fusion.refs_1_, bf16[2,2,256,512]{3,2,1,0:T(8,128)(2,1)S(1)} %constant_dynamic-update-slice_fusion.refs_2_, ...), custom_call_target="tpu_custom_call", output_to_operand_aliasing={{}: (22, {})} | custom-call | tf_op jit(solution)/shard_map/pallas_call | solution.py:270
  84.3 2.4 %collective-permute-start.24 = (bf16[4,128,512]{2,1,0:T(8,128)(2,1)S(1)}, bf16[4,128,512]{2,1,0:T(8,128)(2,1)S(1)}, u32[]{:S(2)}, u32[]{:S(2)}) collective-permute-start(bf16[4,128,512]{2,1,0:T(8,128)(2,1)S(1)} %collective-permute-done.20.refs_14_), channel_id=1, source_target_pairs={{0,32},{1,33},{2,34},{3,35},{4,36},{5,37},{6,38},{7,39},{8,40},{9,... | collective-permute-start | bytes 1572872 | tf_op jit(solution)/shard_map/ppermute | solution.py:28
  86.7 1.5 %collective-permute-done.24.refs_15_ = bf16[4,128,512]{2,1,0:T(8,128)(2,1)S(1)} collective-permute-done((bf16[4,128,512]{2,1,0:T(8,128)(2,1)S(1)}, bf16[4,128,512]{2,1,0:T(8,128)(2,1)S(1)}, u32[]{:S(2)}, u32[]{:S(2)}) %collective-permute-start.24) | collective-permute-done | bytes 524320 | tf_op jit(solution)/shard_map/ppermute | solution.py:28
  88.3 6.1 %shard_map.40 = f32[2,4,4,512]{3,2,1,0:T(4,128)S(1)} custom-call(s32[4]{0:T(128)S(1)} %pad_add_fusion.place.refs_0_, bf16[1,2,256,512]{3,2,1,0:T(8,128)(2,1)S(1)} %maximum_bitcast_fusion.refs_1_, bf16[2,2,256,512]{3,2,1,0:T(8,128)(2,1)S(1)} %constant_dynamic-update-slice_fusion.refs_2_, bf16[1,2,256,512]{3,2,1,0:T(8,128)(2,1)S(1)} %collective-permute-done.3.refs_3_, ...), custom_call_target="tpu_custom_call" | custom-call | tf_op jit(solution)/shard_map/pallas_call | solution.py:270
  94.7 12.3 %all_to_all.10 = bf16[16,2,512]{2,1,0:T(2,128)(2,1)S(1)} all-to-all(bf16[16,2,512]{2,1,0:T(2,128)(2,1)S(1)} %reshape.20), channel_id=1, replica_groups=mesh['y'=4,'c'=2,'x'=4,'z'=8] {'z','c'}, dimensions={0} | all-to-all | bytes 65536 | tf_op jit(solution)/shard_map/all_to_all | solution.py:288
  (48 shorter events, 5.2 us)
Async XLA Ops:
  0.1 1.0 copy-start
  1.1 1.0 copy-start.1
  2.2 0.7 copy-start.2
  4.3 4.4 %collective-permute-start = (bf16[256,512]{1,0:T(8,128)(2,1)S(1)}, bf16[256,512]{1,0:T(8,128)(2,1)S(1)}, u32[]{:S(2)}, u32[]{:S(2)}) collective-permute-start(bf16[256,512]{1,0:T(8,128)(2,1)S(1)} %get-tuple-element.18), channel_id=1, source_target_pairs={{0,32},{1,33},{2,34},{3,35},{4,36},{5,37},{6,38},{7,39},{8,40},{9,... | collective-permute-start | bytes 786440 | tf_op jit(solution)/shard_map/ppermute | solution.py:28
  8.7 15.4 %collective-permute-start.1 = (bf16[1,2,256,512]{3,2,1,0:T(8,128)(2,1)S(1)}, bf16[1,2,256,512]{3,2,1,0:T(8,128)(2,1)S(1)}, u32[]{:S(2)}, u32[]{:S(2)}) collective-permute-start(bf16[1,2,256,512]{3,2,1,0:T(8,128)(2,1)S(1)} %maximum_bitcast_fusion.refs_1_), channel_id=1, source_target_pairs={{0,64},{1,65},{2,66},{3,67},{4,68},{5,69},{6,70},{7,71},{8,72},{9,... | collective-permute-start | bytes 1572872 | tf_op jit(solution)/shard_map/ppermute | solution.py:28
  8.8 15.3 %collective-permute-start.2 = (bf16[1,2,256,512]{3,2,1,0:T(8,128)(2,1)S(1)}, bf16[1,2,256,512]{3,2,1,0:T(8,128)(2,1)S(1)}, u32[]{:S(2)}, u32[]{:S(2)}) collective-permute-start(bf16[1,2,256,512]{3,2,1,0:T(8,128)(2,1)S(1)} %maximum_bitcast_fusion.refs_1_), channel_id=1, source_target_pairs={{0,192},{1,193},{2,194},{3,195},{4,196},{5,197},{6,198},{7,199},{8... | collective-permute-start | bytes 1572872 | tf_op jit(solution)/shard_map/ppermute | solution.py:28
  11.5 12.6 %all-to-all-start = ((bf16[4,128,512]{2,1,0:T(8,128)(2,1)}), bf16[4,128,512]{2,1,0:T(8,128)(2,1)S(1)}, u32[]{:S(2)}, u32[]{:S(2)}) async-start(bf16[4,128,512]{2,1,0:T(8,128)(2,1)} %get-tuple-element.19), calls=%async_computation | async-start | bytes 1048576 | tf_op jit(solution)/shard_map/all_to_all | solution.py:131
  14.9 16.0 %collective-permute-start.7 = (bf16[1,2,256,512]{3,2,1,0:T(8,128)(2,1)S(1)}, bf16[1,2,256,512]{3,2,1,0:T(8,128)(2,1)S(1)}, u32[]{:S(2)}, u32[]{:S(2)}) collective-permute-start(bf16[1,2,256,512]{3,2,1,0:T(8,128)(2,1)S(1)} %maximum_bitcast_fusion.refs_1_), channel_id=1, source_target_pairs={{0,24},{1,25},{2,26},{3,27},{4,28},{5,29},{6,30},{7,31},{8,0},{9,1... | collective-permute-start | bytes 1572872 | tf_op jit(solution)/shard_map/ppermute | solution.py:28
  16.0 14.9 %collective-permute-start.6 = (bf16[1,2,256,512]{3,2,1,0:T(8,128)(2,1)S(1)}, bf16[1,2,256,512]{3,2,1,0:T(8,128)(2,1)S(1)}, u32[]{:S(2)}, u32[]{:S(2)}) collective-permute-start(bf16[1,2,256,512]{3,2,1,0:T(8,128)(2,1)S(1)} %maximum_bitcast_fusion.refs_1_), channel_id=1, source_target_pairs={{0,8},{1,9},{2,10},{3,11},{4,12},{5,13},{6,14},{7,15},{8,16},{9,17... | collective-permute-start | bytes 1572872 | tf_op jit(solution)/shard_map/ppermute | solution.py:28
  24.1 8.3 %collective-permute-start.13 = (bf16[4,128,512]{2,1,0:T(8,128)(2,1)S(1)}, bf16[4,128,512]{2,1,0:T(8,128)(2,1)S(1)}, u32[]{:S(2)}, u32[]{:S(2)}) collective-permute-start(bf16[4,128,512]{2,1,0:T(8,128)(2,1)S(1)} %all-to-all-done.refs_12_.refs_20_), channel_id=1, source_target_pairs={{0,1},{1,2},{2,3},{3,4},{4,5},{5,6},{6,7},{7,0},{8,9},{9,10},{10,1... | collective-permute-start | bytes 1572872 | tf_op jit(solution)/shard_map/ppermute | solution.py:28
  26.3 23.3 %collective-permute-start.4 = (bf16[2,2,256,512]{3,2,1,0:T(8,128)(2,1)S(1)}, bf16[2,2,256,512]{3,2,1,0:T(8,128)(2,1)S(1)}, u32[]{:S(2)}, u32[]{:S(2)}) collective-permute-start(bf16[2,2,256,512]{3,2,1,0:T(8,128)(2,1)S(1)} %constant_dynamic-update-slice_fusion.refs_2_), channel_id=1, source_target_pairs={{0,8},{1,9},{2,10},{3,11},{4,12},{5,13},{6,14},{7,15},{8,16},{9,17... | collective-permute-start | bytes 3145736 | tf_op jit(solution)/shard_map/ppermute | solution.py:28
  29.4 22.5 %collective-permute-start.5 = (bf16[2,2,256,512]{3,2,1,0:T(8,128)(2,1)S(1)}, bf16[2,2,256,512]{3,2,1,0:T(8,128)(2,1)S(1)}, u32[]{:S(2)}, u32[]{:S(2)}) collective-permute-start(bf16[2,2,256,512]{3,2,1,0:T(8,128)(2,1)S(1)} %constant_dynamic-update-slice_fusion.refs_2_), channel_id=1, source_target_pairs={{0,24},{1,25},{2,26},{3,27},{4,28},{5,29},{6,30},{7,31},{8,0},{9,1... | collective-permute-start | bytes 3145736 | tf_op jit(solution)/shard_map/ppermute | solution.py:28
  30.9 13.6 %collective-permute-start.16 = (bf16[4,128,512]{2,1,0:T(8,128)(2,1)S(1)}, bf16[4,128,512]{2,1,0:T(8,128)(2,1)S(1)}, u32[]{:S(2)}, u32[]{:S(2)}) collective-permute-start(bf16[4,128,512]{2,1,0:T(8,128)(2,1)S(1)} %all-to-all-done.refs_12_.refs_20_), channel_id=1, source_target_pairs={{0,39},{1,32},{2,33},{3,34},{4,35},{5,36},{6,37},{7,38},{8,47},{9,... | collective-permute-start | bytes 1572872 | tf_op jit(solution)/shard_map/ppermute | solution.py:28
  30.9 16.1 %collective-permute-start.3 = (bf16[1,2,256,512]{3,2,1,0:T(8,128)(2,1)S(1)}, bf16[1,2,256,512]{3,2,1,0:T(8,128)(2,1)S(1)}, u32[]{:S(2)}, u32[]{:S(2)}) collective-permute-start(bf16[1,2,256,512]{3,2,1,0:T(8,128)(2,1)S(1)} %collective-permute-done.1), channel_id=1, source_target_pairs={{0,64},{1,65},{2,66},{3,67},{4,68},{5,69},{6,70},{7,71},{8,72},{9,... | collective-permute-start | bytes 1572872 | tf_op jit(solution)/shard_map/ppermute | solution.py:28
  32.4 15.3 %collective-permute-start.14 = (bf16[4,128,512]{2,1,0:T(8,128)(2,1)S(1)}, bf16[4,128,512]{2,1,0:T(8,128)(2,1)S(1)}, u32[]{:S(2)}, u32[]{:S(2)}) collective-permute-start(bf16[4,128,512]{2,1,0:T(8,128)(2,1)S(1)} %collective-permute-done.13.refs_8_.refs_18_.refs_16_), channel_id=1, source_target_pairs={{0,1},{1,2},{2,3},{3,4},{4,5},{5,6},{6,7},{7,0},{8,9},{9,10},{10,1... | collective-permute-start | bytes 1572872 | tf_op jit(solution)/shard_map/ppermute | solution.py:28
  44.7 21.7 %collective-permute-start.21 = (bf16[2,4,128,512]{3,2,1,0:T(8,128)(2,1)S(1)}, bf16[2,4,128,512]{3,2,1,0:T(8,128)(2,1)S(1)}, u32[]{:S(2)}, u32[]{:S(2)}) collective-permute-start(bf16[2,4,128,512]{3,2,1,0:T(8,128)(2,1)S(1)} %pad_maximum_fusion.2), channel_id=1, source_target_pairs={{0,32},{1,33},{2,34},{3,35},{4,36},{5,37},{6,38},{7,39},{8,40},{9,... | collective-permute-start | bytes 3145736 | tf_op jit(solution)/shard_map/ppermute | solution.py:28
  47.0 8.3 %collective-permute-start.17 = (bf16[4,128,512]{2,1,0:T(8,128)(2,1)S(1)}, bf16[4,128,512]{2,1,0:T(8,128)(2,1)S(1)}, u32[]{:S(2)}, u32[]{:S(2)}) collective-permute-start(bf16[4,128,512]{2,1,0:T(8,128)(2,1)S(1)} %collective-permute-done.16.refs_9_.refs_19_.refs_17_), channel_id=1, source_target_pairs={{0,1},{1,2},{2,3},{3,4},{4,5},{5,6},{6,7},{7,0},{8,9},{9,10},{10,1... | collective-permute-start | bytes 1572872 | tf_op jit(solution)/shard_map/ppermute | solution.py:28
  47.7 9.2 %collective-permute-start.8 = (bf16[1,2,256,512]{3,2,1,0:T(8,128)(2,1)S(1)}, bf16[1,2,256,512]{3,2,1,0:T(8,128)(2,1)S(1)}, u32[]{:S(2)}, u32[]{:S(2)}) collective-permute-start(bf16[1,2,256,512]{3,2,1,0:T(8,128)(2,1)S(1)} %collective-permute-done.3.refs_3_), channel_id=1, source_target_pairs={{0,24},{1,25},{2,26},{3,27},{4,28},{5,29},{6,30},{7,31},{8,0},{9,1... | collective-permute-start | bytes 1572872 | tf_op jit(solution)/shard_map/ppermute | solution.py:28
  49.6 9.7 %collective-permute-start.22 = (bf16[4,128,512]{2,1,0:T(8,128)(2,1)S(1)}, bf16[4,128,512]{2,1,0:T(8,128)(2,1)S(1)}, u32[]{:S(2)}, u32[]{:S(2)}) collective-permute-start(bf16[4,128,512]{2,1,0:T(8,128)(2,1)S(1)} %all-to-all-done.refs_12_.refs_20_), channel_id=1, source_target_pairs={{0,32},{1,33},{2,34},{3,35},{4,36},{5,37},{6,38},{7,39},{8,40},{9,... | collective-permute-start | bytes 1572872 | tf_op jit(solution)/shard_map/ppermute | solution.py:28
  51.9 17.8 %collective-permute-start.9 = (bf16[2,2,256,512]{3,2,1,0:T(8,128)(2,1)S(1)}, bf16[2,2,256,512]{3,2,1,0:T(8,128)(2,1)S(1)}, u32[]{:S(2)}, u32[]{:S(2)}) collective-permute-start(bf16[2,2,256,512]{3,2,1,0:T(8,128)(2,1)S(1)} %collective-permute-done.4.refs_4_), channel_id=1, source_target_pairs={{0,8},{1,9},{2,10},{3,11},{4,12},{5,13},{6,14},{7,15},{8,16},{9,17... | collective-permute-start | bytes 3145736 | tf_op jit(solution)/shard_map/ppermute | solution.py:28
  55.3 11.1 %collective-permute-start.15 = (bf16[4,128,512]{2,1,0:T(8,128)(2,1)S(1)}, bf16[4,128,512]{2,1,0:T(8,128)(2,1)S(1)}, u32[]{:S(2)}, u32[]{:S(2)}) collective-permute-start(bf16[4,128,512]{2,1,0:T(8,128)(2,1)S(1)} %collective-permute-done.14.refs_10_.refs_20_.refs_18_), channel_id=1, source_target_pairs={{0,1},{1,2},{2,3},{3,4},{4,5},{5,6},{6,7},{7,0},{8,9},{9,10},{10,1... | collective-permute-start | bytes 1572872 | tf_op jit(solution)/shard_map/ppermute | solution.py:28
  57.0 12.6 %collective-permute-start.18 = (bf16[4,128,512]{2,1,0:T(8,128)(2,1)S(1)}, bf16[4,128,512]{2,1,0:T(8,128)(2,1)S(1)}, u32[]{:S(2)}, u32[]{:S(2)}) collective-permute-start(bf16[4,128,512]{2,1,0:T(8,128)(2,1)S(1)} %collective-permute-done.17.refs_11_.refs_21_.refs_19_), channel_id=1, source_target_pairs={{0,1},{1,2},{2,3},{3,4},{4,5},{5,6},{6,7},{7,0},{8,9},{9,10},{10,1... | collective-permute-start | bytes 1572872 | tf_op jit(solution)/shard_map/ppermute | solution.py:28
  59.3 10.4 %collective-permute-start.10 = (bf16[1,2,256,512]{3,2,1,0:T(8,128)(2,1)S(1)}, bf16[1,2,256,512]{3,2,1,0:T(8,128)(2,1)S(1)}, u32[]{:S(2)}, u32[]{:S(2)}) collective-permute-start(bf16[1,2,256,512]{3,2,1,0:T(8,128)(2,1)S(1)} %collective-permute-done.8.refs_8_), channel_id=1, source_target_pairs={{0,24},{1,25},{2,26},{3,27},{4,28},{5,29},{6,30},{7,31},{8,0},{9,1... | collective-permute-start | bytes 1572872 | tf_op jit(solution)/shard_map/ppermute | solution.py:28
  66.4 8.4 %collective-permute-start.11 = (bf16[1,2,256,512]{3,2,1,0:T(8,128)(2,1)S(1)}, bf16[1,2,256,512]{3,2,1,0:T(8,128)(2,1)S(1)}, u32[]{:S(2)}, u32[]{:S(2)}) collective-permute-start(bf16[1,2,256,512]{3,2,1,0:T(8,128)(2,1)S(1)} %collective-permute-done.7.refs_7_), channel_id=1, source_target_pairs={{0,24},{1,25},{2,26},{3,27},{4,28},{5,29},{6,30},{7,31},{8,0},{9,1... | collective-permute-start | bytes 1572872 | tf_op jit(solution)/shard_map/ppermute | solution.py:28
  66.5 9.0 %collective-permute-start.23 = (bf16[2,4,128,512]{3,2,1,0:T(8,128)(2,1)S(1)}, bf16[2,4,128,512]{3,2,1,0:T(8,128)(2,1)S(1)}, u32[]{:S(2)}, u32[]{:S(2)}) collective-permute-start(bf16[2,4,128,512]{3,2,1,0:T(8,128)(2,1)S(1)} %pad_maximum_fusion.1), channel_id=1, source_target_pairs={{0,32},{1,33},{2,34},{3,35},{4,36},{5,37},{6,38},{7,39},{8,40},{9,... | collective-permute-start | bytes 3145736 | tf_op jit(solution)/shard_map/ppermute | solution.py:28
  69.7 14.6 %collective-permute-start.19 = (bf16[2,4,128,512]{3,2,1,0:T(8,128)(2,1)S(1)}, bf16[2,4,128,512]{3,2,1,0:T(8,128)(2,1)S(1)}, u32[]{:S(2)}, u32[]{:S(2)}) collective-permute-start(bf16[2,4,128,512]{3,2,1,0:T(8,128)(2,1)S(1)} %pad_maximum_fusion), channel_id=1, source_target_pairs={{0,32},{1,33},{2,34},{3,35},{4,36},{5,37},{6,38},{7,39},{8,40},{9,... | collective-permute-start | bytes 3145736 | tf_op jit(solution)/shard_map/ppermute | solution.py:28
  74.7 9.5 %collective-permute-start.12 = (bf16[1,2,256,512]{3,2,1,0:T(8,128)(2,1)S(1)}, bf16[1,2,256,512]{3,2,1,0:T(8,128)(2,1)S(1)}, u32[]{:S(2)}, u32[]{:S(2)}) collective-permute-start(bf16[1,2,256,512]{3,2,1,0:T(8,128)(2,1)S(1)} %collective-permute-done.3.refs_3_), channel_id=1, source_target_pairs={{0,8},{1,9},{2,10},{3,11},{4,12},{5,13},{6,14},{7,15},{8,16},{9,17... | collective-permute-start | bytes 1572872 | tf_op jit(solution)/shard_map/ppermute | solution.py:28
  74.8 9.5 %collective-permute-start.20 = (bf16[4,128,512]{2,1,0:T(8,128)(2,1)S(1)}, bf16[4,128,512]{2,1,0:T(8,128)(2,1)S(1)}, u32[]{:S(2)}, u32[]{:S(2)}) collective-permute-start(bf16[4,128,512]{2,1,0:T(8,128)(2,1)S(1)} %collective-permute-done.15.refs_14_.refs_22_), channel_id=1, source_target_pairs={{0,1},{1,2},{2,3},{3,4},{4,5},{5,6},{6,7},{7,0},{8,9},{9,10},{10,1... | collective-permute-start | bytes 1572872 | tf_op jit(solution)/shard_map/ppermute | solution.py:28
  84.3 4.0 %collective-permute-start.24 = (bf16[4,128,512]{2,1,0:T(8,128)(2,1)S(1)}, bf16[4,128,512]{2,1,0:T(8,128)(2,1)S(1)}, u32[]{:S(2)}, u32[]{:S(2)}) collective-permute-start(bf16[4,128,512]{2,1,0:T(8,128)(2,1)S(1)} %collective-permute-done.20.refs_14_), channel_id=1, source_target_pairs={{0,32},{1,33},{2,34},{3,35},{4,36},{5,37},{6,38},{7,39},{8,40},{9,... | collective-permute-start | bytes 1572872 | tf_op jit(solution)/shard_map/ppermute | solution.py:28

commit v5 on v4

--- a/solution.py
+++ b/solution.py
@@ -100,15 +100,15 @@
     ("sF-", ()),
     ("gP", ()),
     ("A3", ("sP+", "sP-", "ff")),
-    ("B3", ("sF-",)),
-    ("B0", ("A1",)),
+    ("B3", ()),
+    ("B0", ("B2",)),
     ("c1", ()),
     ("gF", ()),
     ("sF+", ()),
     ("gU", ()),
-    ("c2", ("c1", "B0")),
-    ("A4", ("gU",)),
-    ("c3", ("gP", "gF", "sum1")),
+    ("c2", ("gU",)),
+    ("A4", ("sF-",)),
+    ("c3", ("gP", "gF", "sum1", "c1")),
     ("c4", ("sF+", "c2", "c3", "sum2")),
 )
 

time: 108 us -> 103 us (0.954)
  starting transfers between devices: 46.3 us -> 38.1 us
  waiting for transfers between devices: 25.4 us -> 28.9 us
    ppermute x25, starting transfers between devices: 42.8 us -> 34.6 us  [permute(): return lax.ppermute(block, AXES, pairs)]
    ppermute x25, waiting for transfers between devices: 17.8 us -> 21.3 us  [permute(): return lax.ppermute(block, AXES, pairs)]
  transfers between devices with their start and end apart: 26 -> 26, of which waited for: 9 -> 11; matrix products, arithmetic and copies ran while one was open for 0% -> 0% of each run, Pallas kernels for 11% -> 12%
where the time goes in v5:
time: 103 us
  starting transfers between devices  38.1 us (37%)
  waiting for transfers between devices  28.9 us (28%)
  Pallas kernels  19.4 us (19%)
  blocking collectives  11.7 us (11%)
  local copies, waits for them, and re-layouts  3.88 us (4%)
    ppermute x25, starting transfers between devices, permute(): return lax.ppermute(block, AXES, pairs)  34.6 us
    ppermute x25, waiting for transfers between devices, permute(): return lax.ppermute(block, AXES, pairs)  21.3 us
    pallas_call x3, Pallas kernels, run_stage(): pl.pallas_call(kernel, out_shape=result if last else total, in_specs=[SME...  18 us
    all_to_all x1, blocking collectives, body(): lax.all_to_all(pooled, ('z', 'c'), split_axis=0, concat_axis=0, tiled=True)  11.7 us
    all_to_all x1, waiting for transfers between devices, piece(): got['A0'] = lax.all_to_all(blocks, 'x', split_axis=0, concat_axis=0)  7.59 us
    all_to_all x1, starting transfers between devices, piece(): got['A0'] = lax.all_to_all(blocks, 'x', split_axis=0, concat_axis=0)  3.47 us
    unnamed x9, local copies, waits for them, and re-layouts  2.99 us
  transfers between devices with their start and end apart: 26, of which 11 were waited for; matrix products, arithmetic and copies ran while one was open for 0% of the time, Pallas kernels for 12%

profile of v5, /device:TPU:1, one launch (start us, length us, event | category | flops | bytes accessed | tf_op | source)
XLA Modules:
  0.0 102.7 jit_solution(8542478632395515481)
XLA Ops:
  0.1 1.0 %copy-done = bf16[512,512]{1,0:T(8,128)(2,1)S(1)} copy-done((bf16[512,512]{1,0:T(8,128)(2,1)S(1)}, bf16[512,512]{1,0:T(8,128)(2,1)}, u32[]{:S(2)}) %copy-start) | copy-done | bytes 524312
  1.1 1.0 %copy-done.1 = bf16[128,2048]{1,0:T(8,128)(2,1)S(1)} copy-done((bf16[128,2048]{1,0:T(8,128)(2,1)S(1)}, bf16[128,2048]{1,0:T(8,128)(2,1)}, u32[]{:S(2)}) %copy-start.1) | copy-done | bytes 524312
  2.8 1.4 %shard_map.37 = (bf16[256,512]{1,0:T(8,128)(2,1)S(1)}, bf16[256,512]{1,0:T(8,128)(2,1)S(1)}, bf16[4,128,512]{2,1,0:T(8,128)(2,1)}) custom-call(s32[4]{0:T(128)S(1)} %pad_add_fusion.place.refs_0_, s32[8]{0:T(128)S(1)} %copy-done.2, bf16[512,512]{1,0:T(8,128)(2,1)S(1)} %copy-done, bf16[128,2048]{1,0:T(8,128)(2,1)S(1)} %copy-done.1), custom_call_target="tpu_custom_call" | custom-call | tf_op jit(solution)/shard_map/pallas_call | solution.py:78
  4.3 3.2 %collective-permute-start = (bf16[256,512]{1,0:T(8,128)(2,1)S(1)}, bf16[256,512]{1,0:T(8,128)(2,1)S(1)}, u32[]{:S(2)}, u32[]{:S(2)}) collective-permute-start(bf16[256,512]{1,0:T(8,128)(2,1)S(1)} %get-tuple-element.17), channel_id=1, source_target_pairs={{0,32},{1,33},{2,34},{3,35},{4,36},{5,37},{6,38},{7,39},{8,40},{9,... | collective-permute-start | bytes 786440 | tf_op jit(solution)/shard_map/ppermute | solution.py:28
  7.5 1.2 %collective-permute-done = bf16[256,512]{1,0:T(8,128)(2,1)S(1)} collective-permute-done((bf16[256,512]{1,0:T(8,128)(2,1)S(1)}, bf16[256,512]{1,0:T(8,128)(2,1)S(1)}, u32[]{:S(2)}, u32[]{:S(2)}) %collective-permute-start) | collective-permute-done | bytes 262176 | tf_op jit(solution)/shard_map/ppermute | solution.py:28
  8.8 2.7 %collective-permute-start.2 = (bf16[1,2,256,512]{3,2,1,0:T(8,128)(2,1)S(1)}, bf16[1,2,256,512]{3,2,1,0:T(8,128)(2,1)S(1)}, u32[]{:S(2)}, u32[]{:S(2)}) collective-permute-start(bf16[1,2,256,512]{3,2,1,0:T(8,128)(2,1)S(1)} %maximum_bitcast_fusion.refs_1_), channel_id=1, source_target_pairs={{0,192},{1,193},{2,194},{3,195},{4,196},{5,197},{6,198},{7,199},{8... | collective-permute-start | bytes 1572872 | tf_op jit(solution)/shard_map/ppermute | solution.py:28
  11.5 3.5 %all-to-all-start = ((bf16[4,128,512]{2,1,0:T(8,128)(2,1)}), bf16[4,128,512]{2,1,0:T(8,128)(2,1)S(1)}, u32[]{:S(2)}, u32[]{:S(2)}) async-start(bf16[4,128,512]{2,1,0:T(8,128)(2,1)} %get-tuple-element.18), calls=%async_computation | async-start | bytes 1048576 | tf_op jit(solution)/shard_map/all_to_all | solution.py:131
  14.9 1.1 %collective-permute-start.7 = (bf16[1,2,256,512]{3,2,1,0:T(8,128)(2,1)S(1)}, bf16[1,2,256,512]{3,2,1,0:T(8,128)(2,1)S(1)}, u32[]{:S(2)}, u32[]{:S(2)}) collective-permute-start(bf16[1,2,256,512]{3,2,1,0:T(8,128)(2,1)S(1)} %maximum_bitcast_fusion.refs_1_), channel_id=1, source_target_pairs={{0,24},{1,25},{2,26},{3,27},{4,28},{5,29},{6,30},{7,31},{8,0},{9,1... | collective-permute-start | bytes 1572872 | tf_op jit(solution)/shard_map/ppermute | solution.py:28
  16.5 7.6 %all-to-all-done.refs_12_.refs_20_ = bf16[4,128,512]{2,1,0:T(8,128)(2,1)S(1)} async-done(((bf16[4,128,512]{2,1,0:T(8,128)(2,1)}), bf16[4,128,512]{2,1,0:T(8,128)(2,1)S(1)}, u32[]{:S(2)}, u32[]{:S(2)}) %all-to-all-start) | async-done | bytes 524320 | tf_op jit(solution)/shard_map/all_to_all | solution.py:131
  24.1 2.1 %collective-permute-start.13 = (bf16[4,128,512]{2,1,0:T(8,128)(2,1)S(1)}, bf16[4,128,512]{2,1,0:T(8,128)(2,1)S(1)}, u32[]{:S(2)}, u32[]{:S(2)}) collective-permute-start(bf16[4,128,512]{2,1,0:T(8,128)(2,1)S(1)} %all-to-all-done.refs_12_.refs_20_), channel_id=1, source_target_pairs={{0,1},{1,2},{2,3},{3,4},{4,5},{5,6},{6,7},{7,0},{8,9},{9,10},{10,1... | collective-permute-start | bytes 1572872 | tf_op jit(solution)/shard_map/ppermute | solution.py:28
  26.3 3.1 %collective-permute-start.4 = (bf16[2,2,256,512]{3,2,1,0:T(8,128)(2,1)S(1)}, bf16[2,2,256,512]{3,2,1,0:T(8,128)(2,1)S(1)}, u32[]{:S(2)}, u32[]{:S(2)}) collective-permute-start(bf16[2,2,256,512]{3,2,1,0:T(8,128)(2,1)S(1)} %constant_dynamic-update-slice_fusion.refs_2_), channel_id=1, source_target_pairs={{0,8},{1,9},{2,10},{3,11},{4,12},{5,13},{6,14},{7,15},{8,16},{9,17... | collective-permute-start | bytes 3145736 | tf_op jit(solution)/shard_map/ppermute | solution.py:28
  29.4 1.5 %collective-permute-start.5 = (bf16[2,2,256,512]{3,2,1,0:T(8,128)(2,1)S(1)}, bf16[2,2,256,512]{3,2,1,0:T(8,128)(2,1)S(1)}, u32[]{:S(2)}, u32[]{:S(2)}) collective-permute-start(bf16[2,2,256,512]{3,2,1,0:T(8,128)(2,1)S(1)} %constant_dynamic-update-slice_fusion.refs_2_), channel_id=1, source_target_pairs={{0,24},{1,25},{2,26},{3,27},{4,28},{5,29},{6,30},{7,31},{8,0},{9,1... | collective-permute-start | bytes 3145736 | tf_op jit(solution)/shard_map/ppermute | solution.py:28
  30.9 1.3 %collective-permute-start.3 = (bf16[1,2,256,512]{3,2,1,0:T(8,128)(2,1)S(1)}, bf16[1,2,256,512]{3,2,1,0:T(8,128)(2,1)S(1)}, u32[]{:S(2)}, u32[]{:S(2)}) collective-permute-start(bf16[1,2,256,512]{3,2,1,0:T(8,128)(2,1)S(1)} %collective-permute-done.1), channel_id=1, source_target_pairs={{0,64},{1,65},{2,66},{3,67},{4,68},{5,69},{6,70},{7,71},{8,72},{9,... | collective-permute-start | bytes 1572872 | tf_op jit(solution)/shard_map/ppermute | solution.py:28
  32.4 3.3 %collective-permute-start.14 = (bf16[4,128,512]{2,1,0:T(8,128)(2,1)S(1)}, bf16[4,128,512]{2,1,0:T(8,128)(2,1)S(1)}, u32[]{:S(2)}, u32[]{:S(2)}) collective-permute-start(bf16[4,128,512]{2,1,0:T(8,128)(2,1)S(1)} %collective-permute-done.13.refs_8_.refs_18_.refs_16_), channel_id=1, source_target_pairs={{0,1},{1,2},{2,3},{3,4},{4,5},{5,6},{6,7},{7,0},{8,9},{9,10},{10,1... | collective-permute-start | bytes 1572872 | tf_op jit(solution)/shard_map/ppermute | solution.py:28
  35.7 8.8 %collective-permute-done.16.refs_9_.refs_19_.refs_17_ = bf16[4,128,512]{2,1,0:T(8,128)(2,1)S(1)} collective-permute-done((bf16[4,128,512]{2,1,0:T(8,128)(2,1)S(1)}, bf16[4,128,512]{2,1,0:T(8,128)(2,1)S(1)}, u32[]{:S(2)}, u32[]{:S(2)}) %collective-permute-start.16) | collective-permute-done | bytes 524320 | tf_op jit(solution)/shard_map/ppermute | solution.py:28
  44.6 2.5 %collective-permute-done.3.refs_3_ = bf16[1,2,256,512]{3,2,1,0:T(8,128)(2,1)S(1)} collective-permute-done((bf16[1,2,256,512]{3,2,1,0:T(8,128)(2,1)S(1)}, bf16[1,2,256,512]{3,2,1,0:T(8,128)(2,1)S(1)}, u32[]{:S(2)}, u32[]{:S(2)}) %collective-permute-start.3) | collective-permute-done | bytes 524320 | tf_op jit(solution)/shard_map/ppermute | solution.py:28
  47.9 2.2 %collective-permute-start.19 = (bf16[2,4,128,512]{3,2,1,0:T(8,128)(2,1)S(1)}, bf16[2,4,128,512]{3,2,1,0:T(8,128)(2,1)S(1)}, u32[]{:S(2)}, u32[]{:S(2)}) collective-permute-start(bf16[2,4,128,512]{3,2,1,0:T(8,128)(2,1)S(1)} %pad_maximum_fusion.1), channel_id=1, source_target_pairs={{0,32},{1,33},{2,34},{3,35},{4,36},{5,37},{6,38},{7,39},{8,40},{9,... | collective-permute-start | bytes 3145736 | tf_op jit(solution)/shard_map/ppermute | solution.py:28
  50.1 3.2 %collective-permute-start.8 = (bf16[1,2,256,512]{3,2,1,0:T(8,128)(2,1)S(1)}, bf16[1,2,256,512]{3,2,1,0:T(8,128)(2,1)S(1)}, u32[]{:S(2)}, u32[]{:S(2)}) collective-permute-start(bf16[1,2,256,512]{3,2,1,0:T(8,128)(2,1)S(1)} %collective-permute-done.3.refs_3_), channel_id=1, source_target_pairs={{0,24},{1,25},{2,26},{3,27},{4,28},{5,29},{6,30},{7,31},{8,0},{9,1... | collective-permute-start | bytes 1572872 | tf_op jit(solution)/shard_map/ppermute | solution.py:28
  53.7 1.6 %collective-permute-done.17.refs_11_.refs_21_.refs_19_ = bf16[4,128,512]{2,1,0:T(8,128)(2,1)S(1)} collective-permute-done((bf16[4,128,512]{2,1,0:T(8,128)(2,1)S(1)}, bf16[4,128,512]{2,1,0:T(8,128)(2,1)S(1)}, u32[]{:S(2)}, u32[]{:S(2)}) %collective-permute-start.17) | collective-permute-done | bytes 524320 | tf_op jit(solution)/shard_map/ppermute | solution.py:28
  55.3 1.6 %collective-permute-start.18 = (bf16[4,128,512]{2,1,0:T(8,128)(2,1)S(1)}, bf16[4,128,512]{2,1,0:T(8,128)(2,1)S(1)}, u32[]{:S(2)}, u32[]{:S(2)}) collective-permute-start(bf16[4,128,512]{2,1,0:T(8,128)(2,1)S(1)} %collective-permute-done.17.refs_11_.refs_21_.refs_19_), channel_id=1, source_target_pairs={{0,1},{1,2},{2,3},{3,4},{4,5},{5,6},{6,7},{7,0},{8,9},{9,10},{10,1... | collective-permute-start | bytes 1572872 | tf_op jit(solution)/shard_map/ppermute | solution.py:28
  57.0 2.4 %collective-permute-done.8.refs_8_ = bf16[1,2,256,512]{3,2,1,0:T(8,128)(2,1)S(1)} collective-permute-done((bf16[1,2,256,512]{3,2,1,0:T(8,128)(2,1)S(1)}, bf16[1,2,256,512]{3,2,1,0:T(8,128)(2,1)S(1)}, u32[]{:S(2)}, u32[]{:S(2)}) %collective-permute-start.8) | collective-permute-done | bytes 524320 | tf_op jit(solution)/shard_map/ppermute | solution.py:28
  59.4 3.4 %collective-permute-start.10 = (bf16[1,2,256,512]{3,2,1,0:T(8,128)(2,1)S(1)}, bf16[1,2,256,512]{3,2,1,0:T(8,128)(2,1)S(1)}, u32[]{:S(2)}, u32[]{:S(2)}) collective-permute-start(bf16[1,2,256,512]{3,2,1,0:T(8,128)(2,1)S(1)} %collective-permute-done.8.refs_8_), channel_id=1, source_target_pairs={{0,24},{1,25},{2,26},{3,27},{4,28},{5,29},{6,30},{7,31},{8,0},{9,1... | collective-permute-start | bytes 1572872 | tf_op jit(solution)/shard_map/ppermute | solution.py:28
  62.9 3.5 %shard_map.38.refs_22_ = f32[2,4,256,512]{3,2,1,0:T(8,128)S(1)} custom-call(s32[4]{0:T(128)S(1)} %pad_add_fusion.place.refs_0_, bf16[1,2,256,512]{3,2,1,0:T(8,128)(2,1)S(1)} %maximum_bitcast_fusion.refs_1_, bf16[2,2,256,512]{3,2,1,0:T(8,128)(2,1)S(1)} %constant_dynamic-update-slice_fusion.refs_2_, ...), custom_call_target="tpu_custom_call" | custom-call | tf_op jit(solution)/shard_map/pallas_call | solution.py:270
  66.6 0.9 collective-permute-done.18.refs_15_.refs_23_
  67.6 1.3 %collective-permute-done.10.refs_10_ = bf16[1,2,256,512]{3,2,1,0:T(8,128)(2,1)S(1)} collective-permute-done((bf16[1,2,256,512]{3,2,1,0:T(8,128)(2,1)S(1)}, bf16[1,2,256,512]{3,2,1,0:T(8,128)(2,1)S(1)}, u32[]{:S(2)}, u32[]{:S(2)}) %collective-permute-start.10) | collective-permute-done | bytes 524320 | tf_op jit(solution)/shard_map/ppermute | solution.py:28
  69.0 1.0 collective-permute-start.20
  70.2 1.3 %collective-permute-start.23 = (bf16[4,128,512]{2,1,0:T(8,128)(2,1)S(1)}, bf16[4,128,512]{2,1,0:T(8,128)(2,1)S(1)}, u32[]{:S(2)}, u32[]{:S(2)}) collective-permute-start(bf16[4,128,512]{2,1,0:T(8,128)(2,1)S(1)} %all-to-all-done.refs_12_.refs_20_), channel_id=1, source_target_pairs={{0,32},{1,33},{2,34},{3,35},{4,36},{5,37},{6,38},{7,39},{8,40},{9,... | collective-permute-start | bytes 1572872 | tf_op jit(solution)/shard_map/ppermute | solution.py:28
  72.3 0.8 collective-permute-done.23.refs_13_.refs_21_
  73.1 8.3 %shard_map.39.refs_26_ = f32[2,4,256,512]{3,2,1,0:T(8,128)S(1)} custom-call(s32[4]{0:T(128)S(1)} %pad_add_fusion.place.refs_0_, bf16[1,2,256,512]{3,2,1,0:T(8,128)(2,1)S(1)} %maximum_bitcast_fusion.refs_1_, bf16[2,2,256,512]{3,2,1,0:T(8,128)(2,1)S(1)} %constant_dynamic-update-slice_fusion.refs_2_, ...), custom_call_target="tpu_custom_call", output_to_operand_aliasing={{}: (22, {})} | custom-call | tf_op jit(solution)/shard_map/pallas_call | solution.py:270
  82.0 1.6 %collective-permute-done.24.refs_15_ = bf16[4,128,512]{2,1,0:T(8,128)(2,1)S(1)} collective-permute-done((bf16[4,128,512]{2,1,0:T(8,128)(2,1)S(1)}, bf16[4,128,512]{2,1,0:T(8,128)(2,1)S(1)}, u32[]{:S(2)}, u32[]{:S(2)}) %collective-permute-start.24) | collective-permute-done | bytes 524320 | tf_op jit(solution)/shard_map/ppermute | solution.py:28
  83.6 6.1 %shard_map.40 = f32[2,4,4,512]{3,2,1,0:T(4,128)S(1)} custom-call(s32[4]{0:T(128)S(1)} %pad_add_fusion.place.refs_0_, bf16[1,2,256,512]{3,2,1,0:T(8,128)(2,1)S(1)} %maximum_bitcast_fusion.refs_1_, bf16[2,2,256,512]{3,2,1,0:T(8,128)(2,1)S(1)} %constant_dynamic-update-slice_fusion.refs_2_, bf16[1,2,256,512]{3,2,1,0:T(8,128)(2,1)S(1)} %collective-permute-done.3.refs_3_, ...), custom_call_target="tpu_custom_call" | custom-call | tf_op jit(solution)/shard_map/pallas_call | solution.py:270
  90.0 11.7 %all_to_all.10 = bf16[16,2,512]{2,1,0:T(2,128)(2,1)S(1)} all-to-all(bf16[16,2,512]{2,1,0:T(2,128)(2,1)S(1)} %reshape.20), channel_id=1, replica_groups=mesh['y'=4,'c'=2,'x'=4,'z'=8] {'z','c'}, dimensions={0} | all-to-all | bytes 65536 | tf_op jit(solution)/shard_map/all_to_all | solution.py:288
  (48 shorter events, 6.0 us)
Async XLA Ops:
  0.1 1.0 %copy-start = (bf16[512,512]{1,0:T(8,128)(2,1)S(1)}, bf16[512,512]{1,0:T(8,128)(2,1)}, u32[]{:S(2)}) copy-start(bf16[512,512]{1,0:T(8,128)(2,1)} %hid.1) | copy-start | bytes 1572868
  1.1 1.0 %copy-start.1 = (bf16[128,2048]{1,0:T(8,128)(2,1)S(1)}, bf16[128,2048]{1,0:T(8,128)(2,1)}, u32[]{:S(2)}) copy-start(bf16[128,2048]{1,0:T(8,128)(2,1)} %head.1) | copy-start | bytes 1572868
  2.2 0.7 copy-start.2
  4.3 4.4 %collective-permute-start = (bf16[256,512]{1,0:T(8,128)(2,1)S(1)}, bf16[256,512]{1,0:T(8,128)(2,1)S(1)}, u32[]{:S(2)}, u32[]{:S(2)}) collective-permute-start(bf16[256,512]{1,0:T(8,128)(2,1)S(1)} %get-tuple-element.17), channel_id=1, source_target_pairs={{0,32},{1,33},{2,34},{3,35},{4,36},{5,37},{6,38},{7,39},{8,40},{9,... | collective-permute-start | bytes 786440 | tf_op jit(solution)/shard_map/ppermute | solution.py:28
  8.7 15.4 %collective-permute-start.1 = (bf16[1,2,256,512]{3,2,1,0:T(8,128)(2,1)S(1)}, bf16[1,2,256,512]{3,2,1,0:T(8,128)(2,1)S(1)}, u32[]{:S(2)}, u32[]{:S(2)}) collective-permute-start(bf16[1,2,256,512]{3,2,1,0:T(8,128)(2,1)S(1)} %maximum_bitcast_fusion.refs_1_), channel_id=1, source_target_pairs={{0,64},{1,65},{2,66},{3,67},{4,68},{5,69},{6,70},{7,71},{8,72},{9,... | collective-permute-start | bytes 1572872 | tf_op jit(solution)/shard_map/ppermute | solution.py:28
  8.8 15.3 %collective-permute-start.2 = (bf16[1,2,256,512]{3,2,1,0:T(8,128)(2,1)S(1)}, bf16[1,2,256,512]{3,2,1,0:T(8,128)(2,1)S(1)}, u32[]{:S(2)}, u32[]{:S(2)}) collective-permute-start(bf16[1,2,256,512]{3,2,1,0:T(8,128)(2,1)S(1)} %maximum_bitcast_fusion.refs_1_), channel_id=1, source_target_pairs={{0,192},{1,193},{2,194},{3,195},{4,196},{5,197},{6,198},{7,199},{8... | collective-permute-start | bytes 1572872 | tf_op jit(solution)/shard_map/ppermute | solution.py:28
  11.5 12.6 %all-to-all-start = ((bf16[4,128,512]{2,1,0:T(8,128)(2,1)}), bf16[4,128,512]{2,1,0:T(8,128)(2,1)S(1)}, u32[]{:S(2)}, u32[]{:S(2)}) async-start(bf16[4,128,512]{2,1,0:T(8,128)(2,1)} %get-tuple-element.18), calls=%async_computation | async-start | bytes 1048576 | tf_op jit(solution)/shard_map/all_to_all | solution.py:131
  14.9 16.0 %collective-permute-start.7 = (bf16[1,2,256,512]{3,2,1,0:T(8,128)(2,1)S(1)}, bf16[1,2,256,512]{3,2,1,0:T(8,128)(2,1)S(1)}, u32[]{:S(2)}, u32[]{:S(2)}) collective-permute-start(bf16[1,2,256,512]{3,2,1,0:T(8,128)(2,1)S(1)} %maximum_bitcast_fusion.refs_1_), channel_id=1, source_target_pairs={{0,24},{1,25},{2,26},{3,27},{4,28},{5,29},{6,30},{7,31},{8,0},{9,1... | collective-permute-start | bytes 1572872 | tf_op jit(solution)/shard_map/ppermute | solution.py:28
  16.0 14.9 %collective-permute-start.6 = (bf16[1,2,256,512]{3,2,1,0:T(8,128)(2,1)S(1)}, bf16[1,2,256,512]{3,2,1,0:T(8,128)(2,1)S(1)}, u32[]{:S(2)}, u32[]{:S(2)}) collective-permute-start(bf16[1,2,256,512]{3,2,1,0:T(8,128)(2,1)S(1)} %maximum_bitcast_fusion.refs_1_), channel_id=1, source_target_pairs={{0,8},{1,9},{2,10},{3,11},{4,12},{5,13},{6,14},{7,15},{8,16},{9,17... | collective-permute-start | bytes 1572872 | tf_op jit(solution)/shard_map/ppermute | solution.py:28
  24.1 8.3 %collective-permute-start.13 = (bf16[4,128,512]{2,1,0:T(8,128)(2,1)S(1)}, bf16[4,128,512]{2,1,0:T(8,128)(2,1)S(1)}, u32[]{:S(2)}, u32[]{:S(2)}) collective-permute-start(bf16[4,128,512]{2,1,0:T(8,128)(2,1)S(1)} %all-to-all-done.refs_12_.refs_20_), channel_id=1, source_target_pairs={{0,1},{1,2},{2,3},{3,4},{4,5},{5,6},{6,7},{7,0},{8,9},{9,10},{10,1... | collective-permute-start | bytes 1572872 | tf_op jit(solution)/shard_map/ppermute | solution.py:28
  26.3 23.8 %collective-permute-start.4 = (bf16[2,2,256,512]{3,2,1,0:T(8,128)(2,1)S(1)}, bf16[2,2,256,512]{3,2,1,0:T(8,128)(2,1)S(1)}, u32[]{:S(2)}, u32[]{:S(2)}) collective-permute-start(bf16[2,2,256,512]{3,2,1,0:T(8,128)(2,1)S(1)} %constant_dynamic-update-slice_fusion.refs_2_), channel_id=1, source_target_pairs={{0,8},{1,9},{2,10},{3,11},{4,12},{5,13},{6,14},{7,15},{8,16},{9,17... | collective-permute-start | bytes 3145736 | tf_op jit(solution)/shard_map/ppermute | solution.py:28
  29.4 23.9 %collective-permute-start.5 = (bf16[2,2,256,512]{3,2,1,0:T(8,128)(2,1)S(1)}, bf16[2,2,256,512]{3,2,1,0:T(8,128)(2,1)S(1)}, u32[]{:S(2)}, u32[]{:S(2)}) collective-permute-start(bf16[2,2,256,512]{3,2,1,0:T(8,128)(2,1)S(1)} %constant_dynamic-update-slice_fusion.refs_2_), channel_id=1, source_target_pairs={{0,24},{1,25},{2,26},{3,27},{4,28},{5,29},{6,30},{7,31},{8,0},{9,1... | collective-permute-start | bytes 3145736 | tf_op jit(solution)/shard_map/ppermute | solution.py:28
  30.9 13.6 %collective-permute-start.16 = (bf16[4,128,512]{2,1,0:T(8,128)(2,1)S(1)}, bf16[4,128,512]{2,1,0:T(8,128)(2,1)S(1)}, u32[]{:S(2)}, u32[]{:S(2)}) collective-permute-start(bf16[4,128,512]{2,1,0:T(8,128)(2,1)S(1)} %all-to-all-done.refs_12_.refs_20_), channel_id=1, source_target_pairs={{0,39},{1,32},{2,33},{3,34},{4,35},{5,36},{6,37},{7,38},{8,47},{9,... | collective-permute-start | bytes 1572872 | tf_op jit(solution)/shard_map/ppermute | solution.py:28
  30.9 16.1 %collective-permute-start.3 = (bf16[1,2,256,512]{3,2,1,0:T(8,128)(2,1)S(1)}, bf16[1,2,256,512]{3,2,1,0:T(8,128)(2,1)S(1)}, u32[]{:S(2)}, u32[]{:S(2)}) collective-permute-start(bf16[1,2,256,512]{3,2,1,0:T(8,128)(2,1)S(1)} %collective-permute-done.1), channel_id=1, source_target_pairs={{0,64},{1,65},{2,66},{3,67},{4,68},{5,69},{6,70},{7,71},{8,72},{9,... | collective-permute-start | bytes 1572872 | tf_op jit(solution)/shard_map/ppermute | solution.py:28
  32.4 15.4 %collective-permute-start.14 = (bf16[4,128,512]{2,1,0:T(8,128)(2,1)S(1)}, bf16[4,128,512]{2,1,0:T(8,128)(2,1)S(1)}, u32[]{:S(2)}, u32[]{:S(2)}) collective-permute-start(bf16[4,128,512]{2,1,0:T(8,128)(2,1)S(1)} %collective-permute-done.13.refs_8_.refs_18_.refs_16_), channel_id=1, source_target_pairs={{0,1},{1,2},{2,3},{3,4},{4,5},{5,6},{6,7},{7,0},{8,9},{9,10},{10,1... | collective-permute-start | bytes 1572872 | tf_op jit(solution)/shard_map/ppermute | solution.py:28
  44.6 8.7 %collective-permute-start.11 = (bf16[1,2,256,512]{3,2,1,0:T(8,128)(2,1)S(1)}, bf16[1,2,256,512]{3,2,1,0:T(8,128)(2,1)S(1)}, u32[]{:S(2)}, u32[]{:S(2)}) collective-permute-start(bf16[1,2,256,512]{3,2,1,0:T(8,128)(2,1)S(1)} %collective-permute-done.7.refs_7_), channel_id=1, source_target_pairs={{0,24},{1,25},{2,26},{3,27},{4,28},{5,29},{6,30},{7,31},{8,0},{9,1... | collective-permute-start | bytes 1572872 | tf_op jit(solution)/shard_map/ppermute | solution.py:28
  47.0 8.3 %collective-permute-start.17 = (bf16[4,128,512]{2,1,0:T(8,128)(2,1)S(1)}, bf16[4,128,512]{2,1,0:T(8,128)(2,1)S(1)}, u32[]{:S(2)}, u32[]{:S(2)}) collective-permute-start(bf16[4,128,512]{2,1,0:T(8,128)(2,1)S(1)} %collective-permute-done.16.refs_9_.refs_19_.refs_17_), channel_id=1, source_target_pairs={{0,1},{1,2},{2,3},{3,4},{4,5},{5,6},{6,7},{7,0},{8,9},{9,10},{10,1... | collective-permute-start | bytes 1572872 | tf_op jit(solution)/shard_map/ppermute | solution.py:28
  47.9 19.8 %collective-permute-start.19 = (bf16[2,4,128,512]{3,2,1,0:T(8,128)(2,1)S(1)}, bf16[2,4,128,512]{3,2,1,0:T(8,128)(2,1)S(1)}, u32[]{:S(2)}, u32[]{:S(2)}) collective-permute-start(bf16[2,4,128,512]{3,2,1,0:T(8,128)(2,1)S(1)} %pad_maximum_fusion.1), channel_id=1, source_target_pairs={{0,32},{1,33},{2,34},{3,35},{4,36},{5,37},{6,38},{7,39},{8,40},{9,... | collective-permute-start | bytes 3145736 | tf_op jit(solution)/shard_map/ppermute | solution.py:28
  50.1 9.4 %collective-permute-start.8 = (bf16[1,2,256,512]{3,2,1,0:T(8,128)(2,1)S(1)}, bf16[1,2,256,512]{3,2,1,0:T(8,128)(2,1)S(1)}, u32[]{:S(2)}, u32[]{:S(2)}) collective-permute-start(bf16[1,2,256,512]{3,2,1,0:T(8,128)(2,1)S(1)} %collective-permute-done.3.refs_3_), channel_id=1, source_target_pairs={{0,24},{1,25},{2,26},{3,27},{4,28},{5,29},{6,30},{7,31},{8,0},{9,1... | collective-permute-start | bytes 1572872 | tf_op jit(solution)/shard_map/ppermute | solution.py:28
  53.3 15.7 %collective-permute-start.9 = (bf16[2,2,256,512]{3,2,1,0:T(8,128)(2,1)S(1)}, bf16[2,2,256,512]{3,2,1,0:T(8,128)(2,1)S(1)}, u32[]{:S(2)}, u32[]{:S(2)}) collective-permute-start(bf16[2,2,256,512]{3,2,1,0:T(8,128)(2,1)S(1)} %collective-permute-done.4.refs_4_), channel_id=1, source_target_pairs={{0,8},{1,9},{2,10},{3,11},{4,12},{5,13},{6,14},{7,15},{8,16},{9,17... | collective-permute-start | bytes 3145736 | tf_op jit(solution)/shard_map/ppermute | solution.py:28
  53.3 13.2 %collective-permute-start.15 = (bf16[4,128,512]{2,1,0:T(8,128)(2,1)S(1)}, bf16[4,128,512]{2,1,0:T(8,128)(2,1)S(1)}, u32[]{:S(2)}, u32[]{:S(2)}) collective-permute-start(bf16[4,128,512]{2,1,0:T(8,128)(2,1)S(1)} %collective-permute-done.14.refs_10_.refs_20_.refs_18_), channel_id=1, source_target_pairs={{0,1},{1,2},{2,3},{3,4},{4,5},{5,6},{6,7},{7,0},{8,9},{9,10},{10,1... | collective-permute-start | bytes 1572872 | tf_op jit(solution)/shard_map/ppermute | solution.py:28
  55.3 12.2 %collective-permute-start.18 = (bf16[4,128,512]{2,1,0:T(8,128)(2,1)S(1)}, bf16[4,128,512]{2,1,0:T(8,128)(2,1)S(1)}, u32[]{:S(2)}, u32[]{:S(2)}) collective-permute-start(bf16[4,128,512]{2,1,0:T(8,128)(2,1)S(1)} %collective-permute-done.17.refs_11_.refs_21_.refs_19_), channel_id=1, source_target_pairs={{0,1},{1,2},{2,3},{3,4},{4,5},{5,6},{6,7},{7,0},{8,9},{9,10},{10,1... | collective-permute-start | bytes 1572872 | tf_op jit(solution)/shard_map/ppermute | solution.py:28
  59.4 9.5 %collective-permute-start.10 = (bf16[1,2,256,512]{3,2,1,0:T(8,128)(2,1)S(1)}, bf16[1,2,256,512]{3,2,1,0:T(8,128)(2,1)S(1)}, u32[]{:S(2)}, u32[]{:S(2)}) collective-permute-start(bf16[1,2,256,512]{3,2,1,0:T(8,128)(2,1)S(1)} %collective-permute-done.8.refs_8_), channel_id=1, source_target_pairs={{0,24},{1,25},{2,26},{3,27},{4,28},{5,29},{6,30},{7,31},{8,0},{9,1... | collective-permute-start | bytes 1572872 | tf_op jit(solution)/shard_map/ppermute | solution.py:28
  66.5 6.6 %collective-permute-start.22 = (bf16[2,4,128,512]{3,2,1,0:T(8,128)(2,1)S(1)}, bf16[2,4,128,512]{3,2,1,0:T(8,128)(2,1)S(1)}, u32[]{:S(2)}, u32[]{:S(2)}) collective-permute-start(bf16[2,4,128,512]{3,2,1,0:T(8,128)(2,1)S(1)} %pad_maximum_fusion.2), channel_id=1, source_target_pairs={{0,32},{1,33},{2,34},{3,35},{4,36},{5,37},{6,38},{7,39},{8,40},{9,... | collective-permute-start | bytes 3145736 | tf_op jit(solution)/shard_map/ppermute | solution.py:28
  69.0 12.4 %collective-permute-start.20 = (bf16[2,4,128,512]{3,2,1,0:T(8,128)(2,1)S(1)}, bf16[2,4,128,512]{3,2,1,0:T(8,128)(2,1)S(1)}, u32[]{:S(2)}, u32[]{:S(2)}) collective-permute-start(bf16[2,4,128,512]{3,2,1,0:T(8,128)(2,1)S(1)} %pad_maximum_fusion), channel_id=1, source_target_pairs={{0,32},{1,33},{2,34},{3,35},{4,36},{5,37},{6,38},{7,39},{8,40},{9,... | collective-permute-start | bytes 3145736 | tf_op jit(solution)/shard_map/ppermute | solution.py:28
  70.0 11.4 %collective-permute-start.12 = (bf16[1,2,256,512]{3,2,1,0:T(8,128)(2,1)S(1)}, bf16[1,2,256,512]{3,2,1,0:T(8,128)(2,1)S(1)}, u32[]{:S(2)}, u32[]{:S(2)}) collective-permute-start(bf16[1,2,256,512]{3,2,1,0:T(8,128)(2,1)S(1)} %collective-permute-done.3.refs_3_), channel_id=1, source_target_pairs={{0,8},{1,9},{2,10},{3,11},{4,12},{5,13},{6,14},{7,15},{8,16},{9,17... | collective-permute-start | bytes 1572872 | tf_op jit(solution)/shard_map/ppermute | solution.py:28
  70.2 2.9 %collective-permute-start.23 = (bf16[4,128,512]{2,1,0:T(8,128)(2,1)S(1)}, bf16[4,128,512]{2,1,0:T(8,128)(2,1)S(1)}, u32[]{:S(2)}, u32[]{:S(2)}) collective-permute-start(bf16[4,128,512]{2,1,0:T(8,128)(2,1)S(1)} %all-to-all-done.refs_12_.refs_20_), channel_id=1, source_target_pairs={{0,32},{1,33},{2,34},{3,35},{4,36},{5,37},{6,38},{7,39},{8,40},{9,... | collective-permute-start | bytes 1572872 | tf_op jit(solution)/shard_map/ppermute | solution.py:28
  71.5 9.8 %collective-permute-start.21 = (bf16[4,128,512]{2,1,0:T(8,128)(2,1)S(1)}, bf16[4,128,512]{2,1,0:T(8,128)(2,1)S(1)}, u32[]{:S(2)}, u32[]{:S(2)}) collective-permute-start(bf16[4,128,512]{2,1,0:T(8,128)(2,1)S(1)} %collective-permute-done.15.refs_14_.refs_22_), channel_id=1, source_target_pairs={{0,1},{1,2},{2,3},{3,4},{4,5},{5,6},{6,7},{7,0},{8,9},{9,10},{10,1... | collective-permute-start | bytes 1572872 | tf_op jit(solution)/shard_map/ppermute | solution.py:28
  81.4 2.2 %collective-permute-start.24 = (bf16[4,128,512]{2,1,0:T(8,128)(2,1)S(1)}, bf16[4,128,512]{2,1,0:T(8,128)(2,1)S(1)}, u32[]{:S(2)}, u32[]{:S(2)}) collective-permute-start(bf16[4,128,512]{2,1,0:T(8,128)(2,1)S(1)} %collective-permute-done.21.refs_14_), channel_id=1, source_target_pairs={{0,32},{1,33},{2,34},{3,35},{4,36},{5,37},{6,38},{7,39},{8,40},{9,... | collective-permute-start | bytes 1572872 | tf_op jit(solution)/shard_map/ppermute | solution.py:28

commit v6 on v5

--- a/solution.py
+++ b/solution.py
@@ -80,7 +80,6 @@
         out_shape=[half, half, blocks],
         in_specs=[SMEM, SMEM, VMEM, VMEM],
         out_specs=[VMEM] * 3,
-        compiler_params=pltpu.CompilerParams(vmem_limit_bytes=6 << 20),
     )(place, lengths, hidden, head)
 
 
@@ -216,10 +215,10 @@
         ref = arrays[PIECES[step][col]]
         return ref.at[1 - col] if len(ref.shape) == 4 else ref
 
-    if before:
+    if not before:
+        acc[...] = jnp.zeros_like(acc)
+    elif last:
         acc[...] = refs[1 + n][...]
-    else:
-        acc[...] = jnp.zeros_like(acc)
     for name, steps in work:
         ref = arrays[name]
         a, b = STEPS[name]

time: 103 us -> 103 us (level)
  local copies, waits for them, and re-layouts: 3.88 us -> 1.14 us
  other arithmetic: 0.51 us -> 2.03 us
    unnamed x9 -> x5, local copies, waits for them, and re-layouts: 2.99 us -> 0.26 us
  transfers between devices with their start and end apart: 26 -> 26, of which waited for: 11 -> 11; matrix products, arithmetic and copies ran while one was open for 0% -> 0% of each run, Pallas kernels for 12% -> 11%
where the time goes in v6:
time: 103 us; the launch traced here: 102 us
  starting transfers between devices  38.7 us (38%)
  waiting for transfers between devices  29.1 us (28%)
  Pallas kernels  19.3 us (19%)
  blocking collectives  11.9 us (12%)
  other arithmetic  2.03 us (2%)
  local copies, waits for them, and re-layouts  1.14 us (1%)
    ppermute x25, starting transfers between devices, permute(): return lax.ppermute(block, AXES, pairs)  35.3 us
    ppermute x25, waiting for transfers between devices, permute(): return lax.ppermute(block, AXES, pairs)  21.5 us
    pallas_call x3, Pallas kernels, run_stage(): pl.pallas_call(kernel, out_shape=result if last else total, in_specs=[SME...  17.1 us
    all_to_all x1, blocking collectives, body(): lax.all_to_all(pooled, ('z', 'c'), split_axis=0, concat_axis=0, tiled=True)  11.9 us
    all_to_all x1, waiting for transfers between devices, piece(): got['A0'] = lax.all_to_all(blocks, 'x', split_axis=0, concat_axis=0)  7.59 us
    all_to_all x1, starting transfers between devices, piece(): got['A0'] = lax.all_to_all(blocks, 'x', split_axis=0, concat_axis=0)  3.47 us
    pallas_call x1, Pallas kernels, prep(): pl.pallas_call(prep_kernel, out_shape=[half, half, blocks], in_specs=[SME...  2.26 us
  transfers between devices with their start and end apart: 26, of which 11 were waited for; matrix products, arithmetic and copies ran while one was open for 0% of the time, Pallas kernels for 11%

profile of v6, /device:TPU:1, one launch (start us, length us, event | category | flops | bytes accessed | tf_op | source)
XLA Modules:
  0.0 102.4 jit_solution(10845297400062149199)
XLA Ops:
  0.6 2.3 %shard_map.37 = (bf16[256,512]{1,0:T(8,128)(2,1)}, bf16[256,512]{1,0:T(8,128)(2,1)}, bf16[4,128,512]{2,1,0:T(8,128)(2,1)}) custom-call(s32[4]{0:T(128)} %pad_add_fusion.place.refs_0_, s32[8]{0:T(128)} %lengths.1, bf16[512,512]{1,0:T(8,128)(2,1)} %hid.1, bf16[128,2048]{1,0:T(8,128)(2,1)} %head.1), custom_call_target="tpu_custom_call" | custom-call | tf_op jit(solution)/shard_map/pallas_call | solution.py:78
  2.9 3.2 %collective-permute-start = (bf16[256,512]{1,0:T(8,128)(2,1)}, bf16[256,512]{1,0:T(8,128)(2,1)S(1)}, u32[]{:S(2)}, u32[]{:S(2)}) collective-permute-start(bf16[256,512]{1,0:T(8,128)(2,1)} %get-tuple-element.17), channel_id=1, source_target_pairs={{0,32},{1,33},{2,34},{3,35},{4,36},{5,37},{6,38},{7,39},{8,40},{9,... | collective-permute-start | bytes 786440 | tf_op jit(solution)/shard_map/ppermute | solution.py:28
  6.1 1.4 %collective-permute-done = bf16[256,512]{1,0:T(8,128)(2,1)S(1)} collective-permute-done((bf16[256,512]{1,0:T(8,128)(2,1)}, bf16[256,512]{1,0:T(8,128)(2,1)S(1)}, u32[]{:S(2)}, u32[]{:S(2)}) %collective-permute-start) | collective-permute-done | bytes 262176 | tf_op jit(solution)/shard_map/ppermute | solution.py:28
  7.5 1.0 maximum_bitcast_fusion.refs_1_
  8.6 2.7 %collective-permute-start.2 = (bf16[1,2,256,512]{3,2,1,0:T(8,128)(2,1)S(1)}, bf16[1,2,256,512]{3,2,1,0:T(8,128)(2,1)S(1)}, u32[]{:S(2)}, u32[]{:S(2)}) collective-permute-start(bf16[1,2,256,512]{3,2,1,0:T(8,128)(2,1)S(1)} %maximum_bitcast_fusion.refs_1_), channel_id=1, source_target_pairs={{0,192},{1,193},{2,194},{3,195},{4,196},{5,197},{6,198},{7,199},{8... | collective-permute-start | bytes 1572872 | tf_op jit(solution)/shard_map/ppermute | solution.py:28
  11.3 3.5 %all-to-all-start = ((bf16[4,128,512]{2,1,0:T(8,128)(2,1)}), bf16[4,128,512]{2,1,0:T(8,128)(2,1)S(1)}, u32[]{:S(2)}, u32[]{:S(2)}) async-start(bf16[4,128,512]{2,1,0:T(8,128)(2,1)} %get-tuple-element.18), calls=%async_computation | async-start | bytes 1048576 | tf_op jit(solution)/shard_map/all_to_all | solution.py:130
  14.8 1.1 %collective-permute-start.7 = (bf16[1,2,256,512]{3,2,1,0:T(8,128)(2,1)S(1)}, bf16[1,2,256,512]{3,2,1,0:T(8,128)(2,1)S(1)}, u32[]{:S(2)}, u32[]{:S(2)}) collective-permute-start(bf16[1,2,256,512]{3,2,1,0:T(8,128)(2,1)S(1)} %maximum_bitcast_fusion.refs_1_), channel_id=1, source_target_pairs={{0,24},{1,25},{2,26},{3,27},{4,28},{5,29},{6,30},{7,31},{8,0},{9,1... | collective-permute-start | bytes 1572872 | tf_op jit(solution)/shard_map/ppermute | solution.py:28
  16.3 7.6 %all-to-all-done.refs_12_.refs_20_ = bf16[4,128,512]{2,1,0:T(8,128)(2,1)S(1)} async-done(((bf16[4,128,512]{2,1,0:T(8,128)(2,1)}), bf16[4,128,512]{2,1,0:T(8,128)(2,1)S(1)}, u32[]{:S(2)}, u32[]{:S(2)}) %all-to-all-start) | async-done | bytes 524320 | tf_op jit(solution)/shard_map/all_to_all | solution.py:130
  23.9 2.1 %collective-permute-start.13 = (bf16[4,128,512]{2,1,0:T(8,128)(2,1)S(1)}, bf16[4,128,512]{2,1,0:T(8,128)(2,1)S(1)}, u32[]{:S(2)}, u32[]{:S(2)}) collective-permute-start(bf16[4,128,512]{2,1,0:T(8,128)(2,1)S(1)} %all-to-all-done.refs_12_.refs_20_), channel_id=1, source_target_pairs={{0,1},{1,2},{2,3},{3,4},{4,5},{5,6},{6,7},{7,0},{8,9},{9,10},{10,1... | collective-permute-start | bytes 1572872 | tf_op jit(solution)/shard_map/ppermute | solution.py:28
  26.1 3.1 %collective-permute-start.4 = (bf16[2,2,256,512]{3,2,1,0:T(8,128)(2,1)S(1)}, bf16[2,2,256,512]{3,2,1,0:T(8,128)(2,1)S(1)}, u32[]{:S(2)}, u32[]{:S(2)}) collective-permute-start(bf16[2,2,256,512]{3,2,1,0:T(8,128)(2,1)S(1)} %constant_dynamic-update-slice_fusion.refs_2_), channel_id=1, source_target_pairs={{0,8},{1,9},{2,10},{3,11},{4,12},{5,13},{6,14},{7,15},{8,16},{9,17... | collective-permute-start | bytes 3145736 | tf_op jit(solution)/shard_map/ppermute | solution.py:28
  29.2 1.5 %collective-permute-start.5 = (bf16[2,2,256,512]{3,2,1,0:T(8,128)(2,1)S(1)}, bf16[2,2,256,512]{3,2,1,0:T(8,128)(2,1)S(1)}, u32[]{:S(2)}, u32[]{:S(2)}) collective-permute-start(bf16[2,2,256,512]{3,2,1,0:T(8,128)(2,1)S(1)} %constant_dynamic-update-slice_fusion.refs_2_), channel_id=1, source_target_pairs={{0,24},{1,25},{2,26},{3,27},{4,28},{5,29},{6,30},{7,31},{8,0},{9,1... | collective-permute-start | bytes 3145736 | tf_op jit(solution)/shard_map/ppermute | solution.py:28
  30.8 1.3 %collective-permute-start.3 = (bf16[1,2,256,512]{3,2,1,0:T(8,128)(2,1)S(1)}, bf16[1,2,256,512]{3,2,1,0:T(8,128)(2,1)S(1)}, u32[]{:S(2)}, u32[]{:S(2)}) collective-permute-start(bf16[1,2,256,512]{3,2,1,0:T(8,128)(2,1)S(1)} %collective-permute-done.1), channel_id=1, source_target_pairs={{0,64},{1,65},{2,66},{3,67},{4,68},{5,69},{6,70},{7,71},{8,72},{9,... | collective-permute-start | bytes 1572872 | tf_op jit(solution)/shard_map/ppermute | solution.py:28
  32.2 3.3 %collective-permute-start.14 = (bf16[4,128,512]{2,1,0:T(8,128)(2,1)S(1)}, bf16[4,128,512]{2,1,0:T(8,128)(2,1)S(1)}, u32[]{:S(2)}, u32[]{:S(2)}) collective-permute-start(bf16[4,128,512]{2,1,0:T(8,128)(2,1)S(1)} %collective-permute-done.13.refs_8_.refs_18_.refs_16_), channel_id=1, source_target_pairs={{0,1},{1,2},{2,3},{3,4},{4,5},{5,6},{6,7},{7,0},{8,9},{9,10},{10,1... | collective-permute-start | bytes 1572872 | tf_op jit(solution)/shard_map/ppermute | solution.py:28
  35.5 8.8 %collective-permute-done.16.refs_9_.refs_19_.refs_17_ = bf16[4,128,512]{2,1,0:T(8,128)(2,1)S(1)} collective-permute-done((bf16[4,128,512]{2,1,0:T(8,128)(2,1)S(1)}, bf16[4,128,512]{2,1,0:T(8,128)(2,1)S(1)}, u32[]{:S(2)}, u32[]{:S(2)}) %collective-permute-start.16) | collective-permute-done | bytes 524320 | tf_op jit(solution)/shard_map/ppermute | solution.py:28
  44.4 2.5 %collective-permute-done.3.refs_3_ = bf16[1,2,256,512]{3,2,1,0:T(8,128)(2,1)S(1)} collective-permute-done((bf16[1,2,256,512]{3,2,1,0:T(8,128)(2,1)S(1)}, bf16[1,2,256,512]{3,2,1,0:T(8,128)(2,1)S(1)}, u32[]{:S(2)}, u32[]{:S(2)}) %collective-permute-start.3) | collective-permute-done | bytes 524320 | tf_op jit(solution)/shard_map/ppermute | solution.py:28
  47.7 2.2 %collective-permute-start.19 = (bf16[2,4,128,512]{3,2,1,0:T(8,128)(2,1)S(1)}, bf16[2,4,128,512]{3,2,1,0:T(8,128)(2,1)S(1)}, u32[]{:S(2)}, u32[]{:S(2)}) collective-permute-start(bf16[2,4,128,512]{3,2,1,0:T(8,128)(2,1)S(1)} %pad_maximum_fusion.1), channel_id=1, source_target_pairs={{0,32},{1,33},{2,34},{3,35},{4,36},{5,37},{6,38},{7,39},{8,40},{9,... | collective-permute-start | bytes 3145736 | tf_op jit(solution)/shard_map/ppermute | solution.py:28
  49.9 3.2 %collective-permute-start.8 = (bf16[1,2,256,512]{3,2,1,0:T(8,128)(2,1)S(1)}, bf16[1,2,256,512]{3,2,1,0:T(8,128)(2,1)S(1)}, u32[]{:S(2)}, u32[]{:S(2)}) collective-permute-start(bf16[1,2,256,512]{3,2,1,0:T(8,128)(2,1)S(1)} %collective-permute-done.3.refs_3_), channel_id=1, source_target_pairs={{0,24},{1,25},{2,26},{3,27},{4,28},{5,29},{6,30},{7,31},{8,0},{9,1... | collective-permute-start | bytes 1572872 | tf_op jit(solution)/shard_map/ppermute | solution.py:28
  53.5 1.6 %collective-permute-done.17.refs_11_.refs_21_.refs_19_ = bf16[4,128,512]{2,1,0:T(8,128)(2,1)S(1)} collective-permute-done((bf16[4,128,512]{2,1,0:T(8,128)(2,1)S(1)}, bf16[4,128,512]{2,1,0:T(8,128)(2,1)S(1)}, u32[]{:S(2)}, u32[]{:S(2)}) %collective-permute-start.17) | collective-permute-done | bytes 524320 | tf_op jit(solution)/shard_map/ppermute | solution.py:28
  55.2 1.6 %collective-permute-start.18 = (bf16[4,128,512]{2,1,0:T(8,128)(2,1)S(1)}, bf16[4,128,512]{2,1,0:T(8,128)(2,1)S(1)}, u32[]{:S(2)}, u32[]{:S(2)}) collective-permute-start(bf16[4,128,512]{2,1,0:T(8,128)(2,1)S(1)} %collective-permute-done.17.refs_11_.refs_21_.refs_19_), channel_id=1, source_target_pairs={{0,1},{1,2},{2,3},{3,4},{4,5},{5,6},{6,7},{7,0},{8,9},{9,10},{10,1... | collective-permute-start | bytes 1572872 | tf_op jit(solution)/shard_map/ppermute | solution.py:28
  56.8 2.4 %collective-permute-done.8.refs_8_ = bf16[1,2,256,512]{3,2,1,0:T(8,128)(2,1)S(1)} collective-permute-done((bf16[1,2,256,512]{3,2,1,0:T(8,128)(2,1)S(1)}, bf16[1,2,256,512]{3,2,1,0:T(8,128)(2,1)S(1)}, u32[]{:S(2)}, u32[]{:S(2)}) %collective-permute-start.8) | collective-permute-done | bytes 524320 | tf_op jit(solution)/shard_map/ppermute | solution.py:28
  59.2 3.4 %collective-permute-start.10 = (bf16[1,2,256,512]{3,2,1,0:T(8,128)(2,1)S(1)}, bf16[1,2,256,512]{3,2,1,0:T(8,128)(2,1)S(1)}, u32[]{:S(2)}, u32[]{:S(2)}) collective-permute-start(bf16[1,2,256,512]{3,2,1,0:T(8,128)(2,1)S(1)} %collective-permute-done.8.refs_8_), channel_id=1, source_target_pairs={{0,24},{1,25},{2,26},{3,27},{4,28},{5,29},{6,30},{7,31},{8,0},{9,1... | collective-permute-start | bytes 1572872 | tf_op jit(solution)/shard_map/ppermute | solution.py:28
  62.8 3.5 %shard_map.38.refs_22_ = f32[2,4,256,512]{3,2,1,0:T(8,128)S(1)} custom-call(s32[4]{0:T(128)S(1)} %copy-done, bf16[1,2,256,512]{3,2,1,0:T(8,128)(2,1)S(1)} %maximum_bitcast_fusion.refs_1_, bf16[2,2,256,512]{3,2,1,0:T(8,128)(2,1)S(1)} %constant_dynamic-update-slice_fusion.refs_2_, bf16[1,2,256,512]{3,2,1,0:T(8,128)(2,1)S(1)} %collective-permute-done.3.refs_3_, ...), custom_call_target="tpu_custom_call" | custom-call | tf_op jit(solution)/shard_map/pallas_call | solution.py:269
  66.4 0.9 collective-permute-done.18.refs_15_.refs_23_
  67.4 1.3 %collective-permute-done.10.refs_10_ = bf16[1,2,256,512]{3,2,1,0:T(8,128)(2,1)S(1)} collective-permute-done((bf16[1,2,256,512]{3,2,1,0:T(8,128)(2,1)S(1)}, bf16[1,2,256,512]{3,2,1,0:T(8,128)(2,1)S(1)}, u32[]{:S(2)}, u32[]{:S(2)}) %collective-permute-start.10) | collective-permute-done | bytes 524320 | tf_op jit(solution)/shard_map/ppermute | solution.py:28
  68.8 1.0 %collective-permute-start.20 = (bf16[2,4,128,512]{3,2,1,0:T(8,128)(2,1)S(1)}, bf16[2,4,128,512]{3,2,1,0:T(8,128)(2,1)S(1)}, u32[]{:S(2)}, u32[]{:S(2)}) collective-permute-start(bf16[2,4,128,512]{3,2,1,0:T(8,128)(2,1)S(1)} %pad_maximum_fusion), channel_id=1, source_target_pairs={{0,32},{1,33},{2,34},{3,35},{4,36},{5,37},{6,38},{7,39},{8,40},{9,... | collective-permute-start | bytes 3145736 | tf_op jit(solution)/shard_map/ppermute | solution.py:28
  70.0 1.3 %collective-permute-start.23 = (bf16[4,128,512]{2,1,0:T(8,128)(2,1)S(1)}, bf16[4,128,512]{2,1,0:T(8,128)(2,1)S(1)}, u32[]{:S(2)}, u32[]{:S(2)}) collective-permute-start(bf16[4,128,512]{2,1,0:T(8,128)(2,1)S(1)} %all-to-all-done.refs_12_.refs_20_), channel_id=1, source_target_pairs={{0,32},{1,33},{2,34},{3,35},{4,36},{5,37},{6,38},{7,39},{8,40},{9,... | collective-permute-start | bytes 1572872 | tf_op jit(solution)/shard_map/ppermute | solution.py:28
  72.1 0.8 collective-permute-done.23.refs_13_.refs_21_
  72.9 7.5 %shard_map.39.refs_26_ = f32[2,4,256,512]{3,2,1,0:T(8,128)S(1)} custom-call(s32[4]{0:T(128)S(1)} %copy-done, bf16[1,2,256,512]{3,2,1,0:T(8,128)(2,1)S(1)} %maximum_bitcast_fusion.refs_1_, bf16[2,2,256,512]{3,2,1,0:T(8,128)(2,1)S(1)} %constant_dynamic-update-slice_fusion.refs_2_, ...), custom_call_target="tpu_custom_call", output_to_operand_aliasing={{}: (22, {})} | custom-call | tf_op jit(solution)/shard_map/pallas_call | solution.py:269
  80.4 1.3 %collective-permute-start.24 = (bf16[4,128,512]{2,1,0:T(8,128)(2,1)S(1)}, bf16[4,128,512]{2,1,0:T(8,128)(2,1)S(1)}, u32[]{:S(2)}, u32[]{:S(2)}) collective-permute-start(bf16[4,128,512]{2,1,0:T(8,128)(2,1)S(1)} %collective-permute-done.21.refs_14_), channel_id=1, source_target_pairs={{0,32},{1,33},{2,34},{3,35},{4,36},{5,37},{6,38},{7,39},{8,40},{9,... | collective-permute-start | bytes 1572872 | tf_op jit(solution)/shard_map/ppermute | solution.py:28
  81.8 1.5 %collective-permute-done.24.refs_15_ = bf16[4,128,512]{2,1,0:T(8,128)(2,1)S(1)} collective-permute-done((bf16[4,128,512]{2,1,0:T(8,128)(2,1)S(1)}, bf16[4,128,512]{2,1,0:T(8,128)(2,1)S(1)}, u32[]{:S(2)}, u32[]{:S(2)}) %collective-permute-start.24) | collective-permute-done | bytes 524320 | tf_op jit(solution)/shard_map/ppermute | solution.py:28
  83.3 6.0 %shard_map.40 = f32[2,4,4,512]{3,2,1,0:T(4,128)S(1)} custom-call(s32[4]{0:T(128)S(1)} %copy-done, bf16[1,2,256,512]{3,2,1,0:T(8,128)(2,1)S(1)} %maximum_bitcast_fusion.refs_1_, bf16[2,2,256,512]{3,2,1,0:T(8,128)(2,1)S(1)} %constant_dynamic-update-slice_fusion.refs_2_, bf16[1,2,256,512]{3,2,1,0:T(8,128)(2,1)S(1)} %collective-permute-done.3.refs_3_, ...), custom_call_target="tpu_custom_call" | custom-call | tf_op jit(solution)/shard_map/pallas_call | solution.py:269
  89.6 11.9 %all_to_all.10 = bf16[16,2,512]{2,1,0:T(2,128)(2,1)S(1)} all-to-all(bf16[16,2,512]{2,1,0:T(2,128)(2,1)S(1)} %reshape.20), channel_id=1, replica_groups=mesh['y'=4,'c'=2,'x'=4,'z'=8] {'z','c'}, dimensions={0} | all-to-all | bytes 65536 | tf_op jit(solution)/shard_map/all_to_all | solution.py:287
  (44 shorter events, 5.2 us)
Async XLA Ops:
  2.9 4.6 %collective-permute-start = (bf16[256,512]{1,0:T(8,128)(2,1)}, bf16[256,512]{1,0:T(8,128)(2,1)S(1)}, u32[]{:S(2)}, u32[]{:S(2)}) collective-permute-start(bf16[256,512]{1,0:T(8,128)(2,1)} %get-tuple-element.17), channel_id=1, source_target_pairs={{0,32},{1,33},{2,34},{3,35},{4,36},{5,37},{6,38},{7,39},{8,40},{9,... | collective-permute-start | bytes 786440 | tf_op jit(solution)/shard_map/ppermute | solution.py:28
  7.5 55.2 %copy-start = (s32[4]{0:T(128)S(1)}, s32[4]{0:T(128)}, u32[]{:S(2)}) copy-start(s32[4]{0:T(128)} %pad_add_fusion.place.refs_0_) | copy-start | bytes 52
  8.5 15.4 %collective-permute-start.1 = (bf16[1,2,256,512]{3,2,1,0:T(8,128)(2,1)S(1)}, bf16[1,2,256,512]{3,2,1,0:T(8,128)(2,1)S(1)}, u32[]{:S(2)}, u32[]{:S(2)}) collective-permute-start(bf16[1,2,256,512]{3,2,1,0:T(8,128)(2,1)S(1)} %maximum_bitcast_fusion.refs_1_), channel_id=1, source_target_pairs={{0,64},{1,65},{2,66},{3,67},{4,68},{5,69},{6,70},{7,71},{8,72},{9,... | collective-permute-start | bytes 1572872 | tf_op jit(solution)/shard_map/ppermute | solution.py:28
  8.6 15.3 %collective-permute-start.2 = (bf16[1,2,256,512]{3,2,1,0:T(8,128)(2,1)S(1)}, bf16[1,2,256,512]{3,2,1,0:T(8,128)(2,1)S(1)}, u32[]{:S(2)}, u32[]{:S(2)}) collective-permute-start(bf16[1,2,256,512]{3,2,1,0:T(8,128)(2,1)S(1)} %maximum_bitcast_fusion.refs_1_), channel_id=1, source_target_pairs={{0,192},{1,193},{2,194},{3,195},{4,196},{5,197},{6,198},{7,199},{8... | collective-permute-start | bytes 1572872 | tf_op jit(solution)/shard_map/ppermute | solution.py:28
  11.3 12.6 %all-to-all-start = ((bf16[4,128,512]{2,1,0:T(8,128)(2,1)}), bf16[4,128,512]{2,1,0:T(8,128)(2,1)S(1)}, u32[]{:S(2)}, u32[]{:S(2)}) async-start(bf16[4,128,512]{2,1,0:T(8,128)(2,1)} %get-tuple-element.18), calls=%async_computation | async-start | bytes 1048576 | tf_op jit(solution)/shard_map/all_to_all | solution.py:130
  14.8 16.0 %collective-permute-start.7 = (bf16[1,2,256,512]{3,2,1,0:T(8,128)(2,1)S(1)}, bf16[1,2,256,512]{3,2,1,0:T(8,128)(2,1)S(1)}, u32[]{:S(2)}, u32[]{:S(2)}) collective-permute-start(bf16[1,2,256,512]{3,2,1,0:T(8,128)(2,1)S(1)} %maximum_bitcast_fusion.refs_1_), channel_id=1, source_target_pairs={{0,24},{1,25},{2,26},{3,27},{4,28},{5,29},{6,30},{7,31},{8,0},{9,1... | collective-permute-start | bytes 1572872 | tf_op jit(solution)/shard_map/ppermute | solution.py:28
  15.8 14.9 %collective-permute-start.6 = (bf16[1,2,256,512]{3,2,1,0:T(8,128)(2,1)S(1)}, bf16[1,2,256,512]{3,2,1,0:T(8,128)(2,1)S(1)}, u32[]{:S(2)}, u32[]{:S(2)}) collective-permute-start(bf16[1,2,256,512]{3,2,1,0:T(8,128)(2,1)S(1)} %maximum_bitcast_fusion.refs_1_), channel_id=1, source_target_pairs={{0,8},{1,9},{2,10},{3,11},{4,12},{5,13},{6,14},{7,15},{8,16},{9,17... | collective-permute-start | bytes 1572872 | tf_op jit(solution)/shard_map/ppermute | solution.py:28
  23.9 8.3 %collective-permute-start.13 = (bf16[4,128,512]{2,1,0:T(8,128)(2,1)S(1)}, bf16[4,128,512]{2,1,0:T(8,128)(2,1)S(1)}, u32[]{:S(2)}, u32[]{:S(2)}) collective-permute-start(bf16[4,128,512]{2,1,0:T(8,128)(2,1)S(1)} %all-to-all-done.refs_12_.refs_20_), channel_id=1, source_target_pairs={{0,1},{1,2},{2,3},{3,4},{4,5},{5,6},{6,7},{7,0},{8,9},{9,10},{10,1... | collective-permute-start | bytes 1572872 | tf_op jit(solution)/shard_map/ppermute | solution.py:28
  26.1 23.8 %collective-permute-start.4 = (bf16[2,2,256,512]{3,2,1,0:T(8,128)(2,1)S(1)}, bf16[2,2,256,512]{3,2,1,0:T(8,128)(2,1)S(1)}, u32[]{:S(2)}, u32[]{:S(2)}) collective-permute-start(bf16[2,2,256,512]{3,2,1,0:T(8,128)(2,1)S(1)} %constant_dynamic-update-slice_fusion.refs_2_), channel_id=1, source_target_pairs={{0,8},{1,9},{2,10},{3,11},{4,12},{5,13},{6,14},{7,15},{8,16},{9,17... | collective-permute-start | bytes 3145736 | tf_op jit(solution)/shard_map/ppermute | solution.py:28
  29.2 23.9 %collective-permute-start.5 = (bf16[2,2,256,512]{3,2,1,0:T(8,128)(2,1)S(1)}, bf16[2,2,256,512]{3,2,1,0:T(8,128)(2,1)S(1)}, u32[]{:S(2)}, u32[]{:S(2)}) collective-permute-start(bf16[2,2,256,512]{3,2,1,0:T(8,128)(2,1)S(1)} %constant_dynamic-update-slice_fusion.refs_2_), channel_id=1, source_target_pairs={{0,24},{1,25},{2,26},{3,27},{4,28},{5,29},{6,30},{7,31},{8,0},{9,1... | collective-permute-start | bytes 3145736 | tf_op jit(solution)/shard_map/ppermute | solution.py:28
  30.7 13.6 %collective-permute-start.16 = (bf16[4,128,512]{2,1,0:T(8,128)(2,1)S(1)}, bf16[4,128,512]{2,1,0:T(8,128)(2,1)S(1)}, u32[]{:S(2)}, u32[]{:S(2)}) collective-permute-start(bf16[4,128,512]{2,1,0:T(8,128)(2,1)S(1)} %all-to-all-done.refs_12_.refs_20_), channel_id=1, source_target_pairs={{0,39},{1,32},{2,33},{3,34},{4,35},{5,36},{6,37},{7,38},{8,47},{9,... | collective-permute-start | bytes 1572872 | tf_op jit(solution)/shard_map/ppermute | solution.py:28
  30.8 16.1 %collective-permute-start.3 = (bf16[1,2,256,512]{3,2,1,0:T(8,128)(2,1)S(1)}, bf16[1,2,256,512]{3,2,1,0:T(8,128)(2,1)S(1)}, u32[]{:S(2)}, u32[]{:S(2)}) collective-permute-start(bf16[1,2,256,512]{3,2,1,0:T(8,128)(2,1)S(1)} %collective-permute-done.1), channel_id=1, source_target_pairs={{0,64},{1,65},{2,66},{3,67},{4,68},{5,69},{6,70},{7,71},{8,72},{9,... | collective-permute-start | bytes 1572872 | tf_op jit(solution)/shard_map/ppermute | solution.py:28
  32.2 15.4 %collective-permute-start.14 = (bf16[4,128,512]{2,1,0:T(8,128)(2,1)S(1)}, bf16[4,128,512]{2,1,0:T(8,128)(2,1)S(1)}, u32[]{:S(2)}, u32[]{:S(2)}) collective-permute-start(bf16[4,128,512]{2,1,0:T(8,128)(2,1)S(1)} %collective-permute-done.13.refs_8_.refs_18_.refs_16_), channel_id=1, source_target_pairs={{0,1},{1,2},{2,3},{3,4},{4,5},{5,6},{6,7},{7,0},{8,9},{9,10},{10,1... | collective-permute-start | bytes 1572872 | tf_op jit(solution)/shard_map/ppermute | solution.py:28
  44.4 8.7 %collective-permute-start.11 = (bf16[1,2,256,512]{3,2,1,0:T(8,128)(2,1)S(1)}, bf16[1,2,256,512]{3,2,1,0:T(8,128)(2,1)S(1)}, u32[]{:S(2)}, u32[]{:S(2)}) collective-permute-start(bf16[1,2,256,512]{3,2,1,0:T(8,128)(2,1)S(1)} %collective-permute-done.7.refs_7_), channel_id=1, source_target_pairs={{0,24},{1,25},{2,26},{3,27},{4,28},{5,29},{6,30},{7,31},{8,0},{9,1... | collective-permute-start | bytes 1572872 | tf_op jit(solution)/shard_map/ppermute | solution.py:28
  46.8 8.3 %collective-permute-start.17 = (bf16[4,128,512]{2,1,0:T(8,128)(2,1)S(1)}, bf16[4,128,512]{2,1,0:T(8,128)(2,1)S(1)}, u32[]{:S(2)}, u32[]{:S(2)}) collective-permute-start(bf16[4,128,512]{2,1,0:T(8,128)(2,1)S(1)} %collective-permute-done.16.refs_9_.refs_19_.refs_17_), channel_id=1, source_target_pairs={{0,1},{1,2},{2,3},{3,4},{4,5},{5,6},{6,7},{7,0},{8,9},{9,10},{10,1... | collective-permute-start | bytes 1572872 | tf_op jit(solution)/shard_map/ppermute | solution.py:28
  47.7 19.8 %collective-permute-start.19 = (bf16[2,4,128,512]{3,2,1,0:T(8,128)(2,1)S(1)}, bf16[2,4,128,512]{3,2,1,0:T(8,128)(2,1)S(1)}, u32[]{:S(2)}, u32[]{:S(2)}) collective-permute-start(bf16[2,4,128,512]{3,2,1,0:T(8,128)(2,1)S(1)} %pad_maximum_fusion.1), channel_id=1, source_target_pairs={{0,32},{1,33},{2,34},{3,35},{4,36},{5,37},{6,38},{7,39},{8,40},{9,... | collective-permute-start | bytes 3145736 | tf_op jit(solution)/shard_map/ppermute | solution.py:28
  49.9 9.4 %collective-permute-start.8 = (bf16[1,2,256,512]{3,2,1,0:T(8,128)(2,1)S(1)}, bf16[1,2,256,512]{3,2,1,0:T(8,128)(2,1)S(1)}, u32[]{:S(2)}, u32[]{:S(2)}) collective-permute-start(bf16[1,2,256,512]{3,2,1,0:T(8,128)(2,1)S(1)} %collective-permute-done.3.refs_3_), channel_id=1, source_target_pairs={{0,24},{1,25},{2,26},{3,27},{4,28},{5,29},{6,30},{7,31},{8,0},{9,1... | collective-permute-start | bytes 1572872 | tf_op jit(solution)/shard_map/ppermute | solution.py:28
  53.1 15.7 %collective-permute-start.9 = (bf16[2,2,256,512]{3,2,1,0:T(8,128)(2,1)S(1)}, bf16[2,2,256,512]{3,2,1,0:T(8,128)(2,1)S(1)}, u32[]{:S(2)}, u32[]{:S(2)}) collective-permute-start(bf16[2,2,256,512]{3,2,1,0:T(8,128)(2,1)S(1)} %collective-permute-done.4.refs_4_), channel_id=1, source_target_pairs={{0,8},{1,9},{2,10},{3,11},{4,12},{5,13},{6,14},{7,15},{8,16},{9,17... | collective-permute-start | bytes 3145736 | tf_op jit(solution)/shard_map/ppermute | solution.py:28
  53.1 13.2 %collective-permute-start.15 = (bf16[4,128,512]{2,1,0:T(8,128)(2,1)S(1)}, bf16[4,128,512]{2,1,0:T(8,128)(2,1)S(1)}, u32[]{:S(2)}, u32[]{:S(2)}) collective-permute-start(bf16[4,128,512]{2,1,0:T(8,128)(2,1)S(1)} %collective-permute-done.14.refs_10_.refs_20_.refs_18_), channel_id=1, source_target_pairs={{0,1},{1,2},{2,3},{3,4},{4,5},{5,6},{6,7},{7,0},{8,9},{9,10},{10,1... | collective-permute-start | bytes 1572872 | tf_op jit(solution)/shard_map/ppermute | solution.py:28
  55.2 12.2 %collective-permute-start.18 = (bf16[4,128,512]{2,1,0:T(8,128)(2,1)S(1)}, bf16[4,128,512]{2,1,0:T(8,128)(2,1)S(1)}, u32[]{:S(2)}, u32[]{:S(2)}) collective-permute-start(bf16[4,128,512]{2,1,0:T(8,128)(2,1)S(1)} %collective-permute-done.17.refs_11_.refs_21_.refs_19_), channel_id=1, source_target_pairs={{0,1},{1,2},{2,3},{3,4},{4,5},{5,6},{6,7},{7,0},{8,9},{9,10},{10,1... | collective-permute-start | bytes 1572872 | tf_op jit(solution)/shard_map/ppermute | solution.py:28
  59.2 9.5 %collective-permute-start.10 = (bf16[1,2,256,512]{3,2,1,0:T(8,128)(2,1)S(1)}, bf16[1,2,256,512]{3,2,1,0:T(8,128)(2,1)S(1)}, u32[]{:S(2)}, u32[]{:S(2)}) collective-permute-start(bf16[1,2,256,512]{3,2,1,0:T(8,128)(2,1)S(1)} %collective-permute-done.8.refs_8_), channel_id=1, source_target_pairs={{0,24},{1,25},{2,26},{3,27},{4,28},{5,29},{6,30},{7,31},{8,0},{9,1... | collective-permute-start | bytes 1572872 | tf_op jit(solution)/shard_map/ppermute | solution.py:28
  66.3 6.6 %collective-permute-start.22 = (bf16[2,4,128,512]{3,2,1,0:T(8,128)(2,1)S(1)}, bf16[2,4,128,512]{3,2,1,0:T(8,128)(2,1)S(1)}, u32[]{:S(2)}, u32[]{:S(2)}) collective-permute-start(bf16[2,4,128,512]{3,2,1,0:T(8,128)(2,1)S(1)} %pad_maximum_fusion.2), channel_id=1, source_target_pairs={{0,32},{1,33},{2,34},{3,35},{4,36},{5,37},{6,38},{7,39},{8,40},{9,... | collective-permute-start | bytes 3145736 | tf_op jit(solution)/shard_map/ppermute | solution.py:28
  68.8 11.7 %collective-permute-start.20 = (bf16[2,4,128,512]{3,2,1,0:T(8,128)(2,1)S(1)}, bf16[2,4,128,512]{3,2,1,0:T(8,128)(2,1)S(1)}, u32[]{:S(2)}, u32[]{:S(2)}) collective-permute-start(bf16[2,4,128,512]{3,2,1,0:T(8,128)(2,1)S(1)} %pad_maximum_fusion), channel_id=1, source_target_pairs={{0,32},{1,33},{2,34},{3,35},{4,36},{5,37},{6,38},{7,39},{8,40},{9,... | collective-permute-start | bytes 3145736 | tf_op jit(solution)/shard_map/ppermute | solution.py:28
  69.8 10.6 %collective-permute-start.12 = (bf16[1,2,256,512]{3,2,1,0:T(8,128)(2,1)S(1)}, bf16[1,2,256,512]{3,2,1,0:T(8,128)(2,1)S(1)}, u32[]{:S(2)}, u32[]{:S(2)}) collective-permute-start(bf16[1,2,256,512]{3,2,1,0:T(8,128)(2,1)S(1)} %collective-permute-done.3.refs_3_), channel_id=1, source_target_pairs={{0,8},{1,9},{2,10},{3,11},{4,12},{5,13},{6,14},{7,15},{8,16},{9,17... | collective-permute-start | bytes 1572872 | tf_op jit(solution)/shard_map/ppermute | solution.py:28
  70.0 2.9 %collective-permute-start.23 = (bf16[4,128,512]{2,1,0:T(8,128)(2,1)S(1)}, bf16[4,128,512]{2,1,0:T(8,128)(2,1)S(1)}, u32[]{:S(2)}, u32[]{:S(2)}) collective-permute-start(bf16[4,128,512]{2,1,0:T(8,128)(2,1)S(1)} %all-to-all-done.refs_12_.refs_20_), channel_id=1, source_target_pairs={{0,32},{1,33},{2,34},{3,35},{4,36},{5,37},{6,38},{7,39},{8,40},{9,... | collective-permute-start | bytes 1572872 | tf_op jit(solution)/shard_map/ppermute | solution.py:28
  71.4 9.1 %collective-permute-start.21 = (bf16[4,128,512]{2,1,0:T(8,128)(2,1)S(1)}, bf16[4,128,512]{2,1,0:T(8,128)(2,1)S(1)}, u32[]{:S(2)}, u32[]{:S(2)}) collective-permute-start(bf16[4,128,512]{2,1,0:T(8,128)(2,1)S(1)} %collective-permute-done.15.refs_14_.refs_22_), channel_id=1, source_target_pairs={{0,1},{1,2},{2,3},{3,4},{4,5},{5,6},{6,7},{7,0},{8,9},{9,10},{10,1... | collective-permute-start | bytes 1572872 | tf_op jit(solution)/shard_map/ppermute | solution.py:28
  80.4 2.9 %collective-permute-start.24 = (bf16[4,128,512]{2,1,0:T(8,128)(2,1)S(1)}, bf16[4,128,512]{2,1,0:T(8,128)(2,1)S(1)}, u32[]{:S(2)}, u32[]{:S(2)}) collective-permute-start(bf16[4,128,512]{2,1,0:T(8,128)(2,1)S(1)} %collective-permute-done.21.refs_14_), channel_id=1, source_target_pairs={{0,32},{1,33},{2,34},{3,35},{4,36},{5,37},{6,38},{7,39},{8,40},{9,... | collective-permute-start | bytes 1572872 | tf_op jit(solution)/shard_map/ppermute | solution.py:28

commit v7 on v6

--- a/solution.py
+++ b/solution.py
@@ -277,6 +277,26 @@
     )(place, *(got[n] for n in names), *carried)
 
 
+def finish_kernel(got, out):
+    values = got[...].astype(jnp.float32)
+    peak = jnp.max(jnp.max(values, axis=0), axis=0, keepdims=True)
+    per = values.shape[1] // NX
+    scaled = values / (1.0 + peak)[None]
+    rows = [scaled[:, x * per : (x + 1) * per, :] for x in range(NX)]
+    rows = [r.reshape(-1, r.shape[-1]) for r in rows]
+    out[...] = jnp.transpose(jnp.concatenate(rows, axis=0)).astype(out.dtype)
+
+
+def finish(got):
+    shape = (got.shape[2], got.shape[0] * got.shape[1])
+    return pl.pallas_call(
+        finish_kernel,
+        out_shape=jax.ShapeDtypeStruct(shape, got.dtype),
+        in_specs=[VMEM],
+        out_specs=VMEM,
+    )(got)
+
+
 def body(hidden, head_weight, lengths):
     place = jnp.stack([lax.axis_index(a) for a in AXES]).astype(jnp.int32)
     kept, other, blocks = prep(place, lengths, hidden, head_weight)
@@ -285,10 +305,7 @@
     pooled = pooled.reshape(NC, NX * pooled.shape[2], NZ, each)
     pooled = jnp.transpose(pooled, (2, 0, 1, 3)).reshape(NZ * NC, -1, each)
     got = lax.all_to_all(pooled, ("z", "c"), split_axis=0, concat_axis=0, tiled=True)
-    got = got.reshape(NZ, NC, NX, -1, each)
-    got = jnp.transpose(got, (2, 0, 1, 3, 4)).reshape(-1, each).astype(jnp.float32)
-    peak = jnp.max(got, axis=0)
-    return jnp.transpose((got / (1.0 + peak)[None, :]).astype(jnp.bfloat16))
+    return finish(got)
 
 
 def solution(mesh):

time: 103 us -> 104 us (level)
  waiting for transfers between devices: 29.1 us -> 25.4 us
  starting transfers between devices: 38.7 us -> 42.4 us
  Pallas kernels: 19.3 us -> 21 us
    ppermute x25, starting transfers between devices: 35.3 us -> 38.9 us  [permute(): return lax.ppermute(block, AXES, pairs)]
    ppermute x25, waiting for transfers between devices: 21.5 us -> 17.9 us  [permute(): return lax.ppermute(block, AXES, pairs)]
    pallas_call x0 -> x1, Pallas kernels: none -> 1.57 us  [finish(): pl.pallas_call(finish_kernel, out_shape=jax.ShapeDtypeStruct(shape, got.d...]
  transfers between devices with their start and end apart: 26 -> 26, of which waited for: 11 -> 12; matrix products, arithmetic and copies ran while one was open for 0% -> 0% of each run, Pallas kernels for 11% -> 11%
where the time goes in v7:
time: 104 us
  starting transfers between devices  42.4 us (41%)
  waiting for transfers between devices  25.4 us (24%)
  Pallas kernels  21 us (20%)
  blocking collectives  11.8 us (11%)
  other arithmetic  1.92 us (2%)
    ppermute x25, starting transfers between devices, permute(): return lax.ppermute(block, AXES, pairs)  38.9 us
    ppermute x25, waiting for transfers between devices, permute(): return lax.ppermute(block, AXES, pairs)  17.9 us
    pallas_call x3, Pallas kernels, run_stage(): pl.pallas_call(kernel, out_shape=result if last else total, in_specs=[SME...  17.2 us
    all_to_all x1, blocking collectives, body(): lax.all_to_all(pooled, ('z', 'c'), split_axis=0, concat_axis=0, tiled=True)  11.8 us
    all_to_all x1, waiting for transfers between devices, piece(): got['A0'] = lax.all_to_all(blocks, 'x', split_axis=0, concat_axis=0)  7.59 us
    all_to_all x1, starting transfers between devices, piece(): got['A0'] = lax.all_to_all(blocks, 'x', split_axis=0, concat_axis=0)  3.47 us
    pallas_call x1, Pallas kernels, prep(): pl.pallas_call(prep_kernel, out_shape=[half, half, blocks], in_specs=[SME...  2.25 us
  transfers between devices with their start and end apart: 26, of which 12 were waited for; matrix products, arithmetic and copies ran while one was open for 0% of the time, Pallas kernels for 11%

profile of v7, /device:TPU:1, one launch (start us, length us, event | category | flops | bytes accessed | tf_op | source)
XLA Modules:
  0.0 103.7 jit_solution(18382401341132192942)
XLA Ops:
  0.6 2.3 %shard_map.37 = (bf16[256,512]{1,0:T(8,128)(2,1)}, bf16[256,512]{1,0:T(8,128)(2,1)}, bf16[4,128,512]{2,1,0:T(8,128)(2,1)}) custom-call(s32[4]{0:T(128)} %pad_add_fusion.place.refs_0_, s32[8]{0:T(128)} %lengths.1, bf16[512,512]{1,0:T(8,128)(2,1)} %hid.1, bf16[128,2048]{1,0:T(8,128)(2,1)} %head.1), custom_call_target="tpu_custom_call" | custom-call | tf_op jit(solution)/shard_map/pallas_call | solution.py:78
  2.9 3.2 %collective-permute-start = (bf16[256,512]{1,0:T(8,128)(2,1)}, bf16[256,512]{1,0:T(8,128)(2,1)S(1)}, u32[]{:S(2)}, u32[]{:S(2)}) collective-permute-start(bf16[256,512]{1,0:T(8,128)(2,1)} %get-tuple-element.17), channel_id=1, source_target_pairs={{0,32},{1,33},{2,34},{3,35},{4,36},{5,37},{6,38},{7,39},{8,40},{9,... | collective-permute-start | bytes 786440 | tf_op jit(solution)/shard_map/ppermute | solution.py:28
  6.1 1.4 %collective-permute-done = bf16[256,512]{1,0:T(8,128)(2,1)S(1)} collective-permute-done((bf16[256,512]{1,0:T(8,128)(2,1)}, bf16[256,512]{1,0:T(8,128)(2,1)S(1)}, u32[]{:S(2)}, u32[]{:S(2)}) %collective-permute-start) | collective-permute-done | bytes 262176 | tf_op jit(solution)/shard_map/ppermute | solution.py:28
  7.5 1.0 maximum_bitcast_fusion.refs_1_
  8.6 2.7 %collective-permute-start.2 = (bf16[1,2,256,512]{3,2,1,0:T(8,128)(2,1)S(1)}, bf16[1,2,256,512]{3,2,1,0:T(8,128)(2,1)S(1)}, u32[]{:S(2)}, u32[]{:S(2)}) collective-permute-start(bf16[1,2,256,512]{3,2,1,0:T(8,128)(2,1)S(1)} %maximum_bitcast_fusion.refs_1_), channel_id=1, source_target_pairs={{0,192},{1,193},{2,194},{3,195},{4,196},{5,197},{6,198},{7,199},{8... | collective-permute-start | bytes 1572872 | tf_op jit(solution)/shard_map/ppermute | solution.py:28
  11.2 3.5 %all-to-all-start = ((bf16[4,128,512]{2,1,0:T(8,128)(2,1)}), bf16[4,128,512]{2,1,0:T(8,128)(2,1)S(1)}, u32[]{:S(2)}, u32[]{:S(2)}) async-start(bf16[4,128,512]{2,1,0:T(8,128)(2,1)} %get-tuple-element.18), calls=%async_computation | async-start | bytes 1048576 | tf_op jit(solution)/shard_map/all_to_all | solution.py:130
  14.7 1.1 %collective-permute-start.7 = (bf16[1,2,256,512]{3,2,1,0:T(8,128)(2,1)S(1)}, bf16[1,2,256,512]{3,2,1,0:T(8,128)(2,1)S(1)}, u32[]{:S(2)}, u32[]{:S(2)}) collective-permute-start(bf16[1,2,256,512]{3,2,1,0:T(8,128)(2,1)S(1)} %maximum_bitcast_fusion.refs_1_), channel_id=1, source_target_pairs={{0,24},{1,25},{2,26},{3,27},{4,28},{5,29},{6,30},{7,31},{8,0},{9,1... | collective-permute-start | bytes 1572872 | tf_op jit(solution)/shard_map/ppermute | solution.py:28
  16.3 7.6 %all-to-all-done.refs_12_.refs_20_ = bf16[4,128,512]{2,1,0:T(8,128)(2,1)S(1)} async-done(((bf16[4,128,512]{2,1,0:T(8,128)(2,1)}), bf16[4,128,512]{2,1,0:T(8,128)(2,1)S(1)}, u32[]{:S(2)}, u32[]{:S(2)}) %all-to-all-start) | async-done | bytes 524320 | tf_op jit(solution)/shard_map/all_to_all | solution.py:130
  23.9 2.1 %collective-permute-start.13 = (bf16[4,128,512]{2,1,0:T(8,128)(2,1)S(1)}, bf16[4,128,512]{2,1,0:T(8,128)(2,1)S(1)}, u32[]{:S(2)}, u32[]{:S(2)}) collective-permute-start(bf16[4,128,512]{2,1,0:T(8,128)(2,1)S(1)} %all-to-all-done.refs_12_.refs_20_), channel_id=1, source_target_pairs={{0,1},{1,2},{2,3},{3,4},{4,5},{5,6},{6,7},{7,0},{8,9},{9,10},{10,1... | collective-permute-start | bytes 1572872 | tf_op jit(solution)/shard_map/ppermute | solution.py:28
  26.0 3.1 %collective-permute-start.4 = (bf16[2,2,256,512]{3,2,1,0:T(8,128)(2,1)S(1)}, bf16[2,2,256,512]{3,2,1,0:T(8,128)(2,1)S(1)}, u32[]{:S(2)}, u32[]{:S(2)}) collective-permute-start(bf16[2,2,256,512]{3,2,1,0:T(8,128)(2,1)S(1)} %constant_dynamic-update-slice_fusion.refs_2_), channel_id=1, source_target_pairs={{0,8},{1,9},{2,10},{3,11},{4,12},{5,13},{6,14},{7,15},{8,16},{9,17... | collective-permute-start | bytes 3145736 | tf_op jit(solution)/shard_map/ppermute | solution.py:28
  29.2 1.5 %collective-permute-start.5 = (bf16[2,2,256,512]{3,2,1,0:T(8,128)(2,1)S(1)}, bf16[2,2,256,512]{3,2,1,0:T(8,128)(2,1)S(1)}, u32[]{:S(2)}, u32[]{:S(2)}) collective-permute-start(bf16[2,2,256,512]{3,2,1,0:T(8,128)(2,1)S(1)} %constant_dynamic-update-slice_fusion.refs_2_), channel_id=1, source_target_pairs={{0,24},{1,25},{2,26},{3,27},{4,28},{5,29},{6,30},{7,31},{8,0},{9,1... | collective-permute-start | bytes 3145736 | tf_op jit(solution)/shard_map/ppermute | solution.py:28
  30.7 1.3 %collective-permute-start.3 = (bf16[1,2,256,512]{3,2,1,0:T(8,128)(2,1)S(1)}, bf16[1,2,256,512]{3,2,1,0:T(8,128)(2,1)S(1)}, u32[]{:S(2)}, u32[]{:S(2)}) collective-permute-start(bf16[1,2,256,512]{3,2,1,0:T(8,128)(2,1)S(1)} %collective-permute-done.1), channel_id=1, source_target_pairs={{0,64},{1,65},{2,66},{3,67},{4,68},{5,69},{6,70},{7,71},{8,72},{9,... | collective-permute-start | bytes 1572872 | tf_op jit(solution)/shard_map/ppermute | solution.py:28
  32.2 3.3 %collective-permute-start.14 = (bf16[4,128,512]{2,1,0:T(8,128)(2,1)S(1)}, bf16[4,128,512]{2,1,0:T(8,128)(2,1)S(1)}, u32[]{:S(2)}, u32[]{:S(2)}) collective-permute-start(bf16[4,128,512]{2,1,0:T(8,128)(2,1)S(1)} %collective-permute-done.13.refs_8_.refs_18_.refs_16_), channel_id=1, source_target_pairs={{0,1},{1,2},{2,3},{3,4},{4,5},{5,6},{6,7},{7,0},{8,9},{9,10},{10,1... | collective-permute-start | bytes 1572872 | tf_op jit(solution)/shard_map/ppermute | solution.py:28
  35.5 8.8 %collective-permute-done.16.refs_9_.refs_19_.refs_17_ = bf16[4,128,512]{2,1,0:T(8,128)(2,1)S(1)} collective-permute-done((bf16[4,128,512]{2,1,0:T(8,128)(2,1)S(1)}, bf16[4,128,512]{2,1,0:T(8,128)(2,1)S(1)}, u32[]{:S(2)}, u32[]{:S(2)}) %collective-permute-start.16) | collective-permute-done | bytes 524320 | tf_op jit(solution)/shard_map/ppermute | solution.py:28
  44.3 2.5 %collective-permute-done.3.refs_3_ = bf16[1,2,256,512]{3,2,1,0:T(8,128)(2,1)S(1)} collective-permute-done((bf16[1,2,256,512]{3,2,1,0:T(8,128)(2,1)S(1)}, bf16[1,2,256,512]{3,2,1,0:T(8,128)(2,1)S(1)}, u32[]{:S(2)}, u32[]{:S(2)}) %collective-permute-start.3) | collective-permute-done | bytes 524320 | tf_op jit(solution)/shard_map/ppermute | solution.py:28
  47.6 1.9 %collective-permute-start.8 = (bf16[1,2,256,512]{3,2,1,0:T(8,128)(2,1)S(1)}, bf16[1,2,256,512]{3,2,1,0:T(8,128)(2,1)S(1)}, u32[]{:S(2)}, u32[]{:S(2)}) collective-permute-start(bf16[1,2,256,512]{3,2,1,0:T(8,128)(2,1)S(1)} %collective-permute-done.3.refs_3_), channel_id=1, source_target_pairs={{0,24},{1,25},{2,26},{3,27},{4,28},{5,29},{6,30},{7,31},{8,0},{9,1... | collective-permute-start | bytes 1572872 | tf_op jit(solution)/shard_map/ppermute | solution.py:28
  49.5 2.3 %collective-permute-start.19 = (bf16[2,4,128,512]{3,2,1,0:T(8,128)(2,1)S(1)}, bf16[2,4,128,512]{3,2,1,0:T(8,128)(2,1)S(1)}, u32[]{:S(2)}, u32[]{:S(2)}) collective-permute-start(bf16[2,4,128,512]{3,2,1,0:T(8,128)(2,1)S(1)} %pad_maximum_fusion.1), channel_id=1, source_target_pairs={{0,32},{1,33},{2,34},{3,35},{4,36},{5,37},{6,38},{7,39},{8,40},{9,... | collective-permute-start | bytes 3145736 | tf_op jit(solution)/shard_map/ppermute | solution.py:28
  52.7 2.4 %collective-permute-start.15 = (bf16[4,128,512]{2,1,0:T(8,128)(2,1)S(1)}, bf16[4,128,512]{2,1,0:T(8,128)(2,1)S(1)}, u32[]{:S(2)}, u32[]{:S(2)}) collective-permute-start(bf16[4,128,512]{2,1,0:T(8,128)(2,1)S(1)} %collective-permute-done.14.refs_10_.refs_20_.refs_18_), channel_id=1, source_target_pairs={{0,1},{1,2},{2,3},{3,4},{4,5},{5,6},{6,7},{7,0},{8,9},{9,10},{10,1... | collective-permute-start | bytes 1572872 | tf_op jit(solution)/shard_map/ppermute | solution.py:28
  55.1 1.6 %collective-permute-start.18 = (bf16[4,128,512]{2,1,0:T(8,128)(2,1)S(1)}, bf16[4,128,512]{2,1,0:T(8,128)(2,1)S(1)}, u32[]{:S(2)}, u32[]{:S(2)}) collective-permute-start(bf16[4,128,512]{2,1,0:T(8,128)(2,1)S(1)} %collective-permute-done.17.refs_11_.refs_21_.refs_19_), channel_id=1, source_target_pairs={{0,1},{1,2},{2,3},{3,4},{4,5},{5,6},{6,7},{7,0},{8,9},{9,10},{10,1... | collective-permute-start | bytes 1572872 | tf_op jit(solution)/shard_map/ppermute | solution.py:28
  56.8 1.5 %collective-permute-done.8.refs_8_ = bf16[1,2,256,512]{3,2,1,0:T(8,128)(2,1)S(1)} collective-permute-done((bf16[1,2,256,512]{3,2,1,0:T(8,128)(2,1)S(1)}, bf16[1,2,256,512]{3,2,1,0:T(8,128)(2,1)S(1)}, u32[]{:S(2)}, u32[]{:S(2)}) %collective-permute-start.8) | collective-permute-done | bytes 524320 | tf_op jit(solution)/shard_map/ppermute | solution.py:28
  58.3 1.2 %collective-permute-start.10 = (bf16[1,2,256,512]{3,2,1,0:T(8,128)(2,1)S(1)}, bf16[1,2,256,512]{3,2,1,0:T(8,128)(2,1)S(1)}, u32[]{:S(2)}, u32[]{:S(2)}) collective-permute-start(bf16[1,2,256,512]{3,2,1,0:T(8,128)(2,1)S(1)} %collective-permute-done.8.refs_8_), channel_id=1, source_target_pairs={{0,24},{1,25},{2,26},{3,27},{4,28},{5,29},{6,30},{7,31},{8,0},{9,1... | collective-permute-start | bytes 1572872 | tf_op jit(solution)/shard_map/ppermute | solution.py:28
  59.6 3.5 %shard_map.38.refs_22_ = f32[2,4,256,512]{3,2,1,0:T(8,128)S(1)} custom-call(s32[4]{0:T(128)S(1)} %copy-done, bf16[1,2,256,512]{3,2,1,0:T(8,128)(2,1)S(1)} %maximum_bitcast_fusion.refs_1_, bf16[2,2,256,512]{3,2,1,0:T(8,128)(2,1)S(1)} %constant_dynamic-update-slice_fusion.refs_2_, bf16[1,2,256,512]{3,2,1,0:T(8,128)(2,1)S(1)} %collective-permute-done.3.refs_3_, ...), custom_call_target="tpu_custom_call" | custom-call | tf_op jit(solution)/shard_map/pallas_call | solution.py:269
  63.2 2.8 %collective-permute-start.22 = (bf16[2,4,128,512]{3,2,1,0:T(8,128)(2,1)S(1)}, bf16[2,4,128,512]{3,2,1,0:T(8,128)(2,1)S(1)}, u32[]{:S(2)}, u32[]{:S(2)}) collective-permute-start(bf16[2,4,128,512]{3,2,1,0:T(8,128)(2,1)S(1)} %pad_maximum_fusion.2), channel_id=1, source_target_pairs={{0,32},{1,33},{2,34},{3,35},{4,36},{5,37},{6,38},{7,39},{8,40},{9,... | collective-permute-start | bytes 3145736 | tf_op jit(solution)/shard_map/ppermute | solution.py:28
  67.0 2.8 %collective-permute-start.20 = (bf16[2,4,128,512]{3,2,1,0:T(8,128)(2,1)S(1)}, bf16[2,4,128,512]{3,2,1,0:T(8,128)(2,1)S(1)}, u32[]{:S(2)}, u32[]{:S(2)}) collective-permute-start(bf16[2,4,128,512]{3,2,1,0:T(8,128)(2,1)S(1)} %pad_maximum_fusion), channel_id=1, source_target_pairs={{0,32},{1,33},{2,34},{3,35},{4,36},{5,37},{6,38},{7,39},{8,40},{9,... | collective-permute-start | bytes 3145736 | tf_op jit(solution)/shard_map/ppermute | solution.py:28
  70.0 1.3 %collective-permute-start.23 = (bf16[4,128,512]{2,1,0:T(8,128)(2,1)S(1)}, bf16[4,128,512]{2,1,0:T(8,128)(2,1)S(1)}, u32[]{:S(2)}, u32[]{:S(2)}) collective-permute-start(bf16[4,128,512]{2,1,0:T(8,128)(2,1)S(1)} %all-to-all-done.refs_12_.refs_20_), channel_id=1, source_target_pairs={{0,32},{1,33},{2,34},{3,35},{4,36},{5,37},{6,38},{7,39},{8,40},{9,... | collective-permute-start | bytes 1572872 | tf_op jit(solution)/shard_map/ppermute | solution.py:28
  72.0 0.8 collective-permute-done.23.refs_13_.refs_21_
  72.9 7.5 %shard_map.39.refs_26_ = f32[2,4,256,512]{3,2,1,0:T(8,128)S(1)} custom-call(s32[4]{0:T(128)S(1)} %copy-done, bf16[1,2,256,512]{3,2,1,0:T(8,128)(2,1)S(1)} %maximum_bitcast_fusion.refs_1_, bf16[2,2,256,512]{3,2,1,0:T(8,128)(2,1)S(1)} %constant_dynamic-update-slice_fusion.refs_2_, ...), custom_call_target="tpu_custom_call", output_to_operand_aliasing={{}: (22, {})} | custom-call | tf_op jit(solution)/shard_map/pallas_call | solution.py:269
  80.4 1.3 %collective-permute-start.24 = (bf16[4,128,512]{2,1,0:T(8,128)(2,1)S(1)}, bf16[4,128,512]{2,1,0:T(8,128)(2,1)S(1)}, u32[]{:S(2)}, u32[]{:S(2)}) collective-permute-start(bf16[4,128,512]{2,1,0:T(8,128)(2,1)S(1)} %collective-permute-done.21.refs_14_), channel_id=1, source_target_pairs={{0,32},{1,33},{2,34},{3,35},{4,36},{5,37},{6,38},{7,39},{8,40},{9,... | collective-permute-start | bytes 1572872 | tf_op jit(solution)/shard_map/ppermute | solution.py:28
  81.7 1.5 %collective-permute-done.24.refs_15_ = bf16[4,128,512]{2,1,0:T(8,128)(2,1)S(1)} collective-permute-done((bf16[4,128,512]{2,1,0:T(8,128)(2,1)S(1)}, bf16[4,128,512]{2,1,0:T(8,128)(2,1)S(1)}, u32[]{:S(2)}, u32[]{:S(2)}) %collective-permute-start.24) | collective-permute-done | bytes 524320 | tf_op jit(solution)/shard_map/ppermute | solution.py:28
  83.3 6.1 %shard_map.40 = f32[2,4,4,512]{3,2,1,0:T(4,128)S(1)} custom-call(s32[4]{0:T(128)S(1)} %copy-done, bf16[1,2,256,512]{3,2,1,0:T(8,128)(2,1)S(1)} %maximum_bitcast_fusion.refs_1_, bf16[2,2,256,512]{3,2,1,0:T(8,128)(2,1)S(1)} %constant_dynamic-update-slice_fusion.refs_2_, bf16[1,2,256,512]{3,2,1,0:T(8,128)(2,1)S(1)} %collective-permute-done.3.refs_3_, ...), custom_call_target="tpu_custom_call" | custom-call | tf_op jit(solution)/shard_map/pallas_call | solution.py:269
  89.7 11.8 %all_to_all.10 = bf16[16,2,512]{2,1,0:T(2,128)(2,1)S(1)} all-to-all(bf16[16,2,512]{2,1,0:T(2,128)(2,1)S(1)} %reshape.8), channel_id=1, replica_groups=mesh['y'=4,'c'=2,'x'=4,'z'=8] {'z','c'}, dimensions={0} | all-to-all | bytes 65536 | tf_op jit(solution)/shard_map/all_to_all | solution.py:307
  102.2 1.6 %shard_map.41 = bf16[64,256]{1,0:T(8,128)(2,1)} custom-call(bf16[16,16,64]{2,1,0:T(8,128)(2,1)} %reshape.9.got), custom_call_target="tpu_custom_call" | custom-call | tf_op jit(solution)/shard_map/pallas_call | solution.py:292
  (40 shorter events, 6.2 us)
Async XLA Ops:
  2.9 4.6 %collective-permute-start = (bf16[256,512]{1,0:T(8,128)(2,1)}, bf16[256,512]{1,0:T(8,128)(2,1)S(1)}, u32[]{:S(2)}, u32[]{:S(2)}) collective-permute-start(bf16[256,512]{1,0:T(8,128)(2,1)} %get-tuple-element.17), channel_id=1, source_target_pairs={{0,32},{1,33},{2,34},{3,35},{4,36},{5,37},{6,38},{7,39},{8,40},{9,... | collective-permute-start | bytes 786440 | tf_op jit(solution)/shard_map/ppermute | solution.py:28
  7.5 52.1 %copy-start = (s32[4]{0:T(128)S(1)}, s32[4]{0:T(128)}, u32[]{:S(2)}) copy-start(s32[4]{0:T(128)} %pad_add_fusion.place.refs_0_) | copy-start | bytes 52
  8.5 15.4 %collective-permute-start.1 = (bf16[1,2,256,512]{3,2,1,0:T(8,128)(2,1)S(1)}, bf16[1,2,256,512]{3,2,1,0:T(8,128)(2,1)S(1)}, u32[]{:S(2)}, u32[]{:S(2)}) collective-permute-start(bf16[1,2,256,512]{3,2,1,0:T(8,128)(2,1)S(1)} %maximum_bitcast_fusion.refs_1_), channel_id=1, source_target_pairs={{0,64},{1,65},{2,66},{3,67},{4,68},{5,69},{6,70},{7,71},{8,72},{9,... | collective-permute-start | bytes 1572872 | tf_op jit(solution)/shard_map/ppermute | solution.py:28
  8.6 15.3 %collective-permute-start.2 = (bf16[1,2,256,512]{3,2,1,0:T(8,128)(2,1)S(1)}, bf16[1,2,256,512]{3,2,1,0:T(8,128)(2,1)S(1)}, u32[]{:S(2)}, u32[]{:S(2)}) collective-permute-start(bf16[1,2,256,512]{3,2,1,0:T(8,128)(2,1)S(1)} %maximum_bitcast_fusion.refs_1_), channel_id=1, source_target_pairs={{0,192},{1,193},{2,194},{3,195},{4,196},{5,197},{6,198},{7,199},{8... | collective-permute-start | bytes 1572872 | tf_op jit(solution)/shard_map/ppermute | solution.py:28
  11.2 12.6 %all-to-all-start = ((bf16[4,128,512]{2,1,0:T(8,128)(2,1)}), bf16[4,128,512]{2,1,0:T(8,128)(2,1)S(1)}, u32[]{:S(2)}, u32[]{:S(2)}) async-start(bf16[4,128,512]{2,1,0:T(8,128)(2,1)} %get-tuple-element.18), calls=%async_computation | async-start | bytes 1048576 | tf_op jit(solution)/shard_map/all_to_all | solution.py:130
  14.7 16.0 %collective-permute-start.7 = (bf16[1,2,256,512]{3,2,1,0:T(8,128)(2,1)S(1)}, bf16[1,2,256,512]{3,2,1,0:T(8,128)(2,1)S(1)}, u32[]{:S(2)}, u32[]{:S(2)}) collective-permute-start(bf16[1,2,256,512]{3,2,1,0:T(8,128)(2,1)S(1)} %maximum_bitcast_fusion.refs_1_), channel_id=1, source_target_pairs={{0,24},{1,25},{2,26},{3,27},{4,28},{5,29},{6,30},{7,31},{8,0},{9,1... | collective-permute-start | bytes 1572872 | tf_op jit(solution)/shard_map/ppermute | solution.py:28
  15.8 14.9 %collective-permute-start.6 = (bf16[1,2,256,512]{3,2,1,0:T(8,128)(2,1)S(1)}, bf16[1,2,256,512]{3,2,1,0:T(8,128)(2,1)S(1)}, u32[]{:S(2)}, u32[]{:S(2)}) collective-permute-start(bf16[1,2,256,512]{3,2,1,0:T(8,128)(2,1)S(1)} %maximum_bitcast_fusion.refs_1_), channel_id=1, source_target_pairs={{0,8},{1,9},{2,10},{3,11},{4,12},{5,13},{6,14},{7,15},{8,16},{9,17... | collective-permute-start | bytes 1572872 | tf_op jit(solution)/shard_map/ppermute | solution.py:28
  23.9 8.3 %collective-permute-start.13 = (bf16[4,128,512]{2,1,0:T(8,128)(2,1)S(1)}, bf16[4,128,512]{2,1,0:T(8,128)(2,1)S(1)}, u32[]{:S(2)}, u32[]{:S(2)}) collective-permute-start(bf16[4,128,512]{2,1,0:T(8,128)(2,1)S(1)} %all-to-all-done.refs_12_.refs_20_), channel_id=1, source_target_pairs={{0,1},{1,2},{2,3},{3,4},{4,5},{5,6},{6,7},{7,0},{8,9},{9,10},{10,1... | collective-permute-start | bytes 1572872 | tf_op jit(solution)/shard_map/ppermute | solution.py:28
  26.0 23.5 %collective-permute-start.4 = (bf16[2,2,256,512]{3,2,1,0:T(8,128)(2,1)S(1)}, bf16[2,2,256,512]{3,2,1,0:T(8,128)(2,1)S(1)}, u32[]{:S(2)}, u32[]{:S(2)}) collective-permute-start(bf16[2,2,256,512]{3,2,1,0:T(8,128)(2,1)S(1)} %constant_dynamic-update-slice_fusion.refs_2_), channel_id=1, source_target_pairs={{0,8},{1,9},{2,10},{3,11},{4,12},{5,13},{6,14},{7,15},{8,16},{9,17... | collective-permute-start | bytes 3145736 | tf_op jit(solution)/shard_map/ppermute | solution.py:28
  29.2 22.7 %collective-permute-start.5 = (bf16[2,2,256,512]{3,2,1,0:T(8,128)(2,1)S(1)}, bf16[2,2,256,512]{3,2,1,0:T(8,128)(2,1)S(1)}, u32[]{:S(2)}, u32[]{:S(2)}) collective-permute-start(bf16[2,2,256,512]{3,2,1,0:T(8,128)(2,1)S(1)} %constant_dynamic-update-slice_fusion.refs_2_), channel_id=1, source_target_pairs={{0,24},{1,25},{2,26},{3,27},{4,28},{5,29},{6,30},{7,31},{8,0},{9,1... | collective-permute-start | bytes 3145736 | tf_op jit(solution)/shard_map/ppermute | solution.py:28
  30.7 13.6 %collective-permute-start.16 = (bf16[4,128,512]{2,1,0:T(8,128)(2,1)S(1)}, bf16[4,128,512]{2,1,0:T(8,128)(2,1)S(1)}, u32[]{:S(2)}, u32[]{:S(2)}) collective-permute-start(bf16[4,128,512]{2,1,0:T(8,128)(2,1)S(1)} %all-to-all-done.refs_12_.refs_20_), channel_id=1, source_target_pairs={{0,39},{1,32},{2,33},{3,34},{4,35},{5,36},{6,37},{7,38},{8,47},{9,... | collective-permute-start | bytes 1572872 | tf_op jit(solution)/shard_map/ppermute | solution.py:28
  30.7 16.1 %collective-permute-start.3 = (bf16[1,2,256,512]{3,2,1,0:T(8,128)(2,1)S(1)}, bf16[1,2,256,512]{3,2,1,0:T(8,128)(2,1)S(1)}, u32[]{:S(2)}, u32[]{:S(2)}) collective-permute-start(bf16[1,2,256,512]{3,2,1,0:T(8,128)(2,1)S(1)} %collective-permute-done.1), channel_id=1, source_target_pairs={{0,64},{1,65},{2,66},{3,67},{4,68},{5,69},{6,70},{7,71},{8,72},{9,... | collective-permute-start | bytes 1572872 | tf_op jit(solution)/shard_map/ppermute | solution.py:28
  32.2 15.4 %collective-permute-start.14 = (bf16[4,128,512]{2,1,0:T(8,128)(2,1)S(1)}, bf16[4,128,512]{2,1,0:T(8,128)(2,1)S(1)}, u32[]{:S(2)}, u32[]{:S(2)}) collective-permute-start(bf16[4,128,512]{2,1,0:T(8,128)(2,1)S(1)} %collective-permute-done.13.refs_8_.refs_18_.refs_16_), channel_id=1, source_target_pairs={{0,1},{1,2},{2,3},{3,4},{4,5},{5,6},{6,7},{7,0},{8,9},{9,10},{10,1... | collective-permute-start | bytes 1572872 | tf_op jit(solution)/shard_map/ppermute | solution.py:28
  44.3 8.3 %collective-permute-start.11 = (bf16[1,2,256,512]{3,2,1,0:T(8,128)(2,1)S(1)}, bf16[1,2,256,512]{3,2,1,0:T(8,128)(2,1)S(1)}, u32[]{:S(2)}, u32[]{:S(2)}) collective-permute-start(bf16[1,2,256,512]{3,2,1,0:T(8,128)(2,1)S(1)} %collective-permute-done.7.refs_7_), channel_id=1, source_target_pairs={{0,24},{1,25},{2,26},{3,27},{4,28},{5,29},{6,30},{7,31},{8,0},{9,1... | collective-permute-start | bytes 1572872 | tf_op jit(solution)/shard_map/ppermute | solution.py:28
  46.8 8.3 %collective-permute-start.17 = (bf16[4,128,512]{2,1,0:T(8,128)(2,1)S(1)}, bf16[4,128,512]{2,1,0:T(8,128)(2,1)S(1)}, u32[]{:S(2)}, u32[]{:S(2)}) collective-permute-start(bf16[4,128,512]{2,1,0:T(8,128)(2,1)S(1)} %collective-permute-done.16.refs_9_.refs_19_.refs_17_), channel_id=1, source_target_pairs={{0,1},{1,2},{2,3},{3,4},{4,5},{5,6},{6,7},{7,0},{8,9},{9,10},{10,1... | collective-permute-start | bytes 1572872 | tf_op jit(solution)/shard_map/ppermute | solution.py:28
  47.6 10.7 %collective-permute-start.8 = (bf16[1,2,256,512]{3,2,1,0:T(8,128)(2,1)S(1)}, bf16[1,2,256,512]{3,2,1,0:T(8,128)(2,1)S(1)}, u32[]{:S(2)}, u32[]{:S(2)}) collective-permute-start(bf16[1,2,256,512]{3,2,1,0:T(8,128)(2,1)S(1)} %collective-permute-done.3.refs_3_), channel_id=1, source_target_pairs={{0,24},{1,25},{2,26},{3,27},{4,28},{5,29},{6,30},{7,31},{8,0},{9,1... | collective-permute-start | bytes 1572872 | tf_op jit(solution)/shard_map/ppermute | solution.py:28
  49.5 17.4 %collective-permute-start.19 = (bf16[2,4,128,512]{3,2,1,0:T(8,128)(2,1)S(1)}, bf16[2,4,128,512]{3,2,1,0:T(8,128)(2,1)S(1)}, u32[]{:S(2)}, u32[]{:S(2)}) collective-permute-start(bf16[2,4,128,512]{3,2,1,0:T(8,128)(2,1)S(1)} %pad_maximum_fusion.1), channel_id=1, source_target_pairs={{0,32},{1,33},{2,34},{3,35},{4,36},{5,37},{6,38},{7,39},{8,40},{9,... | collective-permute-start | bytes 3145736 | tf_op jit(solution)/shard_map/ppermute | solution.py:28
  51.8 15.2 %collective-permute-start.9 = (bf16[2,2,256,512]{3,2,1,0:T(8,128)(2,1)S(1)}, bf16[2,2,256,512]{3,2,1,0:T(8,128)(2,1)S(1)}, u32[]{:S(2)}, u32[]{:S(2)}) collective-permute-start(bf16[2,2,256,512]{3,2,1,0:T(8,128)(2,1)S(1)} %collective-permute-done.4.refs_4_), channel_id=1, source_target_pairs={{0,8},{1,9},{2,10},{3,11},{4,12},{5,13},{6,14},{7,15},{8,16},{9,17... | collective-permute-start | bytes 3145736 | tf_op jit(solution)/shard_map/ppermute | solution.py:28
  52.7 10.5 %collective-permute-start.15 = (bf16[4,128,512]{2,1,0:T(8,128)(2,1)S(1)}, bf16[4,128,512]{2,1,0:T(8,128)(2,1)S(1)}, u32[]{:S(2)}, u32[]{:S(2)}) collective-permute-start(bf16[4,128,512]{2,1,0:T(8,128)(2,1)S(1)} %collective-permute-done.14.refs_10_.refs_20_.refs_18_), channel_id=1, source_target_pairs={{0,1},{1,2},{2,3},{3,4},{4,5},{5,6},{6,7},{7,0},{8,9},{9,10},{10,1... | collective-permute-start | bytes 1572872 | tf_op jit(solution)/shard_map/ppermute | solution.py:28
  55.1 11.7 %collective-permute-start.18 = (bf16[4,128,512]{2,1,0:T(8,128)(2,1)S(1)}, bf16[4,128,512]{2,1,0:T(8,128)(2,1)S(1)}, u32[]{:S(2)}, u32[]{:S(2)}) collective-permute-start(bf16[4,128,512]{2,1,0:T(8,128)(2,1)S(1)} %collective-permute-done.17.refs_11_.refs_21_.refs_19_), channel_id=1, source_target_pairs={{0,1},{1,2},{2,3},{3,4},{4,5},{5,6},{6,7},{7,0},{8,9},{9,10},{10,1... | collective-permute-start | bytes 1572872 | tf_op jit(solution)/shard_map/ppermute | solution.py:28
  58.3 8.6 %collective-permute-start.10 = (bf16[1,2,256,512]{3,2,1,0:T(8,128)(2,1)S(1)}, bf16[1,2,256,512]{3,2,1,0:T(8,128)(2,1)S(1)}, u32[]{:S(2)}, u32[]{:S(2)}) collective-permute-start(bf16[1,2,256,512]{3,2,1,0:T(8,128)(2,1)S(1)} %collective-permute-done.8.refs_8_), channel_id=1, source_target_pairs={{0,24},{1,25},{2,26},{3,27},{4,28},{5,29},{6,30},{7,31},{8,0},{9,1... | collective-permute-start | bytes 1572872 | tf_op jit(solution)/shard_map/ppermute | solution.py:28
  63.2 9.7 %collective-permute-start.22 = (bf16[2,4,128,512]{3,2,1,0:T(8,128)(2,1)S(1)}, bf16[2,4,128,512]{3,2,1,0:T(8,128)(2,1)S(1)}, u32[]{:S(2)}, u32[]{:S(2)}) collective-permute-start(bf16[2,4,128,512]{3,2,1,0:T(8,128)(2,1)S(1)} %pad_maximum_fusion.2), channel_id=1, source_target_pairs={{0,32},{1,33},{2,34},{3,35},{4,36},{5,37},{6,38},{7,39},{8,40},{9,... | collective-permute-start | bytes 3145736 | tf_op jit(solution)/shard_map/ppermute | solution.py:28
  67.0 13.4 %collective-permute-start.20 = (bf16[2,4,128,512]{3,2,1,0:T(8,128)(2,1)S(1)}, bf16[2,4,128,512]{3,2,1,0:T(8,128)(2,1)S(1)}, u32[]{:S(2)}, u32[]{:S(2)}) collective-permute-start(bf16[2,4,128,512]{3,2,1,0:T(8,128)(2,1)S(1)} %pad_maximum_fusion), channel_id=1, source_target_pairs={{0,32},{1,33},{2,34},{3,35},{4,36},{5,37},{6,38},{7,39},{8,40},{9,... | collective-permute-start | bytes 3145736 | tf_op jit(solution)/shard_map/ppermute | solution.py:28
  69.8 10.6 %collective-permute-start.12 = (bf16[1,2,256,512]{3,2,1,0:T(8,128)(2,1)S(1)}, bf16[1,2,256,512]{3,2,1,0:T(8,128)(2,1)S(1)}, u32[]{:S(2)}, u32[]{:S(2)}) collective-permute-start(bf16[1,2,256,512]{3,2,1,0:T(8,128)(2,1)S(1)} %collective-permute-done.3.refs_3_), channel_id=1, source_target_pairs={{0,8},{1,9},{2,10},{3,11},{4,12},{5,13},{6,14},{7,15},{8,16},{9,17... | collective-permute-start | bytes 1572872 | tf_op jit(solution)/shard_map/ppermute | solution.py:28
  70.0 2.9 %collective-permute-start.23 = (bf16[4,128,512]{2,1,0:T(8,128)(2,1)S(1)}, bf16[4,128,512]{2,1,0:T(8,128)(2,1)S(1)}, u32[]{:S(2)}, u32[]{:S(2)}) collective-permute-start(bf16[4,128,512]{2,1,0:T(8,128)(2,1)S(1)} %all-to-all-done.refs_12_.refs_20_), channel_id=1, source_target_pairs={{0,32},{1,33},{2,34},{3,35},{4,36},{5,37},{6,38},{7,39},{8,40},{9,... | collective-permute-start | bytes 1572872 | tf_op jit(solution)/shard_map/ppermute | solution.py:28
  71.3 9.0 %collective-permute-start.21 = (bf16[4,128,512]{2,1,0:T(8,128)(2,1)S(1)}, bf16[4,128,512]{2,1,0:T(8,128)(2,1)S(1)}, u32[]{:S(2)}, u32[]{:S(2)}) collective-permute-start(bf16[4,128,512]{2,1,0:T(8,128)(2,1)S(1)} %collective-permute-done.15.refs_14_.refs_22_), channel_id=1, source_target_pairs={{0,1},{1,2},{2,3},{3,4},{4,5},{5,6},{6,7},{7,0},{8,9},{9,10},{10,1... | collective-permute-start | bytes 1572872 | tf_op jit(solution)/shard_map/ppermute | solution.py:28
  80.4 2.9 %collective-permute-start.24 = (bf16[4,128,512]{2,1,0:T(8,128)(2,1)S(1)}, bf16[4,128,512]{2,1,0:T(8,128)(2,1)S(1)}, u32[]{:S(2)}, u32[]{:S(2)}) collective-permute-start(bf16[4,128,512]{2,1,0:T(8,128)(2,1)S(1)} %collective-permute-done.21.refs_14_), channel_id=1, source_target_pairs={{0,32},{1,33},{2,34},{3,35},{4,36},{5,37},{6,38},{7,39},{8,40},{9,... | collective-permute-start | bytes 1572872 | tf_op jit(solution)/shard_map/ppermute | solution.py:28
